TPU v7x, 32 devices: a whole 2x2x4 slice. The times are simulated.
32 devices in a mesh: dp: 8 (over y, x, core), seq: 4 (over z).
Axes of the slice: x: 2, y: 2, z: 4, core: 2. Of those that a mesh axis runs over, the one named last changes fastest.
Arguments:
- block_input: bfloat16 [8, 1024, 2048], P('dp', 'seq'), may hold values from -6 to 6
- norm_gain: float32 [2048], replicated, may hold values from 0.5 to 1.5
- in_proj: bfloat16 [2048, 2816], P(('dp', 'seq')), may hold values from -0.125 to 0.125
- gate_proj: bfloat16 [2048, 2816], P(('dp', 'seq')), may hold values from -0.125 to 0.125
- conv_kernel: float32 [4, 2816], replicated, may hold values from -3 to 3
- conv_bias: float32 [2816], replicated, may hold values from -3 to 3
- recur_weight: bfloat16 [16, 176, 176], replicated, may hold values from -0.4375 to 0.4375
- recur_bias: float32 [2816], replicated, may hold values from -3 to 3
- input_weight: bfloat16 [16, 176, 176], replicated, may hold values from -0.4375 to 0.4375
- input_bias: float32 [2816], replicated, may hold values from -3 to 3
- decay_param: float32 [2816], replicated, may hold values from 5 to 10
- out_proj: bfloat16 [2816, 2048], P(('dp', 'seq')), may hold values from -0.3125 to 0.3125
- mlp_gain: float32 [2048], replicated, may hold values from 0.5 to 1.5
- mlp_gate: bfloat16 [2048, 6144], P(('dp', 'seq')), may hold values from -0.125 to 0.125
- mlp_up: bfloat16 [2048, 6144], P(('dp', 'seq')), may hold values from -0.125 to 0.125
- mlp_down: bfloat16 [6144, 2048], P(('dp', 'seq')), may hold values from -0.109375 to 0.109375
- out_grad: bfloat16 [8, 1024, 2048], P('dp', 'seq'), may hold values from -6 to 6
Outputs:
- block_output: bfloat16 [8, 1024, 2048], P('dp', 'seq')
- input_grad: float32 [8, 1024, 2048], P('dp', 'seq')
- grad_norm_gain: float32 [2048], replicated
- grad_in_proj: float32 [2048, 2816], P('seq', 'dp')
- grad_gate_proj: float32 [2048, 2816], P('seq', 'dp')
- grad_conv_kernel: float32 [4, 2816], replicated
- grad_conv_bias: float32 [2816], replicated
- grad_recur_weight: float32 [16, 176, 176], replicated
- grad_recur_bias: float32 [2816], replicated
- grad_input_weight: float32 [16, 176, 176], replicated
- grad_input_bias: float32 [2816], replicated
- grad_decay_param: float32 [2816], replicated
- grad_out_proj: float32 [2816, 2048], P('seq', 'dp')
- grad_mlp_gain: float32 [2048], replicated
- grad_mlp_gate: float32 [2048, 6144], P('seq', 'dp')
- grad_mlp_up: float32 [2048, 6144], P('seq', 'dp')
- grad_mlp_down: float32 [6144, 2048], P('seq', 'dp')
All inputs are finite; a program needn't handle non-finite values.
Results may differ from a plain program's by a relative error of at most 0.015.
Values may be sent and summed in bfloat16 or wider, within the bound.
No kernel may reach another device: no remote copies, remote signals or barrier semaphores. Data moves between devices by JAX's collectives and lax.ppermute only.
A program may use at most 640 MiB of HBM per device.

v0:
```python
import jax
import jax.numpy as jnp
from jax import lax
from jax.sharding import PartitionSpec as P

EPSILON = 1e-06


def from_behind(value, axis, steps):
    count = lax.axis_size(axis)
    initial, last = (max(0, -steps), min(count, count - steps))
    return lax.ppermute(value, axis, [(source, source + steps) for source in range(initial, last)])


def scaled_norm(values, gain_vec):
    return (
        values * lax.rsqrt(jnp.mean(values * values, axis=-1, keepdims=True) + EPSILON) * gain_vec
    )


def recurrence_gates(recur_pre, input_pre, conv_out, decay_param):
    recur_gate = jax.nn.sigmoid(recur_pre)
    input_gate = jax.nn.sigmoid(input_pre)
    log_rate = -8.0 * recur_gate * jax.nn.softplus(-decay_param)
    decay_rate = jnp.exp(log_rate)
    driven = jnp.sqrt(-jnp.expm1(2.0 * log_rate)) * input_gate * conv_out
    return (decay_rate, driven)


def gated_product(gate_values, up_values):
    return jax.nn.gelu(gate_values) * up_values


def compose(earlier, later):
    return (earlier[0] * later[0], earlier[1] * later[0] + later[1])


def matmul_back(grad_rows, weight_full):
    return lax.dot_general(
        grad_rows, weight_full, (((1,), (1,)), ((), ())), preferred_element_type=jnp.float32
    )


def reduce_weight_grad(left_side, right_side):
    inner_sum = lax.psum_scatter(
        lax.dot_general(
            left_side, right_side, (((0,), (0,)), ((), ())), preferred_element_type=jnp.float32
        ).astype(jnp.bfloat16),
        "seq",
        scatter_dimension=0,
        tiled=True,
    )
    return lax.psum_scatter(inner_sum, "dp", scatter_dimension=1, tiled=True).astype(jnp.float32)


def local(
    block_input,
    norm_gain,
    in_proj,
    gate_proj,
    conv_kernel,
    conv_bias,
    recur_weight,
    recur_bias,
    input_weight,
    input_bias,
    decay_param,
    out_proj,
    mlp_gain,
    mlp_gate,
    mlp_up,
    mlp_down,
    out_grad,
):
    seq_count = lax.axis_size("seq")
    model_width = block_input.shape[2]
    tokens = block_input.reshape(-1, model_width).astype(jnp.float32)
    length = tokens.shape[0]
    head_count = recur_weight.shape[0]
    head_size = recur_weight.shape[1]
    tap_count = conv_kernel.shape[0]
    conv_lag = tap_count - 1
    fwd_recur = (
        lax.all_gather(in_proj, ("dp", "seq"), axis=0, tiled=True),
        lax.all_gather(gate_proj, ("dp", "seq"), axis=0, tiled=True),
        lax.all_gather(out_proj, ("dp", "seq"), axis=0, tiled=True),
    )
    normed = scaled_norm(tokens, norm_gain).astype(jnp.bfloat16)
    branch = jnp.dot(normed, fwd_recur[0], preferred_element_type=jnp.float32)
    gate_pre = jnp.dot(normed, fwd_recur[1], preferred_element_type=jnp.float32)
    gate_act = jax.nn.gelu(gate_pre)
    recur_width = branch.shape[1]
    prior_rows = from_behind(branch[length - conv_lag :], "seq", 1)
    padded = jnp.concatenate([prior_rows, branch], axis=0)
    conv_out = jnp.zeros((length, recur_width), jnp.float32) + conv_bias
    for tap_index in range(tap_count):
        begin = conv_lag - tap_index
        conv_out = conv_out + conv_kernel[tap_index] * padded[begin : begin + length]
    heads_in = conv_out.astype(jnp.bfloat16).reshape(length, head_count, head_size)
    recur_pre = (
        jnp.einsum(
            "thi,hij->thj", heads_in, recur_weight, preferred_element_type=jnp.float32
        ).reshape(length, recur_width)
        + recur_bias
    )
    input_pre = (
        jnp.einsum(
            "thi,hij->thj", heads_in, input_weight, preferred_element_type=jnp.float32
        ).reshape(length, recur_width)
        + input_bias
    )
    decay_rate, driven = recurrence_gates(recur_pre, input_pre, conv_out, decay_param)
    decay_run, local_states = lax.associative_scan(compose, (decay_rate, driven), axis=0)
    zero_row = jnp.zeros((recur_width,), jnp.float32)
    carried = zero_row
    for repeat in range(seq_count - 1):
        carried = from_behind(decay_run[length - 1] * carried + local_states[length - 1], "seq", 1)
    states = local_states + decay_run * carried
    mixed_out = (states * gate_act).astype(jnp.bfloat16)
    residual = tokens + jnp.dot(mixed_out, fwd_recur[2], preferred_element_type=jnp.float32)
    fwd_ffn = (
        lax.all_gather(mlp_gate, ("dp", "seq"), axis=0, tiled=True),
        lax.all_gather(mlp_up, ("dp", "seq"), axis=0, tiled=True),
        lax.all_gather(mlp_down, ("dp", "seq"), axis=0, tiled=True),
    )
    normed_two = scaled_norm(residual, mlp_gain).astype(jnp.bfloat16)
    ffn_gate = jnp.dot(normed_two, fwd_ffn[0], preferred_element_type=jnp.float32)
    ffn_up = jnp.dot(normed_two, fwd_ffn[1], preferred_element_type=jnp.float32)
    hidden = gated_product(ffn_gate, ffn_up).astype(jnp.bfloat16)
    result = residual + jnp.dot(hidden, fwd_ffn[2], preferred_element_type=jnp.float32)
    block_output = result.astype(jnp.bfloat16).reshape(block_input.shape)
    back_recur = (
        lax.all_gather(in_proj, ("dp", "seq"), axis=0, tiled=True),
        lax.all_gather(gate_proj, ("dp", "seq"), axis=0, tiled=True),
        lax.all_gather(out_proj, ("dp", "seq"), axis=0, tiled=True),
    )
    back_ffn = (
        lax.all_gather(mlp_gate, ("dp", "seq"), axis=0, tiled=True),
        lax.all_gather(mlp_up, ("dp", "seq"), axis=0, tiled=True),
        lax.all_gather(mlp_down, ("dp", "seq"), axis=0, tiled=True),
    )
    grad_low = out_grad.reshape(length, model_width)
    grad_top = grad_low.astype(jnp.float32)
    grad_down_w = reduce_weight_grad(hidden, grad_low)
    grad_hidden = matmul_back(grad_low, back_ffn[2])
    unused, pull_ffn = jax.vjp(gated_product, ffn_gate, ffn_up)
    grad_ffn_gate, grad_ffn_up = pull_ffn(grad_hidden)
    grad_ffn_gate = grad_ffn_gate.astype(jnp.bfloat16)
    grad_ffn_up = grad_ffn_up.astype(jnp.bfloat16)
    grad_mgate_w = reduce_weight_grad(normed_two, grad_ffn_gate)
    grad_mup_w = reduce_weight_grad(normed_two, grad_ffn_up)
    grad_normed_two = matmul_back(grad_ffn_gate, back_ffn[0]) + matmul_back(
        grad_ffn_up, back_ffn[1]
    )
    unused, pull_norm_two = jax.vjp(scaled_norm, residual, mlp_gain)
    grad_resid_part, mlp_gain_term = pull_norm_two(grad_normed_two)
    grad_residual = grad_resid_part + grad_top
    grad_rec = grad_residual.astype(jnp.bfloat16)
    grad_out_w = reduce_weight_grad(mixed_out, grad_rec)
    grad_mixed = matmul_back(grad_rec, back_recur[2])
    grad_states = grad_mixed * gate_act
    unused, pull_gelu = jax.vjp(jax.nn.gelu, gate_pre)
    grad_gate_pre = pull_gelu(grad_mixed * states)[0].astype(jnp.bfloat16)
    next_decay = jnp.concatenate([decay_rate[1:], jnp.ones((1, recur_width), jnp.float32)], axis=0)
    decay_tail, local_grads = lax.associative_scan(
        compose, (next_decay, grad_states), reverse=True, axis=0
    )
    total_decay = decay_rate[0] * decay_tail[0]
    first_grad = decay_rate[0] * local_grads[0]
    later_grad = zero_row
    for repeat in range(seq_count - 1):
        later_grad = from_behind(total_decay * later_grad + first_grad, "seq", -1)
    state_grads = local_grads + decay_tail * later_grad
    prior_states = jnp.concatenate([carried[None], states[: length - 1]], axis=0)
    unused, pull_gates = jax.vjp(recurrence_gates, recur_pre, input_pre, conv_out, decay_param)
    grad_recur_pre, grad_input_pre, grad_conv, decay_term = pull_gates(
        (state_grads * prior_states, state_grads)
    )
    grad_recur_low = grad_recur_pre.astype(jnp.bfloat16).reshape(length, head_count, head_size)
    grad_input_low = grad_input_pre.astype(jnp.bfloat16).reshape(length, head_count, head_size)
    recur_w_term = jnp.einsum(
        "thi,thj->hij", heads_in, grad_recur_low, preferred_element_type=jnp.float32
    )
    input_w_term = jnp.einsum(
        "thi,thj->hij", heads_in, grad_input_low, preferred_element_type=jnp.float32
    )
    recur_b_term = jnp.sum(grad_recur_low.astype(jnp.float32), axis=0).reshape(recur_width)
    input_b_term = jnp.sum(grad_input_low.astype(jnp.float32), axis=0).reshape(recur_width)
    grad_conv = grad_conv + jnp.einsum(
        "thj,hij->thi", grad_recur_low, recur_weight, preferred_element_type=jnp.float32
    ).reshape(length, recur_width)
    grad_conv = grad_conv + jnp.einsum(
        "thj,hij->thi", grad_input_low, input_weight, preferred_element_type=jnp.float32
    ).reshape(length, recur_width)
    later_rows = from_behind(grad_conv[:conv_lag].astype(jnp.bfloat16), "seq", -1).astype(
        jnp.float32
    )
    grad_padded = jnp.concatenate([grad_conv, later_rows], axis=0)
    grad_branch = jnp.zeros((length, recur_width), jnp.float32)
    kernel_rows = []
    for tap_index in range(tap_count):
        grad_branch = (
            grad_branch + conv_kernel[tap_index] * grad_padded[tap_index : tap_index + length]
        )
        begin = conv_lag - tap_index
        kernel_rows.append(jnp.sum(grad_conv * padded[begin : begin + length], axis=0))
    kernel_term = jnp.stack(kernel_rows, axis=0)
    bias_term = jnp.sum(grad_conv, axis=0)
    grad_branch = grad_branch.astype(jnp.bfloat16)
    grad_in_w = reduce_weight_grad(normed, grad_branch)
    grad_gate_w = reduce_weight_grad(normed, grad_gate_pre)
    grad_normed = matmul_back(grad_branch, back_recur[0]) + matmul_back(
        grad_gate_pre, back_recur[1]
    )
    unused, pull_norm = jax.vjp(scaled_norm, tokens, norm_gain)
    grad_tokens, norm_gain_term = pull_norm(grad_normed)
    input_grad = (grad_tokens + grad_residual).reshape(block_input.shape)
    summed = lax.psum(
        (
            norm_gain_term,
            kernel_term,
            bias_term,
            recur_w_term,
            recur_b_term,
            input_w_term,
            input_b_term,
            decay_term,
            mlp_gain_term,
        ),
        ("dp", "seq"),
    )
    return (
        block_output,
        input_grad,
        summed[0],
        grad_in_w,
        grad_gate_w,
        summed[1],
        summed[2],
        summed[3],
        summed[4],
        summed[5],
        summed[6],
        summed[7],
        grad_out_w,
        summed[8],
        grad_mgate_w,
        grad_mup_w,
        grad_down_w,
    )


def solution(mesh):
    return jax.shard_map(
        local,
        mesh=mesh,
        in_specs=(
            P("dp", "seq", None),
            P(),
            P(("dp", "seq"), None),
            P(("dp", "seq"), None),
            P(),
            P(),
            P(),
            P(),
            P(),
            P(),
            P(),
            P(("dp", "seq"), None),
            P(),
            P(("dp", "seq"), None),
            P(("dp", "seq"), None),
            P(("dp", "seq"), None),
            P("dp", "seq", None),
        ),
        out_specs=(
            P("dp", "seq", None),
            P("dp", "seq", None),
            P(),
            P("seq", "dp"),
            P("seq", "dp"),
            P(),
            P(),
            P(),
            P(),
            P(),
            P(),
            P(),
            P("seq", "dp"),
            P(),
            P("seq", "dp"),
            P("seq", "dp"),
            P("seq", "dp"),
        ),
        check_vma=False,
    )
```

profile of v0, /device:TPU:3, one launch (start us, length us, event | category | flops | bytes accessed | tf_op | source)
XLA Modules:
  0.0 3375.3 jit_solution(6021144712687071717)
XLA Ops:
  11.6 92.2 %all-gather.7.cloned.1.call-done = bf16[2048,2816]{1,0:T(8,128)(2,1)} async-done(((bf16[64,2816]{1,0:T(8,128)(2,1)}), bf16[2048,2816]{1,0:T(8,128)(2,1)}) %all-gather.7.cloned.1.call-update) | async-done | bytes 11534352 | tf_op jit(solution)/shard_map/all_gather | solution.py:84
  379.5 13.4 multiply_convert_fusion.2
  401.3 43.4 %all-gather.13.cloned.1.call-done = bf16[2048,6144]{1,0:T(8,128)(2,1)} async-done(((bf16[64,6144]{1,0:T(8,128)(2,1)}), bf16[2048,6144]{1,0:T(8,128)(2,1)}) %all-gather.13.cloned.1.call-update) | async-done | bytes 25165840 | tf_op jit(solution)/shard_map/all_gather | solution.py:122
  444.7 14.2 fusion.108
  458.9 141.4 %all-gather.15.cloned.1.call-done = bf16[2048,6144]{1,0:T(8,128)(2,1)} async-done(((bf16[64,6144]{1,0:T(8,128)(2,1)}), bf16[2048,6144]{1,0:T(8,128)(2,1)}) %all-gather.15.cloned.1.call-update) | async-done | bytes 25165840 | tf_op jit(solution)/shard_map/all_gather | solution.py:123
  600.3 14.4 fusion.109
  614.6 141.2 %all-gather.17.cloned.1.call-done = bf16[6144,2048]{1,0:T(8,128)(2,1)} async-done(((bf16[192,2048]{1,0:T(8,128)(2,1)}), bf16[6144,2048]{1,0:T(8,128)(2,1)}) %all-gather.17.cloned.1.call-update) | async-done | bytes 25165840 | tf_op jit(solution)/shard_map/all_gather | solution.py:124
  755.9 22.1 multiply_convert_fusion
  778.0 13.5 fusion.110
  791.5 15.7 multiply_reduce_fusion.5
  810.6 12.8 fusion.45
  875.5 12.0 slice.695
  898.9 11.9 slice.634
  1099.7 12.0 slice.697
  1159.6 23.0 rev.9
  1182.6 22.7 rev.8
  1239.6 12.1 multiply_reduce_fusion.3
  1267.2 14.4 convolution_convert_fusion.2
  1281.7 13.7 convolution_convert_fusion.1
  1296.6 14.0 convolution_convert_fusion
  1316.0 152.2 %reduce-scatter.17.cloned.1.call-done = bf16[512,2816]{1,0:T(8,128)(2,1)} async-done(((bf16[2048,2816]{1,0:T(8,128)(2,1)}), bf16[512,2816]{1,0:T(8,128)(2,1)}) %reduce-scatter.17.cloned.1.call-update) | async-done | bytes 2883600 | tf_op jit(solution)/shard_map/reduce_scatter | solution.py:45
  1472.7 413.0 %reduce-scatter.25.cloned.1.call-done = bf16[512,6144]{1,0:T(8,128)(2,1)} async-done(((bf16[2048,6144]{1,0:T(8,128)(2,1)}), bf16[512,6144]{1,0:T(8,128)(2,1)}) %reduce-scatter.25.cloned.1.call-update) | async-done | bytes 6291472 | tf_op jit(solution)/shard_map/reduce_scatter | solution.py:45
  1885.8 418.6 %reduce-scatter.29.cloned.1.call-done = bf16[512,6144]{1,0:T(8,128)(2,1)} async-done(((bf16[2048,6144]{1,0:T(8,128)(2,1)}), bf16[512,6144]{1,0:T(8,128)(2,1)}) %reduce-scatter.29.cloned.1.call-update) | async-done | bytes 6291472 | tf_op jit(solution)/shard_map/reduce_scatter | solution.py:45
  2304.5 418.4 %reduce-scatter.33.cloned.1.call-done = bf16[1536,2048]{1,0:T(8,128)(2,1)} async-done(((bf16[6144,2048]{1,0:T(8,128)(2,1)}), bf16[1536,2048]{1,0:T(8,128)(2,1)}) %reduce-scatter.33.cloned.1.call-update) | async-done | bytes 6291472 | tf_op jit(solution)/shard_map/reduce_scatter | solution.py:45
  2746.5 14.7 fusion.35
  2776.1 45.9 %reduce-scatter.23.cloned.1.call-done = bf16[704,256]{1,0:T(8,128)(2,1)} async-done(((bf16[704,2048]{1,0:T(8,128)(2,1)}), bf16[704,256]{1,0:T(8,128)(2,1)}) %reduce-scatter.23.cloned.1.call-update) | async-done | bytes 360464 | tf_op jit(solution)/shard_map/reduce_scatter | solution.py:53
  2823.9 47.2 %reduce-scatter.37.cloned.1.call-done = bf16[352,512]{1,0:T(8,128)(2,1)} async-done(((bf16[2816,512]{1,0:T(8,128)(2,1)}), bf16[352,512]{1,0:T(8,128)(2,1)}) %reduce-scatter.37.cloned.1.call-update) | async-done | bytes 360464
  2873.4 62.7 %reduce-scatter.27.cloned.1.call-done = bf16[512,768]{1,0:T(8,128)(2,1)} async-done(((bf16[512,6144]{1,0:T(8,128)(2,1)}), bf16[512,768]{1,0:T(8,128)(2,1)}) %reduce-scatter.27.cloned.1.call-update) | async-done | bytes 786448 | tf_op jit(solution)/shard_map/reduce_scatter | solution.py:53
  2938.5 63.0 %reduce-scatter.31.cloned.1.call-done = bf16[512,768]{1,0:T(8,128)(2,1)} async-done(((bf16[512,6144]{1,0:T(8,128)(2,1)}), bf16[512,768]{1,0:T(8,128)(2,1)}) %reduce-scatter.31.cloned.1.call-update) | async-done | bytes 786448 | tf_op jit(solution)/shard_map/reduce_scatter | solution.py:53
  3003.9 62.6 %reduce-scatter.35.cloned.1.call-done = bf16[1536,256]{1,0:T(8,128)(2,1)} async-done(((bf16[1536,2048]{1,0:T(8,128)(2,1)}), bf16[1536,256]{1,0:T(8,128)(2,1)}) %reduce-scatter.35.cloned.1.call-update) | async-done | bytes 786448 | tf_op jit(solution)/shard_map/reduce_scatter | solution.py:53
  3068.9 130.3 %all-reduce.71.cloned.1.call-done = (f32[2048]{0:T(1024)}, f32[4,2816]{1,0:T(4,128)}, f32[2816]{0:T(1024)}, f32[2816]{0:T(1024)}, f32[2816]{0:T(1024)}, /*index=5*/f32[2816]{0:T(1024)}, f32[2048]{0:T(1024)}) async-done(((f32[2048]{0:T(1024)}, f32[4,2816]{1,0:T(4,128)}, f32[2816]{0:T(1024)}, f32[2816]{0:T(1024)}, f32[2816]{0:T(1024)}, /*index=5*/f32[2816]{0:T(1024)}, f32[2048]{0:T(1024)}), (f32[2048]{0:T(1024)}, ...) | async-done | bytes 106512 | tf_op jit(solution)/shard_map/psum | solution.py:218
  3199.2 157.3 %all-reduce.73.cloned.1.call-done = (f32[16,176,176]{2,1,0:T(8,128)}, f32[16,176,176]{2,1,0:T(8,128)}) async-done(((f32[16,176,176]{2,1,0:T(8,128)}, f32[16,176,176]{2,1,0:T(8,128)}), (f32[16,176,176]{2,1,0:T(8,128)}, f32[16,176,176]{2,1,0:T(8,128)})) %all-reduce.73.cloned.1.call-update) | async-done | bytes 3964944 | tf_op jit(solution)/shard_map/psum | solution.py:218
  (618 shorter events, 713.0 us)
Async XLA Ops:
  7.2 112.3 %copy-start = (bf16[16,176,176]{2,1,0:T(8,128)(2,1)S(1)}, bf16[16,176,176]{2,1,0:T(8,128)(2,1)}, u32[]{:S(2)}) copy-start(bf16[16,176,176]{2,1,0:T(8,128)(2,1)} %param.23) | copy-start | bytes 2973700
  7.2 96.6 %all-gather.7.cloned.1.call-start = ((), (), s32[]{:S(2)}) async-start(), calls=%async_computation.12 | async-start | bytes 11894784 | tf_op jit(solution)/shard_map/all_gather | solution.py:84
  8.0 370.7 %all-gather.9.cloned.1.call-start = ((), (), s32[]{:S(2)}) async-start(), calls=%async_computation.13 | async-start | bytes 11894784 | tf_op jit(solution)/shard_map/all_gather | solution.py:85
  8.7 384.2 %all-gather.11.cloned.1.call-start = ((), (), s32[]{:S(2)}) async-start(), calls=%async_computation.14 | async-start | bytes 11894784 | tf_op jit(solution)/shard_map/all_gather | solution.py:86
  9.5 435.2 %all-gather.13.cloned.1.call-start = ((), (), s32[]{:S(2)}) async-start(), calls=%async_computation.15 | async-start | bytes 25952256 | tf_op jit(solution)/shard_map/all_gather | solution.py:122
  10.0 590.2 %all-gather.15.cloned.1.call-start = ((), (), s32[]{:S(2)}) async-start(), calls=%async_computation.16 | async-start | bytes 25952256 | tf_op jit(solution)/shard_map/all_gather | solution.py:123
  10.6 745.2 %all-gather.17.cloned.1.call-start = ((), (), s32[]{:S(2)}) async-start(), calls=%async_computation.17 | async-start | bytes 25952256 | tf_op jit(solution)/shard_map/all_gather | solution.py:124
  11.2 1299.6 %reduce-scatter.19.cloned.1.call-start = ((), (), s32[]{:S(2)}) async-start(), calls=%async_computation.19 | async-start | bytes 14417920 | tf_op jit(solution)/shard_map/reduce_scatter | solution.py:45
  11.6 122.5 %copy-start.44 = (f32[2816]{0:T(1024)}, f32[2816]{0:T(1024)S(1)}, u32[]{:S(2)}) copy-start(f32[2816]{0:T(1024)S(1)} %broadcast_multiply_fusion) | copy-start | bytes 33796
  11.6 102.5 %copy-start.108 = (f32[2816]{0:T(1024)S(1)}, f32[2816]{0:T(1024)}, u32[]{:S(2)}) copy-start(f32[2816]{0:T(1024)} %param.22) | copy-start | bytes 33796
  110.2 3.9 collective-permute-start
  364.2 4.4 collective-permute-start.1
  368.6 4.5 collective-permute-start.2
  373.1 6.5 collective-permute-start.3
  401.2 199.0 %copy-start.14 = (bf16[256,2048]{1,0:T(8,128)(2,1)}, bf16[256,2048]{1,0:T(8,128)(2,1)S(1)}, u32[]{:S(2)}) copy-start(bf16[256,2048]{1,0:T(8,128)(2,1)S(1)} %multiply_convert_fusion.3) | copy-start | bytes 3145732
  830.8 484.6 %reduce-scatter.21.cloned.1.call-start = ((), (), s32[]{:S(2)}) async-start(), calls=%async_computation.20 | async-start | bytes 14417920 | tf_op jit(solution)/shard_map/reduce_scatter | solution.py:45
  958.7 509.5 %reduce-scatter.17.cloned.1.call-start = ((), (), s32[]{:S(2)}) async-start(), calls=%async_computation.18 | async-start | bytes 14417920 | tf_op jit(solution)/shard_map/reduce_scatter | solution.py:45
  1141.0 5.3 collective-permute-start.4
  1146.2 5.1 collective-permute-start.5
  1151.3 54.1 %collective-permute-start.6 = (f32[2816]{0:T(1024)S(1)}, f32[2816]{0:T(1024)S(1)}, u32[]{:S(2)}, u32[]{:S(2)}) collective-permute-start(f32[2816]{0:T(1024)S(1)} %multiply_add_fusion.17), channel_id=1, source_target_pairs={{1,0},{2,1},{3,2},{5,4},{6,5},{7,6},{9,8},{10,9},{11,10},{13,12},{... | collective-permute-start | bytes 33800 | tf_op jit(solution)/shard_map/ppermute | solution.py:12
  1251.8 5.1 collective-permute-start.7
  1266.0 619.7 %reduce-scatter.25.cloned.1.call-start = ((), (), s32[]{:S(2)}) async-start(), calls=%async_computation.22 | async-start | bytes 31457280 | tf_op jit(solution)/shard_map/reduce_scatter | solution.py:45
  1281.6 1022.8 %reduce-scatter.29.cloned.1.call-start = ((), (), s32[]{:S(2)}) async-start(), calls=%async_computation.24 | async-start | bytes 31457280 | tf_op jit(solution)/shard_map/reduce_scatter | solution.py:45
  1295.4 1427.4 %reduce-scatter.33.cloned.1.call-start = ((), (), s32[]{:S(2)}) async-start(), calls=%async_computation.26 | async-start | bytes 31457280 | tf_op jit(solution)/shard_map/reduce_scatter | solution.py:45
  1310.7 1463.2 %reduce-scatter.39.cloned.1.call-start = ((), (), s32[]{:S(2)}) async-start(), calls=%async_computation.29 | async-start | bytes 3244032
  1315.3 1506.7 %reduce-scatter.23.cloned.1.call-start = ((), (), s32[]{:S(2)}) async-start(), calls=%async_computation.21 | async-start | bytes 3244032 | tf_op jit(solution)/shard_map/reduce_scatter | solution.py:53
  1315.9 1555.2 %reduce-scatter.37.cloned.1.call-start = ((), (), s32[]{:S(2)}) async-start(), calls=%async_computation.28 | async-start | bytes 3244032
  1472.7 1463.4 %reduce-scatter.27.cloned.1.call-start = ((), (), s32[]{:S(2)}) async-start(), calls=%async_computation.23 | async-start | bytes 7077888 | tf_op jit(solution)/shard_map/reduce_scatter | solution.py:53
  1885.7 1115.8 %reduce-scatter.31.cloned.1.call-start = ((), (), s32[]{:S(2)}) async-start(), calls=%async_computation.25 | async-start | bytes 7077888 | tf_op jit(solution)/shard_map/reduce_scatter | solution.py:53
  2304.4 762.1 %reduce-scatter.35.cloned.1.call-start = ((), (), s32[]{:S(2)}) async-start(), calls=%async_computation.27 | async-start | bytes 7077888 | tf_op jit(solution)/shard_map/reduce_scatter | solution.py:53
  2722.9 476.2 %all-reduce.71.cloned.1.call-start = ((), (), s32[]{:S(2)}) async-start(), calls=%async_computation.30 | async-start | bytes 221184 | tf_op jit(solution)/shard_map/psum | solution.py:218
  2742.4 614.1 %all-reduce.73.cloned.1.call-start = ((), (), s32[]{:S(2)}) async-start(), calls=%async_computation.31 | async-start | bytes 11534336 | tf_op jit(solution)/shard_map/psum | solution.py:218
  (113 other events, 1223.2 us)
Sparse Core Ops, SparseCore 0:
  10.9 92.8 all-gather.6
  106.6 89.6 all-gather.8
  199.2 89.6 all-gather.10
  291.6 153.0 all-gather.12
  447.4 152.8 all-gather.14
  603.0 152.8 all-gather.16
  830.9 192.7 reduce-scatter.18
  1026.1 196.7 reduce-scatter.20
  1266.1 201.9 reduce-scatter.16
  1470.3 415.3 reduce-scatter.24
  1888.2 416.1 reduce-scatter.28
  2306.6 416.1 reduce-scatter.32
  2727.2 46.6 reduce-scatter.38
  2777.1 44.8 reduce-scatter.22
  2826.2 44.8 reduce-scatter.36
  2874.4 61.7 reduce-scatter.26
  2939.7 61.7 reduce-scatter.30
  3004.7 61.7 reduce-scatter.34
  3075.2 123.9 all-reduce.70
  3204.9 151.5 all-reduce.72
where the time goes:
time: 3400 us; the launch traced here: 3380 us
  waiting for transfers between devices  2420 us (71%)
  local copies, waits for them, and re-layouts  523 us (15%)
  matrix products  237 us (7%)
  other arithmetic  158 us (5%)
    reduce_scatter x6, waiting for transfers between devices, reduce_weight_grad(): lax.psum_scatter(lax.dot_general(left_side, right_side, (((0,), (0,)), ((...  1400 us
    psum x2, waiting for transfers between devices, local(): lax.psum((norm_gain_term, kernel_term, bias_term, recur_w_term, recur_b_t...  288 us
    reduce_scatter x4, waiting for transfers between devices, reduce_weight_grad(): lax.psum_scatter(inner_sum, 'dp', scatter_dimension=1, tiled=True)  234 us
    slice x57, local copies, waits for them, and re-layouts, local(): lax.associative_scan(compose, (next_decay, grad_states), reverse=True, ax...  175 us
    all_gather x1, waiting for transfers between devices, local(): lax.all_gather(mlp_up, ('dp', 'seq'), axis=0, tiled=True)  141 us
    all_gather x1, waiting for transfers between devices, local(): lax.all_gather(mlp_down, ('dp', 'seq'), axis=0, tiled=True)  141 us
    slice x52, local copies, waits for them, and re-layouts, local(): lax.associative_scan(compose, (decay_rate, driven), axis=0)  106 us
    all_gather x1, waiting for transfers between devices, local(): lax.all_gather(in_proj, ('dp', 'seq'), axis=0, tiled=True)  92.2 us
  transfers between devices with their start and end apart: 28, of which 23 were waited for; matrix products, arithmetic and copies ran while one was open for 24% of the time, Pallas kernels for 0%

commit v1 on v0

v1 whole, which is shorter than its diff:
```python
import jax
import jax.numpy as jnp
from jax import lax
from jax.experimental import pallas as pl
from jax.experimental.pallas import tpu as pltpu
from jax.sharding import PartitionSpec as P

EPSILON = 1e-06
F32 = jnp.float32
BF16 = jnp.bfloat16
GELU_C = 0.7978845608028654
GELU_A = 0.044715
CHUNK = 32
VMEM_LIMIT = 48 << 20


def xor_send(value, axis, offset):
    count = lax.axis_size(axis)
    return lax.ppermute(value, axis, [(i, i ^ offset) for i in range(count)])


def shift_send(value, axis, steps):
    count = lax.axis_size(axis)
    first, last = max(0, -steps), min(count, count - steps)
    return lax.ppermute(value, axis, [(i, i + steps) for i in range(first, last)])


def gather_tokens(piece):
    count = lax.axis_size("dp")
    slots = {0: piece}
    if count == 8:
        half = piece.shape[0] // 2
        slots[2] = xor_send(piece, "dp", 2)
        slots[4] = xor_send(piece, "dp", 4)
        slots[1] = xor_send(piece, "dp", 1)
        top = xor_send(slots[4][:half], "dp", 2)
        bottom = xor_send(slots[2][half:], "dp", 4)
        slots[3] = xor_send(slots[2], "dp", 1)
        slots[5] = xor_send(slots[4], "dp", 1)
        slots[6] = jnp.concatenate([top, bottom], axis=0)
        slots[7] = jnp.concatenate(
            [xor_send(top, "dp", 1), xor_send(bottom, "dp", 1)], axis=0
        )
    else:
        for offset in range(2, count, 2):
            slots[offset] = xor_send(piece, "dp", offset)
        for offset in range(0, count, 2):
            slots[offset + 1] = xor_send(slots[offset], "dp", 1)
    return jnp.stack([slots[o] for o in range(count)], axis=0)


def scatter_tokens(partial):
    count = lax.axis_size("dp")
    order = [o for o in range(count - 2, -1, -2)]
    pair = {}
    for o in order:
        other = xor_send(partial[o ^ 1], "dp", 1)
        pair[o] = partial[o].astype(F32) + other.astype(F32)
    if count == 8:
        half = partial.shape[1] // 2
        far = pair[6].astype(BF16)
        via_x = xor_send(far[:half], "dp", 2)
        via_y = xor_send(far[half:], "dp", 4)
        x_top = xor_send(pair[2][:half].astype(BF16), "dp", 2)
        y_bottom = xor_send(pair[4][half:].astype(BF16), "dp", 4)
        x_bottom = xor_send((pair[2][half:] + via_y.astype(F32)).astype(BF16), "dp", 2)
        y_top = xor_send((pair[4][:half] + via_x.astype(F32)).astype(BF16), "dp", 4)
        return jnp.concatenate(
            [
                pair[0][:half] + x_top.astype(F32) + y_top.astype(F32),
                pair[0][half:] + x_bottom.astype(F32) + y_bottom.astype(F32),
            ],
            axis=0,
        )
    total = pair[0]
    for o in order[:-1]:
        total = total + xor_send(pair[o].astype(BF16), "dp", o).astype(F32)
    return total


def sum_over(value, axis):
    offset = 1
    total = value.astype(F32)
    while offset < lax.axis_size(axis):
        total = total + xor_send(total.astype(value.dtype), axis, offset).astype(F32)
        offset *= 2
    return total


def carry_in(decay, state, steps):
    count = lax.axis_size("seq")
    both = jnp.stack([decay, state], axis=0)
    moved = [shift_send(both, "seq", steps * k) for k in range(1, count)]
    carried = moved[-1][1]
    for item in reversed(moved[:-1]):
        carried = item[1] + item[0] * carried
    return carried


def place_rows(block):
    dp_count, seq_count = lax.axis_size("dp"), lax.axis_size("seq")
    ratio = dp_count // seq_count
    rows, cols = block.shape
    width = cols // ratio
    mine = lax.axis_index("dp")
    parts = block.reshape(rows, ratio, width)
    out = jnp.zeros((ratio, rows, width), block.dtype)
    for turn in range(ratio):
        perm = []
        for d in range(dp_count):
            for s in range(seq_count):
                j = (d + turn) % ratio
                perm.append((d * seq_count + s, (ratio * s + j) * seq_count + d // ratio))
        chosen = lax.dynamic_index_in_dim(parts, (mine + turn) % ratio, 1, keepdims=False)
        got = lax.ppermute(chosen, ("dp", "seq"), perm)
        out = lax.dynamic_update_index_in_dim(out, got, (mine - turn) % ratio, 0)
    return out.reshape(ratio * rows, width)


def scaled_norm(values, gain_vec):
    return (
        values * lax.rsqrt(jnp.mean(values * values, axis=-1, keepdims=True) + EPSILON) * gain_vec
    )


def gelu_pair(v):
    square = v * v
    t = jnp.tanh(GELU_C * (v + GELU_A * v * square))
    half = 0.5 * (1.0 + t)
    slope = half + 0.5 * v * (1.0 - t * t) * (GELU_C * (1.0 + 3.0 * GELU_A * square))
    return v * half, slope


def logistic(v):
    return 1.0 / (1.0 + jnp.exp(-v))


def one_minus_exp(x, exp_x):
    poly = jnp.full_like(x, 1.0 / 362880.0)
    for coef in (1 / 40320.0, 1 / 5040.0, 1 / 720.0, 1 / 120.0, 1 / 24.0, 1 / 6.0, 0.5, 1.0):
        poly = poly * x + coef
    return jnp.where(x > -0.35, -x * poly, 1.0 - exp_x)


def fwd_gates_kernel(
    branch_ref, prior_ref, taps_ref, vec_ref, wr_ref, wi_ref,
    bt_ref, conv_ref, r_ref, i_ref, rate_ref, m_ref, loc_ref, run_ref,
    halo, state, decay,
):
    chunk, slots, width = bt_ref.shape

    @pl.when(pl.program_id(0) == 0)
    def _():
        halo[...] = prior_ref[...]
        state[...] = jnp.zeros_like(state)
        decay[...] = jnp.ones_like(decay)

    bt = jnp.swapaxes(branch_ref[...], 0, 1)
    bt_ref[...] = bt
    lag = halo.shape[0]
    padded = jnp.concatenate([halo[...], bt], axis=0)
    halo[...] = padded[chunk : chunk + lag]
    conv = jnp.zeros_like(bt) + vec_ref[0, :]
    for k in range(lag + 1):
        conv = conv + taps_ref[k, :] * padded[lag - k : lag - k + chunk]
    conv_ref[...] = conv
    rows = conv.reshape(chunk * slots, width).astype(BF16)
    r = logistic(jnp.dot(rows, wr_ref[...], preferred_element_type=F32) + vec_ref[1, :])
    g = logistic(jnp.dot(rows, wi_ref[...], preferred_element_type=F32) + vec_ref[2, :])
    r = r.reshape(chunk, slots, width)
    g = g.reshape(chunk, slots, width)
    log_rate = r * vec_ref[3, :]
    rate = jnp.exp(log_rate)
    m = jnp.sqrt(one_minus_exp(2.0 * log_rate, rate * rate))
    r_ref[...] = r
    i_ref[...] = g
    rate_ref[...] = rate
    m_ref[...] = m
    driven = m * g * conv
    st, dc = state[...], decay[...]
    for t in range(chunk):
        st = rate[t] * st + driven[t]
        dc = rate[t] * dc
        loc_ref[t] = st
        run_ref[t] = dc
    state[...] = st
    decay[...] = dc


def fwd_mix_kernel(
    loc_ref, run_ref, carry_ref, gate_ref, mixed_ref, prev_ref, across_ref, last
):
    chunk = loc_ref.shape[0]

    @pl.when(pl.program_id(0) == 0)
    def _():
        last[...] = carry_ref[...]

    states = loc_ref[...] + run_ref[...] * carry_ref[...]
    prev_ref[...] = jnp.concatenate([last[...][None], states[: chunk - 1]], axis=0)
    last[...] = states[chunk - 1]
    across = jnp.swapaxes(states, 0, 1)
    across_ref[...] = across
    act, _ = gelu_pair(gate_ref[...])
    mixed_ref[...] = (across * act).astype(BF16)


def back_mix_kernel(
    gm_ref, gate_ref, across_ref, rate_ref, ggate_ref, gl_ref, tail_ref, end_ref, held, decay
):
    chunk = rate_ref.shape[0]

    @pl.when(pl.program_id(0) == 0)
    def _():
        held[...] = jnp.zeros_like(held)
        decay[...] = jnp.ones_like(decay)

    gm = gm_ref[...]
    act, slope = gelu_pair(gate_ref[...])
    ggate_ref[...] = (gm * across_ref[...] * slope).astype(BF16)
    gs = jnp.swapaxes(gm * act, 0, 1)
    rate = rate_ref[...]
    h, dc = held[...], decay[...]
    for t in reversed(range(chunk)):
        grad = gs[t] + h
        gl_ref[t] = grad
        tail_ref[t] = dc
        h = rate[t] * grad
        dc = rate[t] * dc
    held[...] = h
    decay[...] = dc
    end_ref[0] = dc
    end_ref[1] = h


def back_gates_kernel(
    gl_ref, tail_ref, rate_ref, m_ref, r_ref, i_ref, conv_ref, prev_ref, bt_ref,
    hin_ref, prior_ref, taps_ref, vec_ref, wr_ref, wi_ref,
    gbranch_ref, last_ref, head_ref, dwr_ref, dwi_ref, sums_ref,
    later,
):
    chunk, slots, width = rate_ref.shape
    lag = later.shape[0]
    step = pl.program_id(0)

    @pl.when(step == 0)
    def _():
        later[...] = jnp.zeros_like(later)
        dwr_ref[...] = jnp.zeros_like(dwr_ref)
        dwi_ref[...] = jnp.zeros_like(dwi_ref)
        sums_ref[...] = jnp.zeros_like(sums_ref)

    s = gl_ref[...] + tail_ref[...] * hin_ref[...]
    rate, m, r, g, conv = rate_ref[...], m_ref[...], r_ref[...], i_ref[...], conv_ref[...]
    sc = s * conv
    dpi = (sc * m * (g * (1.0 - g))).astype(BF16)
    dlog = s * prev_ref[...] * rate - sc * g * (rate * rate) / m
    dpr = (dlog * vec_ref[3, :] * (r * (1.0 - r))).astype(BF16)
    sums_ref[2] += jnp.sum(dlog * r, axis=0)
    sums_ref[0] += jnp.sum(dpr.astype(F32), axis=0)
    sums_ref[1] += jnp.sum(dpi.astype(F32), axis=0)
    rows = conv.reshape(chunk * slots, width).astype(BF16)
    dpr = dpr.astype(F32).reshape(chunk * slots, width).astype(BF16)
    dpi = dpi.astype(F32).reshape(chunk * slots, width).astype(BF16)
    over_rows = (((0,), (0,)), ((), ()))
    over_cols = (((1,), (1,)), ((), ()))
    dwr_ref[...] += lax.dot_general(rows, dpr, over_rows, preferred_element_type=F32)
    dwi_ref[...] += lax.dot_general(rows, dpi, over_rows, preferred_element_type=F32)
    gconv = lax.dot_general(dpr, wr_ref[...], over_cols, preferred_element_type=F32)
    gconv = gconv + lax.dot_general(dpi, wi_ref[...], over_cols, preferred_element_type=F32)
    gconv = gconv.reshape(chunk, slots, width) + s * m * g
    padded = jnp.concatenate([gconv, later[...]], axis=0)
    later[...] = gconv[:lag]
    head_ref[...] = gconv[:lag]
    sums_ref[3] += jnp.sum(gconv, axis=0)
    bt = bt_ref[...]
    gb = jnp.zeros_like(gconv)
    for k in range(lag + 1):
        shifted = padded[k : k + chunk]
        gb = gb + taps_ref[k, :] * shifted
        sums_ref[4 + k] += jnp.sum(bt * shifted, axis=0)

    @pl.when(step == 0)
    def _():
        last_ref[...] = gb[chunk - lag :]

    gbranch_ref[...] = jnp.swapaxes(gb, 0, 1).astype(BF16)

    @pl.when(step == pl.num_programs(0) - 1)
    def _():
        for k in range(1, lag + 1):
            for j in range(1, k + 1):
                sums_ref[4 + k] += prior_ref[lag - j] * gconv[k - j]


def specs_for(slots, length, width, backwards):
    count = length // CHUNK

    def at(c):
        return count - 1 - c if backwards else c

    time_major = pl.BlockSpec((CHUNK, slots, width), lambda c: (at(c), 0, 0))
    slot_major = pl.BlockSpec((slots, CHUNK, width), lambda c: (0, at(c), 0))
    return count, time_major, slot_major


def whole(*shape):
    return pl.BlockSpec(shape, lambda c: (0,) * len(shape))


def params():
    return pltpu.CompilerParams(
        dimension_semantics=("arbitrary",), vmem_limit_bytes=VMEM_LIMIT
    )


def cost(flops, size, trans):
    return pl.CostEstimate(flops=flops, bytes_accessed=size, transcendentals=trans)


def fwd_gates(branch, prior, taps, vecs, wr, wi):
    slots, length, width = branch.shape
    count, tm, sm = specs_for(slots, length, width, False)
    full = jax.ShapeDtypeStruct((length, slots, width), F32)
    n = slots * length * width
    return pl.pallas_call(
        fwd_gates_kernel,
        out_shape=(full,) * 8,
        grid=(count,),
        in_specs=[
            sm, whole(*prior.shape), whole(*taps.shape), whole(*vecs.shape),
            whole(*wr.shape), whole(*wi.shape),
        ],
        out_specs=(tm,) * 8,
        scratch_shapes=[
            pltpu.VMEM(prior.shape, F32),
            pltpu.VMEM((slots, width), F32),
            pltpu.VMEM((slots, width), F32),
        ],
        compiler_params=params(),
        cost_estimate=cost(4 * n * width + 60 * n, 36 * n, 5 * n),
        name="gates_forward",
    )(branch, prior, taps, vecs, wr, wi)


def fwd_mix(loc, run, carry, gate_pre):
    length, slots, width = loc.shape
    count, tm, sm = specs_for(slots, length, width, False)
    n = slots * length * width
    return pl.pallas_call(
        fwd_mix_kernel,
        out_shape=(
            jax.ShapeDtypeStruct((slots, length, width), BF16),
            jax.ShapeDtypeStruct((length, slots, width), F32),
            jax.ShapeDtypeStruct((slots, length, width), F32),
        ),
        grid=(count,),
        in_specs=[tm, tm, whole(slots, width), sm],
        out_specs=(sm, tm, sm),
        scratch_shapes=[pltpu.VMEM((slots, width), F32)],
        compiler_params=params(),
        cost_estimate=cost(20 * n, 22 * n, n),
        name="mix_forward",
    )(loc, run, carry, gate_pre)


def back_mix(gm, gate_pre, across, rate):
    length, slots, width = rate.shape
    count, tm, sm = specs_for(slots, length, width, True)
    n = slots * length * width
    return pl.pallas_call(
        back_mix_kernel,
        out_shape=(
            jax.ShapeDtypeStruct((slots, length, width), BF16),
            jax.ShapeDtypeStruct((length, slots, width), F32),
            jax.ShapeDtypeStruct((length, slots, width), F32),
            jax.ShapeDtypeStruct((2, slots, width), F32),
        ),
        grid=(count,),
        in_specs=[sm, sm, sm, tm],
        out_specs=(sm, tm, tm, whole(2, slots, width)),
        scratch_shapes=[pltpu.VMEM((slots, width), F32), pltpu.VMEM((slots, width), F32)],
        compiler_params=params(),
        cost_estimate=cost(30 * n, 26 * n, n),
        name="mix_backward",
    )(gm, gate_pre, across, rate)


def back_gates(kept, hin, prior, taps, vecs, wr, wi):
    length, slots, width = kept[0].shape
    lag = prior.shape[0]
    count, tm, sm = specs_for(slots, length, width, True)
    n = slots * length * width
    return pl.pallas_call(
        back_gates_kernel,
        out_shape=(
            jax.ShapeDtypeStruct((slots, length, width), BF16),
            jax.ShapeDtypeStruct((lag, slots, width), F32),
            jax.ShapeDtypeStruct((lag, slots, width), F32),
            jax.ShapeDtypeStruct((width, width), F32),
            jax.ShapeDtypeStruct((width, width), F32),
            jax.ShapeDtypeStruct((5 + lag, slots, width), F32),
        ),
        grid=(count,),
        in_specs=[tm] * 9
        + [
            whole(slots, width), whole(*prior.shape), whole(*taps.shape), whole(*vecs.shape),
            whole(*wr.shape), whole(*wi.shape),
        ],
        out_specs=(
            sm, whole(lag, slots, width), whole(lag, slots, width),
            whole(width, width), whole(width, width), whole(5 + lag, slots, width),
        ),
        scratch_shapes=[pltpu.VMEM((lag, slots, width), F32)],
        compiler_params=params(),
        cost_estimate=cost(8 * n * width + 80 * n, 40 * n, 2 * n),
        name="gates_backward",
    )(*kept, hin, prior, taps, vecs, wr, wi)


def rows_of(value):
    return value.reshape(-1, value.shape[-1])


def mm(left, right):
    return jnp.dot(left, right, preferred_element_type=F32)


def mm_back(grad_rows, weight):
    return lax.dot_general(grad_rows, weight, (((1,), (1,)), ((), ())), preferred_element_type=F32)


def mm_weight(left, right):
    return lax.dot_general(left, right, (((0,), (0,)), ((), ())), preferred_element_type=F32)


def after(value, *others):
    return lax.optimization_barrier((value,) + others)[0]


def local(
    block_input, norm_gain, in_proj, gate_proj, conv_kernel, conv_bias,
    recur_weight, recur_bias, input_weight, input_bias, decay_param,
    out_proj, mlp_gain, mlp_gate, mlp_up, mlp_down, out_grad,
):
    dp_count, seq_count = lax.axis_size("dp"), lax.axis_size("seq")
    mine = lax.axis_index("dp")
    model = block_input.shape[2]
    tokens = block_input.reshape(-1, model).astype(F32)
    length = tokens.shape[0]
    recur_width = in_proj.shape[1]
    own = recur_width // dp_count
    width = -(-own // 128) * 128
    hidden_width = mlp_gate.shape[1] // dp_count
    head = recur_weight.shape[1]
    own_heads = own // head
    lag = conv_kernel.shape[0] - 1

    def split_cols(weight, padded):
        part = weight.reshape(weight.shape[0], dp_count, -1)
        return jnp.pad(part, ((0, 0), (0, 0), (0, padded - part.shape[2])))

    def spread(pieces):
        joined = jnp.concatenate(pieces, axis=2)
        got = lax.all_to_all(joined, "dp", split_axis=1, concat_axis=1, tiled=False)
        return got

    def gather_rows(piece):
        full = lax.all_gather(piece, "seq", axis=0)
        return full.transpose(2, 0, 1, 3).reshape(-1, piece.shape[2])

    first = spread([split_cols(in_proj, width), split_cols(gate_proj, width)])
    second = spread([split_cols(mlp_gate, hidden_width), split_cols(mlp_up, hidden_width)])
    w_first = gather_rows(first)
    w_out = lax.all_gather(out_proj, "seq", axis=0, tiled=True)
    w_out = jnp.pad(w_out, ((0, width - own), (0, 0)))
    w_second = gather_rows(second)
    w_down = lax.all_gather(mlp_down, "seq", axis=0, tiled=True)

    def own_cols(value):
        part = lax.dynamic_slice_in_dim(value, mine * own, own, axis=value.ndim - 1)
        return jnp.pad(part, [(0, 0)] * (value.ndim - 1) + [(0, width - own)])

    taps = own_cols(conv_kernel)
    own_decay = own_cols(decay_param)
    vecs = jnp.stack(
        [
            own_cols(conv_bias), own_cols(recur_bias), own_cols(input_bias),
            -8.0 * jax.nn.softplus(-own_decay),
        ],
        axis=0,
    )

    def block_diagonal(weight):
        part = lax.dynamic_slice_in_dim(weight, mine * own_heads, own_heads, axis=0)
        full = jnp.zeros((width, width), weight.dtype)
        for h in range(own_heads):
            full = lax.dynamic_update_slice(full, part[h], (h * head, h * head))
        return full

    wr, wi = block_diagonal(recur_weight), block_diagonal(input_weight)

    normed = scaled_norm(tokens, norm_gain).astype(BF16)
    normed_all = gather_tokens(normed)
    grad_low = out_grad.reshape(length, model)
    grad_all = gather_tokens(after(grad_low, normed_all))
    both = mm(rows_of(normed_all), w_first)
    branch = both[:, :width].reshape(dp_count, length, width)
    gate_pre = both[:, width:].reshape(dp_count, length, width)
    prior = shift_send(jnp.swapaxes(branch[:, length - lag :], 0, 1), "seq", 1)
    bt, conv, r, g, rate, m, loc, run = fwd_gates(branch, prior, taps, vecs, wr, wi)
    carry = carry_in(run[length - 1], loc[length - 1], 1)
    mixed, prev, across = fwd_mix(loc, run, carry, gate_pre)
    partial = mm(rows_of(mixed), w_out).astype(BF16).reshape(dp_count, length, model)
    residual = tokens + scatter_tokens(partial)

    inv_two = lax.rsqrt(jnp.mean(residual * residual, axis=-1, keepdims=True) + EPSILON)
    normed_two = (residual * inv_two * mlp_gain).astype(BF16)
    normed_two_all = rows_of(gather_tokens(normed_two))
    ffn = mm(normed_two_all, w_second)
    act, slope = gelu_pair(ffn[:, :hidden_width])
    up = ffn[:, hidden_width:]
    hidden = (act * up).astype(BF16)
    grad_all = rows_of(grad_all)
    grad_down = mm_weight(hidden, grad_all).astype(BF16)
    down_cols = lax.psum_scatter(grad_down, "seq", scatter_dimension=1, tiled=True)
    grad_hidden = mm_back(grad_all, w_down)
    grad_ffn = jnp.concatenate(
        [(grad_hidden * up * slope).astype(BF16), (grad_hidden * act).astype(BF16)], axis=1
    )
    partial = mm_back(grad_ffn, w_second).astype(BF16).reshape(dp_count, length, model)
    grad_normed_two = scatter_tokens(partial)
    grad_second = mm_weight(normed_two_all, grad_ffn).astype(BF16)
    grad_second = lax.psum_scatter(grad_second, "seq", scatter_dimension=0, tiled=True)
    grad_mgate_w = grad_second[:, :hidden_width].astype(F32)
    grad_mup_w = grad_second[:, hidden_width:].astype(F32)

    def norm_back(grad, values, inv, gain):
        unit = values * inv
        scaled = grad * gain
        mean = jnp.mean(scaled * unit, axis=-1, keepdims=True)
        return inv * (scaled - unit * mean), jnp.sum(grad * unit, axis=0)

    grad_resid, mlp_gain_term = norm_back(grad_normed_two, residual, inv_two, mlp_gain)
    grad_residual = grad_resid + grad_low.astype(F32)

    grad_rec_all = gather_tokens(grad_residual.astype(BF16))
    out_partial = mm(hidden, w_down).astype(BF16).reshape(dp_count, length, model)
    result = residual + scatter_tokens(after(out_partial, grad_rec_all))
    block_output = result.astype(BF16).reshape(block_input.shape)
    grad_rec_all = rows_of(grad_rec_all)
    gm = mm_back(grad_rec_all, w_out).reshape(dp_count, length, width)
    grad_out = mm_weight(rows_of(mixed), grad_rec_all)[:own].astype(BF16)
    out_cols = lax.psum_scatter(grad_out, "seq", scatter_dimension=1, tiled=True)
    ggate, gl, tail, end = back_mix(gm, gate_pre, across, rate)
    hin = carry_in(end[0], end[1], -1)
    gbranch, last, head_rows, dwr, dwi, sums = back_gates(
        (gl, tail, rate, m, r, g, conv, prev, bt), hin, prior, taps, vecs, wr, wi
    )
    later = shift_send(head_rows, "seq", -1)
    fixed = []
    for j in range(lag):
        row = last[j]
        for k in range(lag - j, lag + 1):
            row = row + taps[k] * later[j + k - lag]
        fixed.append(row)
    fixed = jnp.stack(fixed, axis=1).astype(BF16)
    gbranch = lax.dynamic_update_slice(gbranch, fixed, (0, length - lag, 0))
    grad_first = jnp.concatenate([rows_of(gbranch), rows_of(ggate)], axis=1)
    partial = mm_back(grad_first, w_first).astype(BF16).reshape(dp_count, length, model)
    grad_normed = scatter_tokens(partial)
    grad_first_w = mm_weight(rows_of(normed_all), grad_first).astype(BF16)
    grad_first_w = lax.psum_scatter(grad_first_w, "seq", scatter_dimension=0, tiled=True)
    grad_in_w = grad_first_w[:, :own].astype(F32)
    grad_gate_w = grad_first_w[:, width : width + own].astype(F32)
    inv_one = lax.rsqrt(jnp.mean(tokens * tokens, axis=-1, keepdims=True) + EPSILON)
    grad_tokens, norm_gain_term = norm_back(grad_normed, tokens, inv_one, norm_gain)
    input_grad = (grad_tokens + grad_residual).reshape(block_input.shape)

    grad_down_w = place_rows(down_cols).astype(F32)
    grad_out_w = place_rows(out_cols).astype(F32)

    sums = jnp.sum(sums, axis=1)[:, :own]
    decay_scale = 8.0 * jax.nn.sigmoid(-own_decay[:own])
    sums = jnp.concatenate([sums[:2], (sums[2] * decay_scale)[None], sums[3:]], axis=0)
    sums = lax.all_gather(sum_over(sums, "seq"), "dp", axis=1, tiled=True)

    def diagonal(full):
        return jnp.stack(
            [full[h * head : (h + 1) * head, h * head : (h + 1) * head] for h in range(own_heads)]
        )

    blocks = jnp.stack([diagonal(dwr), diagonal(dwi)]).astype(BF16)
    blocks = sum_over(blocks, "seq").astype(BF16)
    blocks = lax.all_gather(blocks, "dp", axis=1, tiled=True).astype(F32)
    gains = sum_over(sum_over(jnp.stack([norm_gain_term, mlp_gain_term]), "dp"), "seq")
    return (
        block_output,
        input_grad,
        gains[0],
        grad_in_w,
        grad_gate_w,
        sums[4:],
        sums[3],
        blocks[0],
        sums[0],
        blocks[1],
        sums[1],
        sums[2],
        grad_out_w,
        gains[1],
        grad_mgate_w,
        grad_mup_w,
        grad_down_w,
    )


def solution(mesh):
    rows = P(("dp", "seq"), None)
    acts = P("dp", "seq", None)
    grads = P("seq", "dp")
    return jax.shard_map(
        local,
        mesh=mesh,
        in_specs=(
            acts, P(), rows, rows, P(), P(), P(), P(), P(), P(), P(), rows, P(), rows, rows, rows,
            acts,
        ),
        out_specs=(
            acts, acts, P(), grads, grads, P(), P(), P(), P(), P(), P(), P(), grads, P(), grads,
            grads, grads,
        ),
        check_vma=False,
    )
```

time: 3400 us -> 852 us (0.25)
  waiting for transfers between devices: 2420 us -> 346 us
  local copies, waits for them, and re-layouts: 523 us -> 79 us
  starting transfers between devices: 21.7 us -> 124 us
  other arithmetic: 158 us -> 57.6 us
  matrix products: 237 us -> 150 us
  Pallas kernels: 0 us -> 44.4 us
    reduce_scatter x10 -> x4, waiting for transfers between devices: 1640 us -> 0.03 us  [the longest x1 0.02 us: local(): lax.psum_scatter(grad_out, 'seq', scatter_dimension=1, tiled=True)]
    all_gather x6 -> x5, waiting for transfers between devices: 418 us -> 0.01 us  [the longest x2 0.01 us: gather_rows(): full = lax.all_gather(piece, 'seq', axis=0)]
    ppermute x8 -> x97, waiting for transfers between devices: 14.7 us -> 329 us  [the longest x85 281 us: xor_send(): return lax.ppermute(value, axis, [(i, i ^ offset) for i in range(count)])]
    psum x2 -> x0, waiting for transfers between devices: 288 us -> none  [local(): lax.psum((norm_gain_term, kernel_term, bias_term, recur_w_term, recur_b_t...]
    slice x113 -> x35, local copies, waits for them, and re-layouts: 283 us -> 20.5 us  [the longest x3 7.3 us: scatter_tokens(): other = xor_send(partial[o ^ 1], 'dp', 1)]
    pad x56 -> x4, local copies, waits for them, and re-layouts: 137 us -> 0.02 us  [own_cols(): return jnp.pad(part, [(0, 0)] * (value.ndim - 1) + [(0, width - own)])]
    ppermute x8 -> x97, starting transfers between devices: 20.9 us -> 118 us  [the longest x85 87.5 us: xor_send(): return lax.ppermute(value, axis, [(i, i ^ offset) for i in range(count)])]
    dot_general x24 -> x12, matrix products: 237 us -> 150 us  [the longest x4 58.2 us: mm_back(): lax.dot_general(grad_rows, weight, (((1,), (1,)), ((), ())), preferred_el...]
  transfers between devices with their start and end apart: 28 -> 107, of which waited for: 23 -> 47; matrix products, arithmetic and copies ran while one was open for 24% -> 26% of each run, Pallas kernels for 0% -> 5%
where the time goes in v1:
time: 852 us; the launch traced here: 842 us
  waiting for transfers between devices  346 us (41%)
  matrix products  150 us (18%)
  starting transfers between devices  124 us (15%)
  local copies, waits for them, and re-layouts  79 us (9%)
  other arithmetic  57.6 us (7%)
  Pallas kernels  44.4 us (5%)
  blocking collectives  25.2 us (3%)
  between operations  15.8 us (2%)
    ppermute x85, waiting for transfers between devices, xor_send(): return lax.ppermute(value, axis, [(i, i ^ offset) for i in range(count)])  281 us
    ppermute x85, starting transfers between devices, xor_send(): return lax.ppermute(value, axis, [(i, i ^ offset) for i in range(count)])  87.5 us
    dot_general x4, matrix products, mm_back(): lax.dot_general(grad_rows, weight, (((1,), (1,)), ((), ())), preferred_el...  58.2 us
    dot_general x4, matrix products, mm(): return jnp.dot(left, right, preferred_element_type=F32)  47.4 us
    dot_general x4, matrix products, mm_weight(): lax.dot_general(left, right, (((0,), (0,)), ((), ())), preferred_element_...  44.5 us
    ppermute x4, waiting for transfers between devices, place_rows(): got = lax.ppermute(chosen, ('dp', 'seq'), perm)  36.5 us
    unnamed x123, local copies, waits for them, and re-layouts  32.4 us
    convert_element_type x4, other arithmetic, scatter_tokens(): far = pair[6].astype(BF16)  19.6 us
  transfers between devices with their start and end apart: 107, of which 47 were waited for; matrix products, arithmetic and copies ran while one was open for 26% of the time, Pallas kernels for 5%

profile of v1, /device:TPU:3, one launch (start us, length us, event | category | flops | bytes accessed | tf_op | source)
XLA Modules:
  0.0 841.5 jit_solution(11449278292195275925)
XLA Ops:
  10.9 15.3 %all_to_all.10 = bf16[64,8,768]{2,0,1:T(8,128)(2,1)} all-to-all(bf16[64,8,768]{2,0,1:T(8,128)(2,1)S(1)} %fusion.56), channel_id=1, replica_groups=mesh['dp'=8,'seq'=4] {'dp'}, dimensions={1} | all-to-all | bytes 1572864 | tf_op jit(solution)/shard_map/all_to_all | solution.py:465
  37.8 15.6 %all-to-all-done.1 = bf16[64,8,1536]{2,0,1:T(8,128)(2,1)S(1)} async-done(((bf16[64,8,1536]{2,0,1:T(8,128)(2,1)}), bf16[64,8,1536]{2,0,1:T(8,128)(2,1)S(1)}, u32[]{:S(2)}, u32[]{:S(2)}) %all-to-all-start.1) | async-done | bytes 1572896 | tf_op jit(solution)/shard_map/all_to_all | solution.py:465
  57.8 16.8 %collective-permute-done.1 = bf16[256,2048]{1,0:T(8,128)(2,1)} collective-permute-done((bf16[256,2048]{1,0:T(8,128)(2,1)}, bf16[256,2048]{1,0:T(8,128)(2,1)}, u32[]{:S(2)}, u32[]{:S(2)}) %collective-permute-start.1) | collective-permute-done | bytes 1048608 | tf_op jit(solution)/shard_map/ppermute | solution.py:19
  102.3 10.0 %fusion.90 = f32[2048,768]{1,0:T(8,128)S(1)} fusion(bf16[2048,2048]{1,0:T(8,128)(2,1)} %bitcast.8, bf16[2048,768]{1,0:T(8,128)(2,1)} %bitcast.342), kind=kOutput, calls=%fused_computation.263 | convolution fusion | flops 6442450944 | bytes 17825792 | tf_op jit(solution)/shard_map/dot_general | solution.py:426
  121.5 12.2 %gates_forward.1 = (f32[256,8,384]{2,1,0:T(8,128)S(1)}, f32[256,8,384]{2,1,0:T(8,128)}, f32[256,8,384]{2,1,0:T(8,128)}, f32[256,8,384]{2,1,0:T(8,128)}, f32[256,...) custom-call(f32[8,256,384]{2,1,0:T(8,128)} %bitcast.320, ...), custom_call_target="tpu_custom_call" | custom-call | flops 1255145472 | bytes 28311552 | tf_op jit(solution)/shard_map/gates_forward/pallas_call | solution.py:326
  146.7 8.3 mix_forward.1
  184.6 14.9 %collective-permute-done.35 = bf16[256,2048]{1,0:T(8,128)(2,1)S(1)} collective-permute-done((bf16[256,2048]{1,0:T(8,128)(2,1)}, bf16[256,2048]{1,0:T(8,128)(2,1)S(1)}, u32[]{:S(2)}, u32[]{:S(2)}) %collective-permute-start.35) | collective-permute-done | bytes 1048608 | tf_op jit(solution)/shard_map/ppermute | solution.py:19
  211.0 11.5 %collective-permute-done.18 = bf16[128,2048]{1,0:T(8,128)(2,1)S(1)} collective-permute-done((bf16[128,2048]{1,0:T(8,128)(2,1)S(1)}, bf16[128,2048]{1,0:T(8,128)(2,1)S(1)}, u32[]{:S(2)}, u32[]{:S(2)}) %collective-permute-start.18) | collective-permute-done | bytes 524320 | tf_op jit(solution)/shard_map/ppermute | solution.py:19
  252.0 16.1 %collective-permute-done.24 = bf16[256,2048]{1,0:T(8,128)(2,1)S(1)} collective-permute-done((bf16[256,2048]{1,0:T(8,128)(2,1)S(1)}, bf16[256,2048]{1,0:T(8,128)(2,1)S(1)}, u32[]{:S(2)}, u32[]{:S(2)}) %collective-permute-start.24) | collective-permute-done | bytes 1048608 | tf_op jit(solution)/shard_map/ppermute | solution.py:19
  296.4 19.4 %fusion.91 = f32[2048,1536]{0,1:T(8,128)} fusion(bf16[2048,2048]{1,0:T(8,128)(2,1)} %bitcast.30, bf16[2048,1536]{1,0:T(8,128)(2,1)} %bitcast.340), kind=kOutput, calls=%fused_computation.264 | convolution fusion | flops 12884901888 | bytes 27262976 | tf_op jit(solution)/shard_map/dot_general | solution.py:426
  315.8 19.3 %multiply_convert_fusion.1 = (bf16[2048,768]{0,1:T(8,128)(2,1)}, bf16[2048,768]{0,1:T(8,128)(2,1)}, bf16[2048,768]{0,1:T(8,128)(2,1)S(1)}) fusion(f32[2048,1536]{0,1:T(8,128)} %fusion.91, bf16[2048,2048]{1,0:T(8,128)(2,1)} %bitcast.335, bf16[768,2048]{1,0:T(8,128)(2,1)} %all-gather.11.cloned.1.call-done), kind=kOutput, calls=%fused_computation.7 | convolution fusion | flops 6480199680 | bytes 33554432 | tf_op jit(solution)/shard_map/dot_general | solution.py:430
  335.1 20.4 %convolution_convert_fusion.1 = bf16[2048,2048]{1,0:T(8,128)(2,1)} fusion(bf16[2048,1536]{1,0:T(8,128)(2,1)} %bitcast.341, bf16[2048,768]{0,1:T(8,128)(2,1)} %get-tuple-element.143, bf16[2048,768]{0,1:T(8,128)(2,1)} %get-tuple-element.142), kind=kOutput, calls=%fused_computation.1 | convolution fusion | flops 12901679104 | bytes 20971520 | tf_op jit(solution)/shard_map/dot_general | solution.py:430
  373.7 8.7 %collective-permute-done.48 = bf16[128,2048]{1,0:T(8,128)(2,1)S(1)} collective-permute-done((bf16[128,2048]{1,0:T(8,128)(2,1)S(1)}, bf16[128,2048]{1,0:T(8,128)(2,1)S(1)}, u32[]{:S(2)}, u32[]{:S(2)}) %collective-permute-start.48) | collective-permute-done | bytes 524320 | tf_op jit(solution)/shard_map/ppermute | solution.py:19
  385.6 10.5 %convolution_convert_fusion.5 = bf16[768,2048]{1,0:T(8,128)(2,1)} fusion(bf16[2048,768]{0,1:T(8,128)(2,1)S(1)} %get-tuple-element.144, bf16[2048,2048]{1,0:T(8,128)(2,1)} %bitcast.336), kind=kOutput, calls=%fused_computation.13 | convolution fusion | flops 6444023808 | bytes 14680064 | tf_op jit(solution)/shard_map/dot_general | solution.py:434
  396.2 9.7 %collective-permute-done.49 = bf16[128,2048]{1,0:T(8,128)(2,1)} collective-permute-done((bf16[128,2048]{1,0:T(8,128)(2,1)}, bf16[128,2048]{1,0:T(8,128)(2,1)}, u32[]{:S(2)}, u32[]{:S(2)}) %collective-permute-start.49) | collective-permute-done | bytes 524320 | tf_op jit(solution)/shard_map/ppermute | solution.py:19
  413.8 21.2 %collective-permute-done.52 = bf16[256,2048]{1,0:T(8,128)(2,1)S(1)} collective-permute-done((bf16[256,2048]{1,0:T(8,128)(2,1)S(1)}, bf16[256,2048]{1,0:T(8,128)(2,1)S(1)}, u32[]{:S(2)}, u32[]{:S(2)}) %collective-permute-start.52) | collective-permute-done | bytes 1048608 | tf_op jit(solution)/shard_map/ppermute | solution.py:19
  440.2 11.5 %collective-permute-done.56 = bf16[128,2048]{1,0:T(8,128)(2,1)S(1)} collective-permute-done((bf16[128,2048]{1,0:T(8,128)(2,1)S(1)}, bf16[128,2048]{1,0:T(8,128)(2,1)S(1)}, u32[]{:S(2)}, u32[]{:S(2)}) %collective-permute-start.56) | collective-permute-done | bytes 524320 | tf_op jit(solution)/shard_map/ppermute | solution.py:19
  460.3 9.0 %fusion.22.gm_ref = f32[8,256,384]{2,1,0:T(8,128)} fusion(bf16[8,256,2048]{2,1,0:T(8,128)(2,1)} %copy-done.37, bf16[352,2048]{1,0:T(8,128)(2,1)S(1)} %copy-done.43), kind=kOutput, calls=%fused_computation.74 | convolution fusion | flops 3221225472 | bytes 12976128 | tf_op jit(solution)/shard_map/dot_general | solution.py:430
  469.3 9.4 %mix_backward.1 = (bf16[8,256,384]{2,1,0:T(8,128)(2,1)S(1)}, f32[256,8,384]{2,1,0:T(8,128)S(1)}, f32[256,8,384]{2,1,0:T(8,128)}, f32[2,8,384]{2,1,0:T(8,128)S(1)}) custom-call(f32[8,256,384]{2,1,0:T(8,128)} %fusion.22.gm_ref, f32[8,256,384]{2,1,0:T(8,128)} %bitcast.304, f32[8,256,384]{2,1,0:T(8,128)} %get-tuple-element.45.across_ref, ...), custom_call_target="tpu_custom_call" | custom-call | flops 23592960 | bytes 20447232 | tf_op jit(solution)/shard_map/mix_backward/pallas_call | solution.py:371
  491.5 14.5 %gates_backward.1 = (bf16[8,256,384]{2,1,0:T(8,128)(2,1)S(1)}, f32[3,8,384]{2,1,0:T(8,128)S(1)}, f32[3,8,384]{2,1,0:T(8,128)S(1)}, f32[384,384]{1,0:T(8,128)S(1)...) custom-call(f32[256,8,384]{2,1,0:T(8,128)} %copy-done.4, f32[256,8,384]{2,1,0:T(8,128)} %get-tuple-element.48.tail_ref, ...), custom_call_target="tpu_custom_call" | custom-call | flops 2478833664 | bytes 31457280 | tf_op jit(solution)/shard_map/gates_backward/pallas_call | solution.py:394
  507.6 8.6 %collective-permute-done.91 = bf16[2,2,176,176]{3,2,1,0:T(8,128)(2,1)S(1)} collective-permute-done((bf16[2,2,176,176]{3,2,1,0:T(8,128)(2,1)S(1)}, bf16[2,2,176,176]{3,2,1,0:T(8,128)(2,1)S(1)}, u32[]{:S(2)}, u32[]{:S(2)}) %collective-permute-start.91) | collective-permute-done | bytes 247840 | tf_op jit(solution)/shard_map/ppermute | solution.py:19
  516.4 18.9 %collective-permute-done.92 = bf16[2,2,176,176]{3,2,1,0:T(8,128)(2,1)S(1)} collective-permute-done((bf16[2,2,176,176]{3,2,1,0:T(8,128)(2,1)S(1)}, bf16[2,2,176,176]{3,2,1,0:T(8,128)(2,1)S(1)}, u32[]{:S(2)}, u32[]{:S(2)}) %collective-permute-start.92) | collective-permute-done | bytes 247840 | tf_op jit(solution)/shard_map/ppermute | solution.py:19
  542.5 10.9 %convolution_convert_fusion.6 = bf16[2048,768]{1,0:T(8,128)(2,1)} fusion(bf16[2048,2048]{1,0:T(8,128)(2,1)} %bitcast.8, bf16[2048,384]{1,0:T(8,128)(2,1)S(1)} %bitcast.293, bf16[2048,384]{1,0:T(8,128)(2,1)} %bitcast.295), kind=kOutput, calls=%fused_computation.14 | convolution fusion | flops 6450315264 | bytes 14680064 | tf_op jit(solution)/shard_map/dot_general | solution.py:434
  553.6 19.4 %convolution_convert_fusion.4 = bf16[2048,1536]{1,0:T(8,128)(2,1)} fusion(bf16[2048,2048]{1,0:T(8,128)(2,1)} %bitcast.30, bf16[2048,768]{0,1:T(8,128)(2,1)} %get-tuple-element.143, bf16[2048,768]{0,1:T(8,128)(2,1)} %get-tuple-element.142), kind=kOutput, calls=%fused_computation.4 | convolution fusion | flops 12900630528 | bytes 20971520 | tf_op jit(solution)/shard_map/dot_general | solution.py:434
  573.0 11.8 %convolution_convert_fusion.2 = bf16[2048,2048]{1,0:T(8,128)(2,1)} fusion(bf16[2048,768]{0,1:T(8,128)(2,1)} %copy-done.44, bf16[768,2048]{1,0:T(8,128)(2,1)} %all-gather.11.cloned.1.call-done), kind=kOutput, calls=%fused_computation.2 | convolution fusion | flops 6446645248 | bytes 14680064 | tf_op jit(solution)/shard_map/dot_general | solution.py:426
  586.3 9.5 %convolution_convert_fusion = bf16[2048,2048]{1,0:T(8,128)(2,1)S(1)} fusion(bf16[2048,768]{1,0:T(8,128)(2,1)} %bitcast.343, bf16[2048,384]{1,0:T(8,128)(2,1)S(1)} %bitcast.294, bf16[2048,384]{1,0:T(8,128)(2,1)} %bitcast.296), kind=kOutput, calls=%fused_computation | convolution fusion | flops 6452936704 | bytes 14680064 | tf_op jit(solution)/shard_map/dot_general | solution.py:430
  607.9 9.9 %all-gather.2 = f32[8,352,8]{1,2,0:T(8,128)S(1)} all-gather(f32[1,352,8]{1,2,0:T(8,128)S(1)} %add_bitcast_fusion), channel_id=1, replica_groups=mesh['dp'=8,'seq'=4] {'dp'}, dimensions={0}, use_global_device_ids=true | all-gather | bytes 101376 | tf_op jit(solution)/shard_map/all_gather | solution.py:586
  686.6 14.0 %collective-permute-done.85 = f32[2,2048]{1,0:T(2,128)S(1)} collective-permute-done((f32[2,2048]{1,0:T(2,128)S(1)}, f32[2,2048]{1,0:T(2,128)S(1)}, u32[]{:S(2)}, u32[]{:S(2)}) %collective-permute-start.85) | collective-permute-done | bytes 16416 | tf_op jit(solution)/shard_map/ppermute | solution.py:19
  711.7 25.3 %collective-permute-done.87 = f32[2,2048]{1,0:T(2,128)S(1)} collective-permute-done((f32[2,2048]{1,0:T(2,128)S(1)}, f32[2,2048]{1,0:T(2,128)S(1)}, u32[]{:S(2)}, u32[]{:S(2)}) %collective-permute-start.87) | collective-permute-done | bytes 16416 | tf_op jit(solution)/shard_map/ppermute | solution.py:19
  742.2 31.2 %collective-permute-done.88 = f32[2,2048]{1,0:T(2,128)S(1)} collective-permute-done((f32[2,2048]{1,0:T(2,128)S(1)}, f32[2,2048]{1,0:T(2,128)S(1)}, u32[]{:S(2)}, u32[]{:S(2)}) %collective-permute-start.88) | collective-permute-done | bytes 16416 | tf_op jit(solution)/shard_map/ppermute | solution.py:19
  774.1 15.8 %collective-permute-done.96 = bf16[768,256]{1,0:T(8,128)(2,1)S(1)} collective-permute-done((bf16[768,256]{1,0:T(8,128)(2,1)S(1)}, bf16[768,256]{1,0:T(8,128)(2,1)S(1)}, u32[]{:S(2)}, u32[]{:S(2)}) %collective-permute-start.96) | collective-permute-done | bytes 393248 | tf_op jit(solution)/shard_map/ppermute | solution.py:115
  800.7 20.7 %collective-permute-done.94 = bf16[352,256]{1,0:T(8,128)(2,1)S(1)} collective-permute-done((bf16[352,256]{1,0:T(8,128)(2,1)S(1)}, bf16[352,256]{1,0:T(8,128)(2,1)S(1)}, u32[]{:S(2)}, u32[]{:S(2)}) %collective-permute-start.94) | collective-permute-done | bytes 180256 | tf_op jit(solution)/shard_map/ppermute | solution.py:115
  (480 shorter events, 355.2 us)
Async XLA Ops:
  7.2 95.1 %all-gather.15.cloned.1.call-start = ((), (), s32[]{:S(2)}) async-start(), calls=%async_computation.13 | async-start | bytes 3932160 | tf_op jit(solution)/shard_map/all_gather | solution.py:469
  26.3 130.4 %all-gather.9.cloned.1.call-start = ((), (), s32[]{:S(2)}) async-start(), calls=%async_computation.6 | async-start | bytes 1802240 | tf_op jit(solution)/shard_map/all_gather | solution.py:475
  33.8 262.5 %all-gather.17.cloned.1.call-start = ((), (), s32[]{:S(2)}) async-start(), calls=%async_computation.14 | async-start | bytes 7864320 | tf_op jit(solution)/shard_map/all_gather | solution.py:469
  35.4 39.2 %collective-permute-start.1 = (bf16[256,2048]{1,0:T(8,128)(2,1)}, bf16[256,2048]{1,0:T(8,128)(2,1)}, u32[]{:S(2)}, u32[]{:S(2)}) collective-permute-start(bf16[256,2048]{1,0:T(8,128)(2,1)} %fusion.13), channel_id=1, source_target_pairs={{0,8},{4,12},{8,0},{12,4},{16,24},{20,28},{24,16},{28,20},{1,9},{5... | collective-permute-start | bytes 3145736 | tf_op jit(solution)/shard_map/ppermute | solution.py:19
  35.5 42.1 %collective-permute-start.3 = (bf16[256,2048]{1,0:T(8,128)(2,1)}, bf16[256,2048]{1,0:T(8,128)(2,1)}, u32[]{:S(2)}, u32[]{:S(2)}) collective-permute-start(bf16[256,2048]{1,0:T(8,128)(2,1)} %fusion.13), channel_id=1, source_target_pairs={{0,16},{4,20},{8,24},{12,28},{16,0},{20,4},{24,8},{28,12},{1,17},{... | collective-permute-start | bytes 3145736 | tf_op jit(solution)/shard_map/ppermute | solution.py:19
  36.9 46.2 %collective-permute-start = (bf16[256,2048]{1,0:T(8,128)(2,1)}, bf16[256,2048]{1,0:T(8,128)(2,1)}, u32[]{:S(2)}, u32[]{:S(2)}) collective-permute-start(bf16[256,2048]{1,0:T(8,128)(2,1)} %fusion.13), channel_id=1, source_target_pairs={{0,4},{4,0},{8,12},{12,8},{16,20},{20,16},{24,28},{28,24},{1,5},{5... | collective-permute-start | bytes 3145736 | tf_op jit(solution)/shard_map/ppermute | solution.py:19
  54.6 261.2 %all-gather.11.cloned.1.call-start = ((), (), s32[]{:S(2)}) async-start(), calls=%async_computation.7 | async-start | bytes 3932160 | tf_op jit(solution)/shard_map/all_gather | solution.py:478
  169.7 509.1 %reduce-scatter.11.cloned.1.call-start = ((), (), s32[]{:S(2)}) async-start(), calls=%async_computation.12 | async-start | bytes 3932160 | tf_op jit(solution)/shard_map/reduce_scatter | solution.py:526
  169.8 33.8 %collective-permute-start.32 = (bf16[256,2048]{1,0:T(8,128)(2,1)}, bf16[256,2048]{1,0:T(8,128)(2,1)S(1)}, u32[]{:S(2)}, u32[]{:S(2)}) collective-permute-start(bf16[256,2048]{1,0:T(8,128)(2,1)} %bitcast.309), channel_id=1, source_target_pairs={{0,4},{4,0},{8,12},{12,8},{16,20},{20,16},{24,28},{28,24},{1,5},{5... | collective-permute-start | bytes 3145736 | tf_op jit(solution)/shard_map/ppermute | solution.py:19
  171.8 28.0 %collective-permute-start.33 = (bf16[256,2048]{1,0:T(8,128)(2,1)}, bf16[256,2048]{1,0:T(8,128)(2,1)S(1)}, u32[]{:S(2)}, u32[]{:S(2)}) collective-permute-start(bf16[256,2048]{1,0:T(8,128)(2,1)} %bitcast.310), channel_id=1, source_target_pairs={{0,8},{4,12},{8,0},{12,4},{16,24},{20,28},{24,16},{28,20},{1,9},{5... | collective-permute-start | bytes 3145736 | tf_op jit(solution)/shard_map/ppermute | solution.py:19
  183.3 27.5 %collective-permute-start.20 = (bf16[128,2048]{1,0:T(8,128)(2,1)S(1)}, bf16[128,2048]{1,0:T(8,128)(2,1)S(1)}, u32[]{:S(2)}, u32[]{:S(2)}) collective-permute-start(bf16[128,2048]{1,0:T(8,128)(2,1)S(1)} %get-tuple-element.204), channel_id=1, source_target_pairs={{0,16},{4,20},{8,24},{12,28},{16,0},{20,4},{24,8},{28,12},{1,17},{... | collective-permute-start | bytes 1572872 | tf_op jit(solution)/shard_map/ppermute | solution.py:19
  224.5 25.8 %collective-permute-start.36 = (bf16[256,2048]{1,0:T(8,128)(2,1)S(1)}, bf16[256,2048]{1,0:T(8,128)(2,1)S(1)}, u32[]{:S(2)}, u32[]{:S(2)}) collective-permute-start(bf16[256,2048]{1,0:T(8,128)(2,1)S(1)} %collective-permute-done.35), channel_id=1, source_target_pairs={{0,4},{4,0},{8,12},{12,8},{16,20},{20,16},{24,28},{28,24},{1,5},{5... | collective-permute-start | bytes 3145736 | tf_op jit(solution)/shard_map/ppermute | solution.py:19
  246.8 32.5 %collective-permute-start.23 = (bf16[256,2048]{1,0:T(8,128)(2,1)S(1)}, bf16[256,2048]{1,0:T(8,128)(2,1)S(1)}, u32[]{:S(2)}, u32[]{:S(2)}) collective-permute-start(bf16[256,2048]{1,0:T(8,128)(2,1)S(1)} %multiply_convert_fusion.3), channel_id=1, source_target_pairs={{0,4},{4,0},{8,12},{12,8},{16,20},{20,16},{24,28},{28,24},{1,5},{5... | collective-permute-start | bytes 3145736 | tf_op jit(solution)/shard_map/ppermute | solution.py:19
  371.3 24.9 %collective-permute-start.43 = (bf16[128,2048]{1,0:T(8,128)(2,1)}, bf16[128,2048]{1,0:T(8,128)(2,1)}, u32[]{:S(2)}, u32[]{:S(2)}) collective-permute-start(bf16[128,2048]{1,0:T(8,128)(2,1)} %slice.816), channel_id=1, source_target_pairs={{0,8},{4,12},{8,0},{12,4},{16,24},{20,28},{24,16},{28,20},{1,9},{5... | collective-permute-start | bytes 1572872 | tf_op jit(solution)/shard_map/ppermute | solution.py:19
  396.1 393.8 %reduce-scatter.7.cloned.1.call-start = ((), (), s32[]{:S(2)}) async-start(), calls=%async_computation.10 | async-start | bytes 1802240 | tf_op jit(solution)/shard_map/reduce_scatter | solution.py:554
  411.7 26.2 %collective-permute-start.54 = (bf16[256,2048]{1,0:T(8,128)(2,1)S(1)}, bf16[256,2048]{1,0:T(8,128)(2,1)S(1)}, u32[]{:S(2)}, u32[]{:S(2)}) collective-permute-start(bf16[256,2048]{1,0:T(8,128)(2,1)S(1)} %add_convert_fusion.1), channel_id=1, source_target_pairs={{0,16},{4,20},{8,24},{12,28},{16,0},{20,4},{24,8},{28,12},{1,17},{... | collective-permute-start | bytes 3145736 | tf_op jit(solution)/shard_map/ppermute | solution.py:19
  412.4 27.6 %collective-permute-start.51 = (bf16[256,2048]{1,0:T(8,128)(2,1)S(1)}, bf16[256,2048]{1,0:T(8,128)(2,1)S(1)}, u32[]{:S(2)}, u32[]{:S(2)}) collective-permute-start(bf16[256,2048]{1,0:T(8,128)(2,1)S(1)} %add_convert_fusion.1), channel_id=1, source_target_pairs={{0,4},{4,0},{8,12},{12,8},{16,20},{20,16},{24,28},{28,24},{1,5},{5... | collective-permute-start | bytes 3145736 | tf_op jit(solution)/shard_map/ppermute | solution.py:19
  459.7 362.7 %all-gather.13.cloned.1.call-start = ((), (), s32[]{:S(2)}) async-start(), calls=%async_computation.9 | async-start | bytes 3244032 | tf_op jit(solution)/shard_map/all_gather | solution.py:595
  536.3 291.6 %reduce-scatter.5.cloned.1.call-start = ((), (), s32[]{:S(2)}) async-start(), calls=%async_computation.8 | async-start | bytes 3932160 | tf_op jit(solution)/shard_map/reduce_scatter | solution.py:573
  553.5 277.8 %reduce-scatter.9.cloned.1.call-start = ((), (), s32[]{:S(2)}) async-start(), calls=%async_computation.11 | async-start | bytes 7864320 | tf_op jit(solution)/shard_map/reduce_scatter | solution.py:534
  633.1 26.7 %collective-permute-start.83 = (bf16[128,2048]{1,0:T(8,128)(2,1)S(1)}, bf16[128,2048]{1,0:T(8,128)(2,1)S(1)}, u32[]{:S(2)}, u32[]{:S(2)}) collective-permute-start(bf16[128,2048]{1,0:T(8,128)(2,1)S(1)} %slice.811), channel_id=1, source_target_pairs={{0,16},{4,20},{8,24},{12,28},{16,0},{20,4},{24,8},{28,12},{1,17},{... | collective-permute-start | bytes 1572872 | tf_op jit(solution)/shard_map/ppermute | solution.py:19
  637.4 29.1 %collective-permute-start.82 = (bf16[128,2048]{1,0:T(8,128)(2,1)S(1)}, bf16[128,2048]{1,0:T(8,128)(2,1)S(1)}, u32[]{:S(2)}, u32[]{:S(2)}) collective-permute-start(bf16[128,2048]{1,0:T(8,128)(2,1)S(1)} %fusion.30), channel_id=1, source_target_pairs={{0,8},{4,12},{8,0},{12,4},{16,24},{20,28},{24,16},{28,20},{1,9},{5... | collective-permute-start | bytes 1572872 | tf_op jit(solution)/shard_map/ppermute | solution.py:19
  644.2 26.9 %collective-permute-start.80 = (bf16[128,2048]{1,0:T(8,128)(2,1)S(1)}, bf16[128,2048]{1,0:T(8,128)(2,1)S(1)}, u32[]{:S(2)}, u32[]{:S(2)}) collective-permute-start(bf16[128,2048]{1,0:T(8,128)(2,1)S(1)} %fusion.32), channel_id=1, source_target_pairs={{0,16},{4,20},{8,24},{12,28},{16,0},{20,4},{24,8},{28,12},{1,17},{... | collective-permute-start | bytes 1572872 | tf_op jit(solution)/shard_map/ppermute | solution.py:19
  648.6 29.1 %collective-permute-start.65 = (bf16[128,2048]{1,0:T(8,128)(2,1)S(1)}, bf16[128,2048]{1,0:T(8,128)(2,1)S(1)}, u32[]{:S(2)}, u32[]{:S(2)}) collective-permute-start(bf16[128,2048]{1,0:T(8,128)(2,1)S(1)} %get-tuple-element.199), channel_id=1, source_target_pairs={{0,8},{4,12},{8,0},{12,4},{16,24},{20,28},{24,16},{28,20},{1,9},{5... | collective-permute-start | bytes 1572872 | tf_op jit(solution)/shard_map/ppermute | solution.py:19
  655.3 47.2 %collective-permute-start.62 = (bf16[128,2048]{1,0:T(8,128)(2,1)}, bf16[128,2048]{1,0:T(8,128)(2,1)}, u32[]{:S(2)}, u32[]{:S(2)}) collective-permute-start(bf16[128,2048]{1,0:T(8,128)(2,1)} %slice.814), channel_id=1, source_target_pairs={{0,8},{4,12},{8,0},{12,4},{16,24},{20,28},{24,16},{28,20},{1,9},{5... | collective-permute-start | bytes 1572872 | tf_op jit(solution)/shard_map/ppermute | solution.py:19
  659.9 46.7 %collective-permute-start.69 = (bf16[128,2048]{1,0:T(8,128)(2,1)}, bf16[128,2048]{1,0:T(8,128)(2,1)}, u32[]{:S(2)}, u32[]{:S(2)}) collective-permute-start(bf16[128,2048]{1,0:T(8,128)(2,1)} %slice.813), channel_id=1, source_target_pairs={{0,16},{4,20},{8,24},{12,28},{16,0},{20,4},{24,8},{28,12},{1,17},{... | collective-permute-start | bytes 1572872 | tf_op jit(solution)/shard_map/ppermute | solution.py:19
  666.5 42.9 %collective-permute-start.68 = (bf16[128,2048]{1,0:T(8,128)(2,1)}, bf16[128,2048]{1,0:T(8,128)(2,1)}, u32[]{:S(2)}, u32[]{:S(2)}) collective-permute-start(bf16[128,2048]{1,0:T(8,128)(2,1)} %fusion.34), channel_id=1, source_target_pairs={{0,8},{4,12},{8,0},{12,4},{16,24},{20,28},{24,16},{28,20},{1,9},{5... | collective-permute-start | bytes 1572872 | tf_op jit(solution)/shard_map/ppermute | solution.py:19
  678.7 30.7 %collective-permute-start.66 = (bf16[128,2048]{1,0:T(8,128)(2,1)}, bf16[128,2048]{1,0:T(8,128)(2,1)}, u32[]{:S(2)}, u32[]{:S(2)}) collective-permute-start(bf16[128,2048]{1,0:T(8,128)(2,1)} %fusion.37), channel_id=1, source_target_pairs={{0,16},{4,20},{8,24},{12,28},{16,0},{20,4},{24,8},{28,12},{1,17},{... | collective-permute-start | bytes 1572872 | tf_op jit(solution)/shard_map/ppermute | solution.py:19
  700.6 73.4 %collective-permute-start.95 = (bf16[768,256]{1,0:T(8,128)(2,1)S(1)}, bf16[768,256]{1,0:T(8,128)(2,1)S(1)}, u32[]{:S(2)}, u32[]{:S(2)}) collective-permute-start(bf16[768,256]{1,0:T(8,128)(2,1)S(1)} %bitcast.324), channel_id=1, source_target_pairs={{0,0},{1,8},{2,16},{3,24},{4,4},{5,12},{6,20},{7,28},{8,1},{9,9},{... | collective-permute-start | bytes 1179656 | tf_op jit(solution)/shard_map/ppermute | solution.py:115
  702.5 87.4 %collective-permute-start.96 = (bf16[768,256]{1,0:T(8,128)(2,1)S(1)}, bf16[768,256]{1,0:T(8,128)(2,1)S(1)}, u32[]{:S(2)}, u32[]{:S(2)}) collective-permute-start(bf16[768,256]{1,0:T(8,128)(2,1)S(1)} %bitcast.323), channel_id=1, source_target_pairs={{0,4},{1,12},{2,20},{3,28},{4,0},{5,8},{6,16},{7,24},{8,5},{9,13},... | collective-permute-start | bytes 1179656 | tf_op jit(solution)/shard_map/ppermute | solution.py:115
  711.6 25.4 %collective-permute-start.87 = (f32[2,2048]{1,0:T(2,128)S(1)}, f32[2,2048]{1,0:T(2,128)S(1)}, u32[]{:S(2)}, u32[]{:S(2)}) collective-permute-start(f32[2,2048]{1,0:T(2,128)S(1)} %add.431), channel_id=1, source_target_pairs={{0,1},{1,0},{2,3},{3,2},{4,5},{5,4},{6,7},{7,6},{8,9},{9,8},{10,11... | collective-permute-start | bytes 49160 | tf_op jit(solution)/shard_map/ppermute | solution.py:19
  737.1 36.3 %collective-permute-start.88 = (f32[2,2048]{1,0:T(2,128)S(1)}, f32[2,2048]{1,0:T(2,128)S(1)}, u32[]{:S(2)}, u32[]{:S(2)}) collective-permute-start(f32[2,2048]{1,0:T(2,128)S(1)} %add.432), channel_id=1, source_target_pairs={{0,2},{1,3},{2,0},{3,1},{4,6},{5,7},{6,4},{7,5},{8,10},{9,11},{10,... | collective-permute-start | bytes 49160 | tf_op jit(solution)/shard_map/ppermute | solution.py:19
  (122 other events, 1824.5 us)
Sparse Core Ops, SparseCore 0:
  26.4 63.6 all-gather.14
  91.7 32.8 all-gather.8
  126.8 115.9 all-gather.16
  244.2 63.3 all-gather.10
  396.3 62.5 reduce-scatter.10
  461.6 34.8 reduce-scatter.6
  536.4 28.6 all-gather.12
  567.4 60.1 reduce-scatter.4
  629.9 127.0 reduce-scatter.8

commit v2 on v1

v2 whole, which is shorter than its diff:
```python
import jax
import jax.numpy as jnp
from jax import lax
from jax.experimental import pallas as pl
from jax.experimental.pallas import tpu as pltpu
from jax.sharding import PartitionSpec as P

EPSILON = 1e-06
F32 = jnp.float32
BF16 = jnp.bfloat16
GELU_C = 0.7978845608028654
GELU_A = 0.044715
CHUNK = 32
VMEM_LIMIT = 48 << 20


def tie(*values):
    return lax.optimization_barrier(values)


def xor_send(value, axis, offset):
    count = lax.axis_size(axis)
    return lax.ppermute(value, axis, [(i, i ^ offset) for i in range(count)])


def shift_send(value, axis, steps):
    count = lax.axis_size(axis)
    first, last = max(0, -steps), min(count, count - steps)
    return lax.ppermute(value, axis, [(i, i + steps) for i in range(first, last)])


def gather_tokens(piece, *beside):
    chips = lax.axis_size("dp") // 2
    if chips == 4:
        half = piece.shape[0] // 2
        via_x = xor_send(piece, "dp", 2)
        via_y = xor_send(piece, "dp", 4)
        via_x, via_y, *beside = tie(via_x, via_y, *beside)
        top = xor_send(via_y[:half], "dp", 2)
        bottom = xor_send(via_x[half:], "dp", 4)
        return jnp.concatenate([piece, via_x, via_y, top, bottom], axis=0), *beside
    slots = [piece] + [xor_send(piece, "dp", 2 * o) for o in range(1, chips)]
    return jnp.concatenate(slots, axis=0), *beside


def scatter_tokens(partial, *beside):
    chips = lax.axis_size("dp") // 2
    wide = [partial[o].astype(F32) for o in range(chips)]
    if chips == 4:
        half = partial.shape[1] // 2
        via_x = xor_send(partial[3, :half], "dp", 2)
        via_y = xor_send(partial[3, half:], "dp", 4)
        x_top = xor_send(partial[1, :half], "dp", 2)
        y_bottom = xor_send(partial[2, half:], "dp", 4)
        via_x, via_y, *beside = tie(via_x, via_y, *beside)
        x_bottom = xor_send((wide[1][half:] + via_y.astype(F32)).astype(BF16), "dp", 2)
        y_top = xor_send((wide[2][:half] + via_x.astype(F32)).astype(BF16), "dp", 4)
        total = jnp.concatenate(
            [
                wide[0][:half] + x_top.astype(F32) + y_top.astype(F32),
                wide[0][half:] + x_bottom.astype(F32) + y_bottom.astype(F32),
            ],
            axis=0,
        )
        return total, *beside
    total = wide[0]
    for o in range(1, chips):
        total = total + xor_send(partial[o], "dp", 2 * o).astype(F32)
    return total, *beside


def join_cores(own_half, other_half):
    moved = xor_send(other_half.astype(BF16), "dp", 1)
    return (own_half + moved.astype(F32)).astype(BF16)


def gather_small(value):
    count = lax.axis_size("dp")
    evens = [value] + [xor_send(value, "dp", o) for o in range(2, count, 2)]
    evens = jnp.stack(evens, axis=0)
    both = jnp.stack([evens, xor_send(evens, "dp", 1)], axis=1)
    return both.reshape((count,) + value.shape)


def natural_order(slots):
    count, mine = slots.shape[0], lax.axis_index("dp")
    step = 1
    while step < count:
        pairs = slots.reshape((-1, 2, step) + slots.shape[1:])
        swapped = jnp.concatenate([pairs[:, 1:], pairs[:, :1]], axis=1)
        slots = jnp.where((mine // step) % 2 == 1, swapped, pairs).reshape(slots.shape)
        step *= 2
    return slots


def widen_blocks_kernel(mine_ref, slot_ref, out_ref):
    out_ref[...] = slot_ref[0].astype(F32)


def widen_blocks(slots):
    count, kinds, heads, rows, cols = slots.shape
    mine = lax.axis_index("dp").astype(jnp.int32).reshape(1)
    return pl.pallas_call(
        widen_blocks_kernel,
        out_shape=jax.ShapeDtypeStruct((kinds, count * heads, rows, cols), F32),
        grid_spec=pltpu.PrefetchScalarGridSpec(
            num_scalar_prefetch=1,
            grid=(count,),
            in_specs=[
                pl.BlockSpec((1, kinds, heads, rows, cols), lambda d, m: (d ^ m[0], 0, 0, 0, 0))
            ],
            out_specs=pl.BlockSpec((kinds, heads, rows, cols), lambda d, m: (0, d, 0, 0)),
        ),
        compiler_params=params(),
        name="widen_blocks",
    )(mine, slots)


def sum_over(value, axis):
    offset = 1
    total = value
    while offset < lax.axis_size(axis):
        moved = xor_send(total, axis, offset)
        total = (total.astype(F32) + moved.astype(F32)).astype(value.dtype)
        offset *= 2
    return total


def carry_in(decay, state, steps):
    count = lax.axis_size("seq")
    both = jnp.stack([decay, state], axis=0)
    moved = [shift_send(both, "seq", steps * k) for k in range(1, count)]
    carried = moved[-1][1]
    for item in reversed(moved[:-1]):
        carried = item[1] + item[0] * carried
    return carried


def quarter_shift():
    dp_count, seq_count = lax.axis_size("dp"), lax.axis_size("seq")
    mine = lax.axis_index("dp")
    ratio = dp_count // seq_count
    return shift_of(mine, ratio, seq_count)


def shift_of(d, ratio, seq_count):
    group = d // ratio
    flip = (d % 2) * (seq_count - 1)
    return group ^ flip


def place_rows(block):
    dp_count, seq_count = lax.axis_size("dp"), lax.axis_size("seq")
    ratio = dp_count // seq_count
    rows, cols = block.shape
    width = cols // ratio
    mine, seat = lax.axis_index("dp"), lax.axis_index("seq")
    parts = block.reshape(rows, ratio, width)
    out = jnp.zeros((ratio, rows, width), block.dtype)
    for turn in range(ratio):
        perm = []
        for d in range(dp_count):
            for s in range(seq_count):
                quarter = s ^ shift_of(d, ratio, seq_count)
                to = ratio * quarter + (d + turn) % ratio
                perm.append((d * seq_count + s, to * seq_count + d // ratio))
        chosen = lax.dynamic_index_in_dim(parts, (mine + turn) % ratio, 1, keepdims=False)
        got = lax.ppermute(chosen, ("dp", "seq"), perm)
        out = lax.dynamic_update_index_in_dim(out, got, (mine - turn) % ratio, 0)
    return out.reshape(ratio * rows, width)


def scaled_norm(values, gain_vec):
    return (
        values * lax.rsqrt(jnp.mean(values * values, axis=-1, keepdims=True) + EPSILON) * gain_vec
    )


def gelu_pair(v):
    square = v * v
    t = jnp.tanh(GELU_C * (v + GELU_A * v * square))
    half = 0.5 * (1.0 + t)
    slope = half + 0.5 * v * (1.0 - t * t) * (GELU_C * (1.0 + 3.0 * GELU_A * square))
    return v * half, slope


def logistic(v):
    return 1.0 / (1.0 + jnp.exp(-v))


def one_minus_exp(x, exp_x):
    poly = jnp.full_like(x, 1.0 / 362880.0)
    for coef in (1 / 40320.0, 1 / 5040.0, 1 / 720.0, 1 / 120.0, 1 / 24.0, 1 / 6.0, 0.5, 1.0):
        poly = poly * x + coef
    return jnp.where(x > -0.35, -x * poly, 1.0 - exp_x)


def half_mask(chunk, slots, width):
    return lax.broadcasted_iota(jnp.int32, (chunk, slots, width), 1) < slots // 2


def join_slots(own_ref, other_ref):
    return jnp.concatenate([own_ref[...], other_ref[...]], axis=0)


def fwd_gates_kernel(
    own_ref, other_ref, prior_ref, taps_ref, vec_ref, w_ref,
    bt_ref, conv_ref, r_ref, i_ref, rate_ref, m_ref, loc_ref, run_ref,
    halo, state, decay,
):
    chunk, slots, width = bt_ref.shape

    @pl.when(pl.program_id(0) == 0)
    def _():
        halo[...] = prior_ref[...]
        state[...] = jnp.zeros_like(state)
        decay[...] = jnp.ones_like(decay)

    bt = jnp.swapaxes(join_slots(own_ref, other_ref), 0, 1)
    bt_ref[...] = bt
    lag = halo.shape[0]
    padded = jnp.concatenate([halo[...], bt], axis=0)
    halo[...] = padded[chunk : chunk + lag]
    conv = jnp.zeros_like(bt) + vec_ref[0]
    for k in range(lag + 1):
        conv = conv + taps_ref[k] * padded[lag - k : lag - k + chunk]
    conv_ref[...] = conv
    rows = conv.reshape(chunk * slots, width).astype(BF16)
    mask = half_mask(chunk, slots, width)

    def gate(which):
        own = jnp.dot(rows, w_ref[2 * which], preferred_element_type=F32)
        other = jnp.dot(rows, w_ref[2 * which + 1], preferred_element_type=F32)
        shape = (chunk, slots, width)
        pre = jnp.where(mask, own.reshape(shape), other.reshape(shape))
        return logistic(pre + vec_ref[1 + which])

    r, g = gate(0), gate(1)
    log_rate = r * vec_ref[3]
    rate = jnp.exp(log_rate)
    m = jnp.sqrt(one_minus_exp(2.0 * log_rate, rate * rate))
    r_ref[...] = r
    i_ref[...] = g
    rate_ref[...] = rate
    m_ref[...] = m
    driven = m * g * conv
    st, dc = state[...], decay[...]
    for t in range(chunk):
        st = rate[t] * st + driven[t]
        dc = rate[t] * dc
        loc_ref[t] = st
        run_ref[t] = dc
    state[...] = st
    decay[...] = dc


def fwd_mix_kernel(
    loc_ref, run_ref, carry_ref, gate_own_ref, gate_other_ref,
    mixed_ref, prev_ref, across_ref, last,
):
    chunk, slots, width = loc_ref.shape

    @pl.when(pl.program_id(0) == 0)
    def _():
        last[...] = carry_ref[...]

    states = loc_ref[...] + run_ref[...] * carry_ref[...]
    prev_ref[...] = jnp.concatenate([last[...][None], states[: chunk - 1]], axis=0)
    last[...] = states[chunk - 1]
    across = jnp.swapaxes(states, 0, 1)
    across_ref[...] = across
    half = slots // 2
    own, _ = gelu_pair(gate_own_ref[...])
    other, _ = gelu_pair(gate_other_ref[...])
    mixed_ref[:, :, :width] = (across[:half] * own).astype(BF16)
    mixed_ref[:, :, width:] = (across[half:] * other).astype(BF16)


def back_mix_kernel(
    gm_own_ref, gm_other_ref, gate_own_ref, gate_other_ref, across_ref, rate_ref,
    ggate_ref, gl_ref, tail_ref, end_ref, held, decay,
):
    chunk, slots, width = rate_ref.shape

    @pl.when(pl.program_id(0) == 0)
    def _():
        held[...] = jnp.zeros_like(held)
        decay[...] = jnp.ones_like(decay)

    half = slots // 2
    gm = join_slots(gm_own_ref, gm_other_ref)
    act, slope = gelu_pair(join_slots(gate_own_ref, gate_other_ref))
    ggate = (gm * across_ref[...] * slope).astype(BF16)
    ggate_ref[:, :, :width] = ggate[:half]
    ggate_ref[:, :, width:] = ggate[half:]
    gs = jnp.swapaxes(gm * act, 0, 1)
    rate = rate_ref[...]
    h, dc = held[...], decay[...]
    for t in reversed(range(chunk)):
        grad = gs[t] + h
        gl_ref[t] = grad
        tail_ref[t] = dc
        h = rate[t] * grad
        dc = rate[t] * dc
    held[...] = h
    decay[...] = dc
    end_ref[0] = dc
    end_ref[1] = h


def back_gates_kernel(
    gl_ref, tail_ref, rate_ref, m_ref, r_ref, i_ref, conv_ref, prev_ref, bt_ref,
    hin_ref, prior_ref, taps_ref, vec_ref, w_ref,
    gbranch_ref, last_ref, head_ref, dw_ref, total_ref,
    later, sums_ref,
):
    chunk, slots, width = rate_ref.shape
    lag = later.shape[0]
    step = pl.program_id(0)

    @pl.when(step == 0)
    def _():
        later[...] = jnp.zeros_like(later)
        dw_ref[...] = jnp.zeros_like(dw_ref)
        sums_ref[...] = jnp.zeros_like(sums_ref)

    s = gl_ref[...] + tail_ref[...] * hin_ref[...]
    rate, m, r, g, conv = rate_ref[...], m_ref[...], r_ref[...], i_ref[...], conv_ref[...]
    sc = s * conv
    dpi = (sc * m * (g * (1.0 - g))).astype(BF16).astype(F32)
    dlog = s * prev_ref[...] * rate - sc * g * (rate * rate) / m
    dpr = (dlog * vec_ref[3] * (r * (1.0 - r))).astype(BF16).astype(F32)
    sums_ref[2] += jnp.sum(dlog * r, axis=0)
    sums_ref[0] += jnp.sum(dpr, axis=0)
    sums_ref[1] += jnp.sum(dpi, axis=0)
    mask = half_mask(chunk, slots, width)
    flat = (chunk * slots, width)
    rows_own = jnp.where(mask, conv, 0.0).reshape(flat).astype(BF16)
    rows_other = jnp.where(mask, 0.0, conv).reshape(flat).astype(BF16)
    dpr = dpr.reshape(flat).astype(BF16)
    dpi = dpi.reshape(flat).astype(BF16)
    over_rows = (((0,), (0,)), ((), ()))
    over_cols = (((1,), (1,)), ((), ()))
    dw_ref[0] += lax.dot_general(rows_own, dpr, over_rows, preferred_element_type=F32)
    dw_ref[1] += lax.dot_general(rows_other, dpr, over_rows, preferred_element_type=F32)
    dw_ref[2] += lax.dot_general(rows_own, dpi, over_rows, preferred_element_type=F32)
    dw_ref[3] += lax.dot_general(rows_other, dpi, over_rows, preferred_element_type=F32)

    def through(which):
        part = lax.dot_general(dpr, w_ref[which], over_cols, preferred_element_type=F32)
        part += lax.dot_general(dpi, w_ref[2 + which], over_cols, preferred_element_type=F32)
        return part.reshape(chunk, slots, width)

    gconv = jnp.where(mask, through(0), through(1)) + s * m * g
    padded = jnp.concatenate([gconv, later[...]], axis=0)
    later[...] = gconv[:lag]
    head_ref[...] = gconv[:lag]
    sums_ref[3] += jnp.sum(gconv, axis=0)
    bt = bt_ref[...]
    gb = jnp.zeros_like(gconv)
    for k in range(lag + 1):
        shifted = padded[k : k + chunk]
        gb = gb + taps_ref[k] * shifted
        sums_ref[4 + k] += jnp.sum(bt * shifted, axis=0)

    @pl.when(step == 0)
    def _():
        last_ref[...] = gb[chunk - lag :]

    across = jnp.swapaxes(gb, 0, 1).astype(BF16)
    gbranch_ref[:, :, :width] = across[: slots // 2]
    gbranch_ref[:, :, width:] = across[slots // 2 :]

    @pl.when(step == pl.num_programs(0) - 1)
    def _():
        for k in range(1, lag + 1):
            for j in range(1, k + 1):
                sums_ref[4 + k] += prior_ref[lag - j] * gconv[k - j]
        half = slots // 2
        for kind in range(total_ref.shape[1]):
            total_ref[0, kind] = jnp.sum(sums_ref[kind, :half], axis=0)
            total_ref[1, kind] = jnp.sum(sums_ref[kind, half:], axis=0)


def specs_for(slots, length, width, backwards):
    count = length // CHUNK

    def at(c):
        return count - 1 - c if backwards else c

    time_major = pl.BlockSpec((CHUNK, slots, width), lambda c: (at(c), 0, 0))

    def columns(j, times=1, halves=2):
        return pl.BlockSpec((slots // halves, CHUNK, times * width), lambda c: (0, at(c), j))

    return count, time_major, columns


def whole(*shape):
    return pl.BlockSpec(shape, lambda c: (0,) * len(shape))


def params():
    return pltpu.CompilerParams(
        dimension_semantics=("arbitrary",), vmem_limit_bytes=VMEM_LIMIT
    )


def cost(flops, size, trans):
    return pl.CostEstimate(flops=flops, bytes_accessed=size, transcendentals=trans)


def fwd_gates(both, prior, taps, vecs, w):
    length = both.shape[1]
    lag, slots, width = prior.shape
    count, tm, cols = specs_for(slots, length, width, False)
    full = jax.ShapeDtypeStruct((length, slots, width), F32)
    n = slots * length * width
    return pl.pallas_call(
        fwd_gates_kernel,
        out_shape=(full,) * 8,
        grid=(count,),
        in_specs=[
            cols(0), cols(2), whole(*prior.shape), whole(*taps.shape), whole(*vecs.shape),
            whole(*w.shape),
        ],
        out_specs=(tm,) * 8,
        scratch_shapes=[
            pltpu.VMEM(prior.shape, F32),
            pltpu.VMEM((slots, width), F32),
            pltpu.VMEM((slots, width), F32),
        ],
        compiler_params=params(),
        cost_estimate=cost(n, 58 * n, n),
        name="gates_forward",
    )(both, both, prior, taps, vecs, w)


def fwd_mix(loc, run, carry, both):
    length, slots, width = loc.shape
    count, tm, cols = specs_for(slots, length, width, False)
    n = slots * length * width
    return pl.pallas_call(
        fwd_mix_kernel,
        out_shape=(
            jax.ShapeDtypeStruct((slots // 2, length, 2 * width), BF16),
            jax.ShapeDtypeStruct((length, slots, width), F32),
            jax.ShapeDtypeStruct((slots, length, width), F32),
        ),
        grid=(count,),
        in_specs=[tm, tm, whole(slots, width), cols(1), cols(3)],
        out_specs=(cols(0, 2), tm, cols(0, 1, 1)),
        scratch_shapes=[pltpu.VMEM((slots, width), F32)],
        compiler_params=params(),
        cost_estimate=cost(n, 36 * n, n),
        name="mix_forward",
    )(loc, run, carry, both, both)


def back_mix(gm, both, across, rate):
    length, slots, width = rate.shape
    count, tm, cols = specs_for(slots, length, width, True)
    n = slots * length * width
    return pl.pallas_call(
        back_mix_kernel,
        out_shape=(
            jax.ShapeDtypeStruct((slots // 2, length, 2 * width), BF16),
            jax.ShapeDtypeStruct((length, slots, width), F32),
            jax.ShapeDtypeStruct((length, slots, width), F32),
            jax.ShapeDtypeStruct((2, slots, width), F32),
        ),
        grid=(count,),
        in_specs=[cols(0), cols(1), cols(1), cols(3), cols(0, 1, 1), tm],
        out_specs=(cols(0, 2), tm, tm, whole(2, slots, width)),
        scratch_shapes=[pltpu.VMEM((slots, width), F32), pltpu.VMEM((slots, width), F32)],
        compiler_params=params(),
        cost_estimate=cost(n, 44 * n, n),
        name="mix_backward",
    )(gm, gm, both, both, across, rate)


def back_gates(kept, hin, prior, taps, vecs, w):
    length, slots, width = kept[0].shape
    lag = prior.shape[0]
    count, tm, cols = specs_for(slots, length, width, True)
    n = slots * length * width
    return pl.pallas_call(
        back_gates_kernel,
        out_shape=(
            jax.ShapeDtypeStruct((slots // 2, length, 2 * width), BF16),
            jax.ShapeDtypeStruct((lag, slots, width), F32),
            jax.ShapeDtypeStruct((lag, slots, width), F32),
            jax.ShapeDtypeStruct(w.shape, F32),
            jax.ShapeDtypeStruct((2, 5 + lag, width), F32),
        ),
        grid=(count,),
        in_specs=[tm] * 9
        + [
            whole(slots, width), whole(*prior.shape), whole(*taps.shape), whole(*vecs.shape),
            whole(*w.shape),
        ],
        out_specs=(
            cols(0, 2), whole(lag, slots, width), whole(lag, slots, width),
            whole(*w.shape), whole(2, 5 + lag, width),
        ),
        scratch_shapes=[
            pltpu.VMEM((lag, slots, width), F32),
            pltpu.VMEM((5 + lag, slots, width), F32),
        ],
        compiler_params=params(),
        cost_estimate=cost(n, 76 * n, n),
        name="gates_backward",
    )(*kept, hin, prior, taps, vecs, w)


def tile_of(hidden_width):
    return 256 if hidden_width % 256 == 0 else 128


def row_blocks(rows):
    step = 256 if rows % 256 == 0 else rows
    return [slice(at, at + step) for at in range(0, rows, step)]


def mlp_forward_kernel(x_ref, w_ref, hidden_ref, kept_ref):
    tile = hidden_ref.shape[1]
    weight = jnp.swapaxes(w_ref[...], 0, 1).reshape(x_ref.shape[1], 2 * tile)
    for rows in row_blocks(x_ref.shape[0]):
        ffn = jnp.dot(x_ref[rows, :], weight, preferred_element_type=F32)
        act, slope = gelu_pair(ffn[:, :tile])
        up = ffn[:, tile:]
        hidden_ref[rows, :] = (act * up).astype(BF16)
        kept_ref[rows, :tile] = (slope * up).astype(BF16)
        kept_ref[rows, tile:] = act.astype(BF16)


def mlp_forward(x, weight):
    rows, model = x.shape
    hidden_width = weight.shape[3] // 2
    tile = tile_of(hidden_width)
    return pl.pallas_call(
        mlp_forward_kernel,
        out_shape=(
            jax.ShapeDtypeStruct((rows, hidden_width), BF16),
            jax.ShapeDtypeStruct((rows, 2 * hidden_width), BF16),
        ),
        grid=(hidden_width // tile,),
        in_specs=[
            pl.BlockSpec((rows, model), lambda j: (0, 0), pipeline_mode=pl.Buffered(1)),
            pl.BlockSpec(weight.shape[:3] + (2 * tile,), lambda j: (0, 0, 0, j)),
        ],
        out_specs=(
            pl.BlockSpec((rows, tile), lambda j: (0, j)),
            pl.BlockSpec((rows, 2 * tile), lambda j: (0, j)),
        ),
        compiler_params=params(),
        cost_estimate=cost(7 * rows * hidden_width * model, rows * model, 0),
        name="mlp_forward",
    )(x, weight)


OVER_COLS = (((1,), (1,)), ((), ()))


def hidden_backward_kernel(g_ref, down0_ref, down1_ref, kept0_ref, kept1_ref, ffn0_ref, ffn1_ref):
    step = pl.program_id(0)
    tile = down0_ref.shape[0]

    def half(down_ref, kept_ref, ffn_ref):
        for rows in row_blocks(g_ref.shape[0]):
            grad = lax.dot_general(
                g_ref[rows, :], down_ref[...], OVER_COLS, preferred_element_type=F32
            )
            ffn_ref[rows, :tile] = (grad * kept_ref[rows, :tile].astype(F32)).astype(BF16)
            ffn_ref[rows, tile:] = (grad * kept_ref[rows, tile:].astype(F32)).astype(BF16)

    @pl.when(step < pl.num_programs(0) // 2)
    def _():
        half(down1_ref, kept1_ref, ffn1_ref)

    @pl.when(step >= pl.num_programs(0) // 2)
    def _():
        half(down0_ref, kept0_ref, ffn0_ref)


def hidden_backward(grad, down, kept):
    rows, model = grad.shape
    hidden_width = down[0].shape[0]
    tile = tile_of(hidden_width)
    half = hidden_width // tile

    def own(j):
        return jnp.maximum(j - half, 0)

    def other(j):
        return jnp.minimum(j, half - 1)

    full = jax.ShapeDtypeStruct((rows, 2 * hidden_width), BF16)
    return pl.pallas_call(
        hidden_backward_kernel,
        out_shape=(full, full),
        grid=(2 * half,),
        in_specs=[
            pl.BlockSpec((rows, model), lambda j: (0, 0), pipeline_mode=pl.Buffered(1)),
            pl.BlockSpec((tile, model), lambda j: (own(j), 0)),
            pl.BlockSpec((tile, model), lambda j: (other(j), 0)),
            pl.BlockSpec((rows, 2 * tile), lambda j: (0, own(j))),
            pl.BlockSpec((rows, 2 * tile), lambda j: (0, other(j))),
        ],
        out_specs=(
            pl.BlockSpec((rows, 2 * tile), lambda j: (0, own(j))),
            pl.BlockSpec((rows, 2 * tile), lambda j: (0, other(j))),
        ),
        compiler_params=params(),
        cost_estimate=cost(7 * rows * hidden_width * model, rows * model, 0),
        name="hidden_backward",
    )(grad, *down, *kept)


def normed_backward_kernel(ffn0_ref, ffn1_ref, w0_ref, w1_ref, out_ref):
    width = ffn0_ref.shape[1]
    for rows in row_blocks(ffn0_ref.shape[0]):
        total = None
        for ffn_ref, w_ref in ((ffn0_ref, w0_ref), (ffn1_ref, w1_ref)):
            part = lax.dot_general(
                ffn_ref[rows, :],
                w_ref[...].reshape(out_ref.shape[1], width),
                OVER_COLS,
                preferred_element_type=F32,
            )
            total = part if total is None else total + part
        out_ref[rows, :] = total.astype(BF16)


def normed_backward(ffn, weight):
    rows, width = ffn[0].shape
    seq_count, dp_count, shard, _ = weight[0].shape
    cols = seq_count * shard
    kept = pl.BlockSpec((rows, width), lambda j: (0, 0), pipeline_mode=pl.Buffered(1))
    block = pl.BlockSpec((seq_count, 1, shard, width), lambda j: (0, j, 0, 0))
    return pl.pallas_call(
        normed_backward_kernel,
        out_shape=jax.ShapeDtypeStruct((rows, cols * dp_count), BF16),
        grid=(dp_count,),
        in_specs=[kept, kept, block, block],
        out_specs=pl.BlockSpec((rows, cols), lambda j: (0, j)),
        compiler_params=params(),
        cost_estimate=cost(7 * rows * width * cols * dp_count, rows * width, 0),
        name="normed_backward",
    )(*ffn, *weight)


def unpack_down_kernel(packed_ref, out_ref):
    out_ref[...] = jnp.concatenate(
        [packed_ref[0, block] for block in range(packed_ref.shape[1])], axis=1
    )


def unpack_down(packed, first_column, rows):
    seq_count, dp_count, shard, _ = packed.shape
    lay = rows // (seq_count * shard)
    part = (packed.shape[3] - first_column) // lay
    begin = first_column // part
    return pl.pallas_call(
        unpack_down_kernel,
        out_shape=jax.ShapeDtypeStruct((rows, dp_count * part), packed.dtype),
        grid=(seq_count, lay),
        in_specs=[
            pl.BlockSpec((1, dp_count, shard, part), lambda s, k: (s, 0, 0, begin + k))
        ],
        out_specs=pl.BlockSpec((shard, dp_count * part), lambda s, k: (s * lay + k, 0)),
        compiler_params=pltpu.CompilerParams(
            dimension_semantics=("arbitrary", "arbitrary"), vmem_limit_bytes=VMEM_LIMIT
        ),
        cost_estimate=cost(0, 2 * rows * dp_count * part * 2, 0),
        name="unpack_down",
    )(packed)


def rows_of(value):
    return value.reshape(-1, value.shape[-1])


def mm(left, right):
    return jnp.dot(left, right, preferred_element_type=F32)


def mm_back(grad_rows, weight):
    return lax.dot_general(grad_rows, weight, (((1,), (1,)), ((), ())), preferred_element_type=F32)


def weight_kernel(left_ref, right_ref, *refs):
    out_ref = refs[-1]
    product = lax.dot_general(
        left_ref[...], right_ref[...], (((0,), (0,)), ((), ())), preferred_element_type=F32
    )
    if len(refs) == 2:
        product = product + refs[0][...].astype(F32)
    out_ref[...] = product.astype(BF16)


def mm_weight(left, right, *added):
    depth, rows = left.shape
    cols = right.shape[1]
    tile = 256 if rows % 256 == 0 else 128
    block = pl.BlockSpec((tile, cols), lambda i: (i, 0))
    return pl.pallas_call(
        weight_kernel,
        out_shape=jax.ShapeDtypeStruct((rows, cols), BF16),
        grid=(rows // tile,),
        in_specs=[
            pl.BlockSpec((depth, tile), lambda i: (0, i)),
            pl.BlockSpec((depth, cols), lambda i: (0, 0), pipeline_mode=pl.Buffered(1)),
        ]
        + [block] * len(added),
        out_specs=block,
        compiler_params=params(),
        cost_estimate=cost(3 * rows * cols * depth, rows * cols, 0),
        name="weight_gradient",
    )(left, right, *added)


def weight_rows_kernel(shift_ref, left_ref, right_ref, added_ref, *refs):
    out_ref = refs[-1]
    product = lax.dot_general(
        left_ref[...], right_ref[...], (((0,), (0,)), ((), ())), preferred_element_type=F32
    )
    product = (product + added_ref[...].astype(F32)).astype(BF16)
    count, _, cols = out_ref.shape
    for quarter in range(count):
        out_ref[quarter ^ shift_ref[0]] = product[:, quarter * cols : (quarter + 1) * cols]


def weight_rows(left, right, added, total_rows, first_row, into=None):
    depth, rows = left.shape
    cols = right.shape[1]
    count = lax.axis_size("seq")
    tile = 128
    shift = quarter_shift().astype(jnp.int32).reshape(1)
    begin = first_row // tile
    more = [] if into is None else [into]
    return pl.pallas_call(
        weight_rows_kernel,
        out_shape=jax.ShapeDtypeStruct((count, total_rows, cols // count), BF16),
        grid_spec=pltpu.PrefetchScalarGridSpec(
            num_scalar_prefetch=1,
            grid=(rows // tile,),
            in_specs=[
                pl.BlockSpec((depth, tile), lambda i, s: (0, i)),
                pl.BlockSpec((depth, cols), lambda i, s: (0, 0), pipeline_mode=pl.Buffered(1)),
                pl.BlockSpec((tile, cols), lambda i, s: (i, 0)),
            ]
            + [pl.BlockSpec(memory_space=pl.ANY)] * len(more),
            out_specs=pl.BlockSpec(
                (count, tile, cols // count), lambda i, s: (0, begin + i, 0)
            ),
        ),
        input_output_aliases={4: 0} if more else {},
        compiler_params=params(),
        cost_estimate=cost(3 * rows * cols * depth, rows * cols, 0),
        name="weight_rows",
    )(shift, left, right, added, *more)


def local(
    block_input, norm_gain, in_proj, gate_proj, conv_kernel, conv_bias,
    recur_weight, recur_bias, input_weight, input_bias, decay_param,
    out_proj, mlp_gain, mlp_gate, mlp_up, mlp_down, out_grad,
):
    dp_count, seq_count = lax.axis_size("dp"), lax.axis_size("seq")
    mine = lax.axis_index("dp")
    model = block_input.shape[2]
    tokens = block_input.reshape(-1, model).astype(F32)
    length = tokens.shape[0]
    recur_width = in_proj.shape[1]
    own = recur_width // dp_count
    width = -(-own // 128) * 128
    hidden_width = mlp_gate.shape[1] // dp_count
    head = recur_weight.shape[1]
    own_heads = own // head
    lag = conv_kernel.shape[0] - 1

    chips = dp_count // 2

    shard = in_proj.shape[0]

    def split_cols(weight, padded):
        part = jnp.swapaxes(weight.reshape(shard, dp_count, -1), 0, 1)
        return jnp.pad(part, ((0, 0), (0, 0), (0, padded - part.shape[2])))

    def spread(joined):
        return lax.all_to_all(joined, "dp", split_axis=0, concat_axis=0, tiled=True)

    def natural_rows(full):
        return full.transpose(1, 0, 2, 3).reshape(-1, full.shape[3])

    def partner(value):
        return xor_send(value, "dp", 1)

    w_out = lax.all_gather(out_proj, "seq", axis=0, tiled=True)
    first = jnp.concatenate([split_cols(in_proj, width), split_cols(gate_proj, width)], axis=2)
    first = spread(first)
    first = lax.all_gather(first, "seq", axis=0)
    def per_slot(value):
        rows = []
        for index in (mine, mine ^ 1):
            part = lax.dynamic_slice_in_dim(value, index * own, own, axis=value.ndim - 1)
            rows.append(jnp.pad(part, [(0, 0)] * (value.ndim - 1) + [(0, width - own)]))
        return jnp.repeat(jnp.stack(rows, axis=-2), chips, axis=-2)

    taps = per_slot(conv_kernel)
    vecs = per_slot(jnp.stack([conv_bias, recur_bias, input_bias, decay_param]))
    vecs = jnp.concatenate([vecs[:3], -8.0 * jax.nn.softplus(-vecs[3:])], axis=0)

    def block_diagonal(weight, index):
        part = lax.dynamic_slice_in_dim(weight, index * own_heads, own_heads, axis=0)
        rows = [
            jnp.pad(part[h], ((0, 0), (h * head, width - (h + 1) * head)))
            for h in range(own_heads)
        ]
        return jnp.pad(jnp.concatenate(rows, axis=0), ((0, width - own), (0, 0)))

    w_gates = jnp.stack(
        [block_diagonal(w, i) for w in (recur_weight, input_weight) for i in (mine, mine ^ 1)]
    )

    normed = scaled_norm(tokens, norm_gain).astype(BF16)
    normed_all, w_out = gather_tokens(normed, w_out)
    w_out = jnp.pad(w_out, ((0, width - own), (0, 0)))
    w_out = jnp.concatenate([w_out, partner(w_out)], axis=0)
    tile = tile_of(hidden_width)

    def by_tile(weight):
        return weight.reshape(shard, dp_count, hidden_width // tile, tile)

    second = jnp.concatenate([by_tile(mlp_gate), by_tile(mlp_up)], axis=3)
    second = jnp.swapaxes(second.reshape(shard, dp_count, 2 * hidden_width), 0, 1)
    lay = mlp_down.shape[0] // shard
    part = model // dp_count
    down = mlp_down.reshape(lay, shard, dp_count, part).transpose(2, 1, 0, 3)
    down = down.reshape(dp_count, shard, lay * part)
    second, down, normed_all = tie(second, down, normed_all)
    grad_low, second, first = tie(out_grad.reshape(length, model), spread(second), first)
    second = lax.all_gather(jnp.concatenate([second, down], axis=2), "seq", axis=0)

    w_first = natural_rows(first)
    w_first = jnp.concatenate([w_first, partner(w_first)], axis=1)

    both = mm(normed_all, w_first)
    grad_all, both = gather_tokens(grad_low, both)
    both = both.reshape(chips, length, 4 * width)
    ends = both[:, length - lag :]
    ends = jnp.concatenate([ends[:, :, :width], ends[:, :, 2 * width : 3 * width]], axis=0)
    prior = shift_send(jnp.swapaxes(ends, 0, 1), "seq", 1)
    bt, conv, r, g, rate, m, loc, run = fwd_gates(both, prior, taps, vecs, w_gates)
    carry = carry_in(run[length - 1], loc[length - 1], 1)
    mixed, prev, across = fwd_mix(loc, run, carry, both)
    mixed = rows_of(mixed)
    partial, grad_all = tie(mm(mixed, w_out).astype(BF16), grad_all)
    (total,) = scatter_tokens(partial.reshape(chips, length, model))
    residual = tokens + total

    inv_two = lax.rsqrt(jnp.mean(residual * residual, axis=-1, keepdims=True) + EPSILON)
    normed_two = (residual * inv_two * mlp_gain).astype(BF16)
    (normed_two_all,) = gather_tokens(normed_two)
    normed_two_all, second = tie(normed_two_all, second)
    w_second = second[:, :, :, : 2 * hidden_width]
    w_second = (w_second, partner(w_second))
    w_down = unpack_down(second, 2 * hidden_width, hidden_width)
    w_down = (w_down, partner(w_down))
    hidden, kept = zip(*[mlp_forward(normed_two_all, weight) for weight in w_second])
    hidden = list(hidden)
    grad_ffn = list(hidden_backward(grad_all, w_down, kept))
    moved = mm_weight(normed_two_all, grad_ffn[1])
    grad_ffn[0], moved = tie(grad_ffn[0], moved)
    moved = xor_send(moved, "dp", 1)
    partial = normed_backward(grad_ffn, w_second)
    partial, grad_ffn[0], normed_two_all = tie(partial, grad_ffn[0], normed_two_all)
    grad_normed_two, moved, grad_ffn[0] = scatter_tokens(
        partial.reshape(chips, length, model), moved, grad_ffn[0]
    )
    grad_second = mm_weight(normed_two_all, grad_ffn[0], moved)
    grad_normed_two, grad_second = tie(grad_normed_two, grad_second)
    grad_second_rows = lax.psum_scatter(grad_second, "seq", scatter_dimension=0, tiled=True)

    def norm_back(grad, values, inv, gain):
        unit = values * inv
        scaled = grad * gain
        mean = jnp.mean(scaled * unit, axis=-1, keepdims=True)
        return inv * (scaled - unit * mean), unit

    grad_resid, unit_two = norm_back(grad_normed_two, residual, inv_two, mlp_gain)
    mlp_gain_term = jnp.sum(grad_normed_two * unit_two, axis=0)
    grad_residual = grad_resid + grad_low.astype(F32)

    grad_rec, hidden[0], hidden[1] = tie(grad_residual.astype(BF16), *hidden)
    out_partial = mm(hidden[0], w_down[0]) + mm(hidden[1], w_down[1])
    grad_rec_all, out_partial, hidden[0], hidden[1] = gather_tokens(
        grad_rec, out_partial.astype(BF16), *hidden
    )
    moved = mm_weight(hidden[1], grad_all)
    grad_rec_all, moved = tie(grad_rec_all, moved)
    grad_rows = weight_rows(
        hidden[0], grad_all, xor_send(moved, "dp", 1), hidden_width + width, 0
    )
    gm = mm_back(grad_rec_all, w_out)
    gm = gm.reshape(chips, length, 2 * width)
    ggate, gl, tail, end = back_mix(gm, both, across, rate)
    hin = carry_in(end[0], end[1], -1)
    moved = mm_weight(mixed[:, width:], grad_rec_all)
    hin, moved, grad_rows = tie(hin, moved, grad_rows)
    moved = xor_send(moved, "dp", 1)
    grad_rows = weight_rows(
        mixed[:, :width], grad_rec_all, moved, hidden_width + width, hidden_width, grad_rows
    )
    gbranch, last, head_rows, dw, sums = back_gates(
        (gl, tail, rate, m, r, g, conv, prev, bt), hin, prior, taps, vecs, w_gates
    )
    later = shift_send(head_rows, "seq", -1)
    fixed = []
    for j in range(lag):
        row = last[j]
        for k in range(lag - j, lag + 1):
            row = row + taps[k] * later[j + k - lag]
        fixed.append(row)
    fixed = jnp.stack(fixed, axis=1).astype(BF16)
    fixed = jnp.concatenate([fixed[:chips], fixed[chips:]], axis=2)
    gbranch = lax.dynamic_update_slice(gbranch, fixed, (0, length - lag, 0))
    gbranch, ggate = rows_of(gbranch), rows_of(ggate)
    grad_first = jnp.concatenate(
        [gbranch[:, :width], ggate[:, :width], gbranch[:, width:], ggate[:, width:]], axis=1
    )
    moved = mm_weight(normed_all, grad_first[:, 2 * width :])
    grad_first, moved, grad_rows, grad_second_rows = tie(
        grad_first, moved, grad_rows, grad_second_rows
    )
    row_cols = lax.psum_scatter(grad_rows, "seq", scatter_dimension=0, tiled=False)
    moved = xor_send(moved, "dp", 1)
    partial = mm_back(grad_first, w_first).astype(BF16)
    partial, normed_all = tie(partial, normed_all)
    grad_normed, moved, grad_first, dw, sums = scatter_tokens(
        partial.reshape(chips, length, model), moved, grad_first, dw, sums
    )
    grad_first_w = mm_weight(normed_all, grad_first[:, : 2 * width], moved)
    grad_normed, grad_first_w, out_partial = tie(grad_normed, grad_first_w, out_partial)
    (total,) = scatter_tokens(out_partial.reshape(chips, length, model))
    block_output = (residual + total).astype(BF16).reshape(block_input.shape)
    grad_second_rows = grad_second_rows.reshape(-1, hidden_width // tile, 2, tile).astype(F32)
    grad_mgate_w = grad_second_rows[:, :, 0].reshape(-1, hidden_width)
    grad_mup_w = grad_second_rows[:, :, 1].reshape(-1, hidden_width)
    norm_gain_term = jnp.sum(partial.astype(F32) * normed_all.astype(F32), axis=0) / norm_gain
    grad_first_w = lax.psum_scatter(grad_first_w, "seq", scatter_dimension=0, tiled=True)
    grad_in_w = grad_first_w[:, :own].astype(F32)
    grad_gate_w = grad_first_w[:, width : width + own].astype(F32)
    inv_one = lax.rsqrt(jnp.mean(tokens * tokens, axis=-1, keepdims=True) + EPSILON)
    grad_tokens, _ = norm_back(grad_normed, tokens, inv_one, norm_gain)
    input_grad = (grad_tokens + grad_residual).reshape(block_input.shape)

    down_cols, out_cols = row_cols[:hidden_width], row_cols[hidden_width : hidden_width + own]
    grad_down_w = place_rows(down_cols).astype(F32)
    grad_out_w = place_rows(out_cols).astype(F32)

    sums = sum_over(sums[0] + xor_send(sums[1], "dp", 1), "seq")
    sums = natural_order(gather_small(sums))[:, :, :own]
    sums = jnp.swapaxes(sums, 0, 1).reshape(-1, recur_width)
    decay_term = sums[2] * (8.0 * jax.nn.sigmoid(-decay_param))

    def diagonal(full):
        return jnp.stack(
            [full[h * head : (h + 1) * head, h * head : (h + 1) * head] for h in range(own_heads)]
        )

    blocks = jnp.stack([diagonal(dw[0]), diagonal(dw[2])])
    blocks = join_cores(blocks, jnp.stack([diagonal(dw[1]), diagonal(dw[3])]))
    blocks = sum_over(blocks, "seq")
    blocks = widen_blocks(gather_small(blocks))
    gains = sum_over(sum_over(jnp.stack([norm_gain_term, mlp_gain_term]), "dp"), "seq")
    return (
        block_output,
        input_grad,
        gains[0],
        grad_in_w,
        grad_gate_w,
        sums[4:],
        sums[3],
        blocks[0],
        sums[0],
        blocks[1],
        sums[1],
        decay_term,
        grad_out_w,
        gains[1],
        grad_mgate_w,
        grad_mup_w,
        grad_down_w,
    )


def solution(mesh):
    rows = P(("dp", "seq"), None)
    acts = P("dp", "seq", None)
    grads = P("seq", "dp")
    return jax.shard_map(
        local,
        mesh=mesh,
        in_specs=(
            acts, P(), rows, rows, P(), P(), P(), P(), P(), P(), P(), rows, P(), rows, rows, rows,
            acts,
        ),
        out_specs=(
            acts, acts, P(), grads, grads, P(), P(), P(), P(), P(), P(), P(), grads, P(), grads,
            grads, grads,
        ),
        check_vma=False,
    )
```

time: 852 us -> 824 us (0.967)
  Pallas kernels: 44.4 us -> 185 us
  matrix products: 150 us -> 45.3 us
  waiting for transfers between devices: 346 us -> 274 us
  starting transfers between devices: 124 us -> 85.9 us
  local copies, waits for them, and re-layouts: 79 us -> 113 us
  blocking collectives: 25.2 us -> 40.5 us
    pallas_call x3 -> x17, Pallas kernels: 32.2 us -> 172 us  [the longest x6 54.2 us: mm_weight(): pl.pallas_call(weight_kernel, out_shape=jax.ShapeDtypeStruct((rows, cols)...]
    ppermute x85 -> x67, waiting for transfers between devices: 281 us -> 193 us  [xor_send(): return lax.ppermute(value, axis, [(i, i ^ offset) for i in range(count)])]
    dot_general x4 -> x0, matrix products: 44.5 us -> none  [mm_weight(): lax.dot_general(left, right, (((0,), (0,)), ((), ())), preferred_element_...]
    dot_general x4 -> x2, matrix products: 58.2 us -> 18.6 us  [mm_back(): lax.dot_general(grad_rows, weight, (((1,), (1,)), ((), ())), preferred_el...]
    ppermute x85 -> x67, starting transfers between devices: 87.5 us -> 56.9 us  [xor_send(): return lax.ppermute(value, axis, [(i, i ^ offset) for i in range(count)])]
    all_to_all x1 -> x2, blocking collectives: 15.3 us -> 40.5 us  [spread(): return lax.all_to_all(joined, 'dp', split_axis=0, concat_axis=0, tiled=True)]
    ppermute x4, waiting for transfers between devices: 36.5 us -> 61.4 us  [place_rows(): got = lax.ppermute(chosen, ('dp', 'seq'), perm)]
    dot_general x4, matrix products: 47.4 us -> 26.7 us  [mm(): return jnp.dot(left, right, preferred_element_type=F32)]
  transfers between devices with their start and end apart: 107 -> 85, of which waited for: 47 -> 32; matrix products, arithmetic and copies ran while one was open for 26% -> 21% of each run, Pallas kernels for 5% -> 20%
where the time goes in v2:
time: 824 us; the launch traced here: 814 us
  waiting for transfers between devices  274 us (33%)
  Pallas kernels  185 us (22%)
  local copies, waits for them, and re-layouts  113 us (14%)
  starting transfers between devices  85.9 us (10%)
  other arithmetic  53.8 us (7%)
  matrix products  45.3 us (5%)
  blocking collectives  40.5 us (5%)
  between operations  16.3 us (2%)
    ppermute x67, waiting for transfers between devices, xor_send(): return lax.ppermute(value, axis, [(i, i ^ offset) for i in range(count)])  193 us
    ppermute x4, waiting for transfers between devices, place_rows(): got = lax.ppermute(chosen, ('dp', 'seq'), perm)  61.4 us
    ppermute x67, starting transfers between devices, xor_send(): return lax.ppermute(value, axis, [(i, i ^ offset) for i in range(count)])  56.9 us
    pallas_call x6, Pallas kernels, mm_weight(): pl.pallas_call(weight_kernel, out_shape=jax.ShapeDtypeStruct((rows, cols)...  54.2 us
    all_to_all x2, blocking collectives, spread(): return lax.all_to_all(joined, 'dp', split_axis=0, concat_axis=0, tiled=True)  40.5 us
    unnamed x168, local copies, waits for them, and re-layouts  39.7 us
    dot_general x4, matrix products, mm(): return jnp.dot(left, right, preferred_element_type=F32)  26.7 us
    pallas_call x2, Pallas kernels, mlp_forward(): pl.pallas_call(mlp_forward_kernel, out_shape=(jax.ShapeDtypeStruct((rows,...  25.2 us
  transfers between devices with their start and end apart: 85, of which 32 were waited for; matrix products, arithmetic and copies ran while one was open for 21% of the time, Pallas kernels for 20%

profile of v2, /device:TPU:3, one launch (start us, length us, event | category | flops | bytes accessed | tf_op | source)
XLA Modules:
  0.0 814.0 jit_solution(3386007674892411896)
XLA Ops:
  11.6 15.5 %all_to_all.10 = bf16[8,64,768]{2,1,0:T(8,128)(2,1)} all-to-all(bf16[8,64,768]{2,1,0:T(8,128)(2,1)S(1)} %copy.134), channel_id=1, replica_groups=mesh['dp'=8,'seq'=4] {'dp'}, dimensions={0} | all-to-all | bytes 1572864 | tf_op jit(solution)/shard_map/all_to_all | solution.py:792
  37.0 16.5 %collective-permute-done = bf16[256,2048]{1,0:T(8,128)(2,1)S(1)} collective-permute-done((bf16[256,2048]{1,0:T(8,128)(2,1)}, bf16[256,2048]{1,0:T(8,128)(2,1)S(1)}, u32[]{:S(2)}, u32[]{:S(2)}) %collective-permute-start) | collective-permute-done | bytes 1048608 | tf_op jit(solution)/shard_map/ppermute | solution.py:23
  79.0 25.0 %all_to_all.11 = bf16[8,64,1536]{2,1,0:T(8,128)(2,1)S(1)} all-to-all(bf16[8,64,1536]{2,1,0:T(8,128)(2,1)S(1)} %copy.133), channel_id=1, replica_groups=mesh['dp'=8,'seq'=4] {'dp'}, dimensions={0} | all-to-all | bytes 3145728 | tf_op jit(solution)/shard_map/all_to_all | solution.py:792
  124.8 9.0 %fusion.1 = f32[1024,1536]{1,0:T(8,128)S(1)} fusion(bf16[1024,2048]{1,0:T(8,128)(2,1)S(1)} %copy-done.40, bf16[2048,768]{1,0:T(8,128)(2,1)} %collective-permute-done.6, bf16[2048,768]{1,0:T(8,128)(2,1)} %bitcast.8), kind=kOutput, calls=%fused_computation.4 | convolution fusion | flops 6455033856 | bytes 16777216 | tf_op jit(solution)/shard_map/dot_general | solution.py:685
  133.8 13.0 %collective-permute-done.4 = bf16[256,2048]{1,0:T(8,128)(2,1)S(1)} collective-permute-done((bf16[256,2048]{1,0:T(8,128)(2,1)S(1)}, bf16[256,2048]{1,0:T(8,128)(2,1)S(1)}, u32[]{:S(2)}, u32[]{:S(2)}) %collective-permute-start.4) | collective-permute-done | bytes 1048608 | tf_op jit(solution)/shard_map/ppermute | solution.py:23
  150.3 13.2 %gates_forward.1 = (f32[256,8,384]{2,1,0:T(8,128)S(1)}, f32[256,8,384]{2,1,0:T(8,128)}, f32[256,8,384]{2,1,0:T(8,128)}, f32[256,8,384]{2,1,0:T(8,128)}, f32[256,...) custom-call(f32[4,256,1536]{2,1,0:T(8,128)} %bitcast.314, ...), custom_call_target="tpu_custom_call" | custom-call | flops 786432 | bytes 45613056 | tf_op jit(solution)/shard_map/gates_forward/pallas_call | solution.py:419
  181.7 8.2 %mix_forward.1 = (bf16[4,256,768]{2,1,0:T(8,128)(2,1)S(1)}, f32[256,8,384]{2,1,0:T(8,128)S(1)}, f32[8,256,384]{2,1,0:T(8,128)}) custom-call(f32[256,8,384]{2,1,0:T(8,128)} %get-tuple-element.111.loc_ref, f32[256,8,384]{2,1,0:T(8,128)} %get-tuple-element.112.run_ref, f32[8,384]{1,0:T(8,128)S(1)} %fusion.59.carry_ref, f32[4,256,1536]{2,1,0:T(8,128)} %bitcast.316, ...), custom_call_target="tpu_custom_call" | custom-call | flops 786432 | bytes 28311552 | tf_op jit(solution)/shard_map/mix_forward/pallas_call | solution.py:443
  189.9 7.2 convolution_convert_fusion
  202.1 9.0 %collective-permute-done.15 = bf16[128,2048]{1,0:T(8,128)(2,1)S(1)} collective-permute-done((bf16[128,2048]{1,0:T(8,128)(2,1)S(1)}, bf16[128,2048]{1,0:T(8,128)(2,1)S(1)}, u32[]{:S(2)}, u32[]{:S(2)}) %collective-permute-start.15) | collective-permute-done | bytes 524320 | tf_op jit(solution)/shard_map/ppermute | solution.py:23
  213.2 9.1 %collective-permute-done.14 = bf16[128,2048]{1,0:T(8,128)(2,1)S(1)} collective-permute-done((bf16[128,2048]{1,0:T(8,128)(2,1)S(1)}, bf16[128,2048]{1,0:T(8,128)(2,1)S(1)}, u32[]{:S(2)}, u32[]{:S(2)}) %collective-permute-start.14) | collective-permute-done | bytes 524320 | tf_op jit(solution)/shard_map/ppermute | solution.py:23
  223.1 11.2 %collective-permute-done.17 = bf16[128,2048]{1,0:T(8,128)(2,1)S(1)} collective-permute-done((bf16[128,2048]{1,0:T(8,128)(2,1)S(1)}, bf16[128,2048]{1,0:T(8,128)(2,1)S(1)}, u32[]{:S(2)}, u32[]{:S(2)}) %collective-permute-start.17) | collective-permute-done | bytes 524320 | tf_op jit(solution)/shard_map/ppermute | solution.py:23
  237.6 21.4 %collective-permute-done.20 = bf16[256,2048]{1,0:T(8,128)(2,1)S(1)} collective-permute-done((bf16[256,2048]{1,0:T(8,128)(2,1)S(1)}, bf16[256,2048]{1,0:T(8,128)(2,1)S(1)}, u32[]{:S(2)}, u32[]{:S(2)}) %collective-permute-start.20) | collective-permute-done | bytes 1048608 | tf_op jit(solution)/shard_map/ppermute | solution.py:23
  288.4 12.8 %mlp_forward.2 = (bf16[1024,768]{1,0:T(8,128)(2,1)S(1)}, bf16[1024,1536]{1,0:T(8,128)(2,1)S(1)}) custom-call(bf16[1024,2048]{1,0:T(8,128)(2,1)} %constant_dynamic-update-slice_fusion.10.x_ref.left_ref, bf16[4,8,64,1536]{3,2,1,0:T(8,128)(2,1)} %copy-done.42), custom_call_target="tpu_custom_call" | custom-call | flops 11274289152 | bytes 2097152 | tf_op jit(solution)/shard_map/mlp_forward/pallas_call | solution.py:541
  303.0 12.3 %mlp_forward.3 = (bf16[1024,768]{1,0:T(8,128)(2,1)S(1)}, bf16[1024,1536]{1,0:T(8,128)(2,1)S(1)}) custom-call(bf16[1024,2048]{1,0:T(8,128)(2,1)} %constant_dynamic-update-slice_fusion.10.x_ref.left_ref, bf16[4,8,64,1536]{3,2,1,0:T(8,128)(2,1)} %collective-permute-done.25.w_ref.w1_ref), custom_call_target="tpu_custom_call" | custom-call | flops 11274289152 | bytes 2097152 | tf_op jit(solution)/shard_map/mlp_forward/pallas_call | solution.py:541
  317.0 14.4 %hidden_backward.1 = (bf16[1024,1536]{1,0:T(8,128)(2,1)S(1)}, bf16[1024,1536]{1,0:T(8,128)(2,1)}) custom-call(bf16[1024,2048]{1,0:T(8,128)(2,1)} %constant_dynamic-update-slice_fusion.5.g_ref.right_ref, bf16[768,2048]{1,0:T(8,128)(2,1)} %copy-done.5, bf16[768,2048]{1,0:T(8,128)(2,1)} %collective-permute-done.24.down1_ref, bf16[1024,1536]{1,0:T(8,128)(2,1)} %copy-done.21, ...), custom_call_target="tpu_custom_call" | custom-call | flops 11274289152 | bytes 2097152 | tf_op jit(solution)/shard_map/hidden_backward/pallas_call | solution.py:599
  333.4 11.1 %weight_gradient.6 = bf16[2048,1536]{1,0:T(8,128)(2,1)} custom-call(bf16[1024,2048]{1,0:T(8,128)(2,1)} %constant_dynamic-update-slice_fusion.10.x_ref.left_ref, bf16[1024,1536]{1,0:T(8,128)(2,1)S(1)} %copy-done.20), custom_call_target="tpu_custom_call" | custom-call | flops 9663676416 | bytes 3145728 | tf_op jit(solution)/shard_map/weight_gradient/pallas_call | solution.py:707
  344.5 18.0 %normed_backward.1 = bf16[1024,2048]{1,0:T(8,128)(2,1)} custom-call(bf16[1024,1536]{1,0:T(8,128)(2,1)S(1)} %get-tuple-element.138.ffn0_ref.right_ref, bf16[1024,1536]{1,0:T(8,128)(2,1)} %get-tuple-element.130.right_ref.ffn1_ref, bf16[4,8,64,1536]{3,2,1,0:T(8,128)(2,1)} %copy-done.42, bf16[4,8,64,1536]{3,2,1,0:T(8,128)(2,1)} %collective-permute-done.25.w_ref.w1_ref), custom_call_target="tpu_custom_call" | custom-call | flops 22548578304 | bytes 1572864 | tf_op jit(solution)/shard_map/normed_backward/pallas_call | solution.py:641
  369.8 8.5 %collective-permute-done.27 = bf16[128,2048]{1,0:T(8,128)(2,1)S(1)} collective-permute-done((bf16[128,2048]{1,0:T(8,128)(2,1)S(1)}, bf16[128,2048]{1,0:T(8,128)(2,1)S(1)}, u32[]{:S(2)}, u32[]{:S(2)}) %collective-permute-start.27) | collective-permute-done | bytes 524320 | tf_op jit(solution)/shard_map/ppermute | solution.py:23
  382.1 12.3 %weight_gradient.7 = bf16[2048,1536]{1,0:T(8,128)(2,1)} custom-call(bf16[1024,2048]{1,0:T(8,128)(2,1)} %constant_dynamic-update-slice_fusion.10.x_ref.left_ref, bf16[1024,1536]{1,0:T(8,128)(2,1)S(1)} %get-tuple-element.138.ffn0_ref.right_ref, bf16[2048,1536]{1,0:T(8,128)(2,1)} %collective-permute-done.29.refs_0_), custom_call_target="tpu_custom_call" | custom-call | flops 9663676416 | bytes 3145728 | tf_op jit(solution)/shard_map/weight_gradient/pallas_call | solution.py:707
  425.4 9.2 %collective-permute-done.33 = bf16[256,2048]{1,0:T(8,128)(2,1)S(1)} collective-permute-done((bf16[256,2048]{1,0:T(8,128)(2,1)S(1)}, bf16[256,2048]{1,0:T(8,128)(2,1)S(1)}, u32[]{:S(2)}, u32[]{:S(2)}) %collective-permute-start.33) | collective-permute-done | bytes 1048608 | tf_op jit(solution)/shard_map/ppermute | solution.py:23
  458.7 8.2 %fusion.18 = f32[1024,768]{1,0:T(8,128)} fusion(bf16[1024,2048]{1,0:T(8,128)(2,1)} %constant_dynamic-update-slice_fusion.15.right_ref, bf16[384,2048]{1,0:T(8,128)(2,1)} %collective-permute-done.11, bf16[384,2048]{1,0:T(8,128)(2,1)} %pad.81), kind=kOutput, calls=%fused_computation.38 | convolution fusion | flops 3227516928 | bytes 10485760 | tf_op jit(solution)/shard_map/dot_general | solution.py:689
  466.9 9.5 %mix_backward.1 = (bf16[4,256,768]{2,1,0:T(8,128)(2,1)S(1)}, f32[256,8,384]{2,1,0:T(8,128)S(1)}, f32[256,8,384]{2,1,0:T(8,128)}, f32[2,8,384]{2,1,0:T(8,128)S(1)}) custom-call(f32[4,256,768]{2,1,0:T(8,128)} %bitcast.325, f32[4,256,768]{2,1,0:T(8,128)} %bitcast.326, f32[4,256,1536]{2,1,0:T(8,128)} %bitcast.318, f32[4,256,1536]{2,1,0:T(8,128)} %bitcast.319, ...), custom_call_target="tpu_custom_call" | custom-call | flops 786432 | bytes 34603008 | tf_op jit(solution)/shard_map/mix_backward/pallas_call | solution.py:464
  492.7 8.9 %weight_rows.2.refs_0_ = bf16[4,1152,512]{2,1,0:T(8,128)(2,1)} custom-call(s32[1]{0:T(128)} %bitcast.44.shift_ref, bf16[1024,768]{1,0:T(8,128)(2,1)S(1)} %copy-done.19, bf16[1024,2048]{1,0:T(8,128)(2,1)} %constant_dynamic-update-slice_fusion.5.g_ref.right_ref, bf16[768,2048]{1,0:T(8,128)(2,1)} %collective-permute-done.40.added_ref), custom_call_target="tpu_custom_call" | custom-call | flops 4831838208 | bytes 1572864 | tf_op jit(solution)/shard_map/weight_rows/pallas_call | solution.py:742
  501.7 17.0 %gates_backward.1 = (bf16[4,256,768]{2,1,0:T(8,128)(2,1)S(1)}, f32[3,8,384]{2,1,0:T(8,128)S(1)}, f32[3,8,384]{2,1,0:T(8,128)S(1)}, f32[4,384,384]{2,1,0:T(8,128)S(1)}, f32[2,8,384]{2,1,0:T(8,128)S(1)}) custom-call(f32[256,8,384]{2,1,0:T(8,128)} %copy-done.4, f32[256,8,384]{2,1,0:T(8,128)} %get-tuple-element.153.tail_ref, ...), custom_call_target="tpu_custom_call" | custom-call | flops 786432 | bytes 59768832 | tf_op jit(solution)/shard_map/gates_backward/pallas_call | solution.py:487
  530.2 8.6 %weight_gradient.10 = bf16[2048,768]{1,0:T(8,128)(2,1)} custom-call(bf16[1024,2048]{1,0:T(8,128)(2,1)} %constant_dynamic-update-slice_fusion.left_ref, bf16[1024,768]{1,0:T(8,128)(2,1)S(1)} %pad_maximum_fusion.14.right_ref), custom_call_target="tpu_custom_call" | custom-call | flops 4831838208 | bytes 1572864 | tf_op jit(solution)/shard_map/weight_gradient/pallas_call | solution.py:707
  544.2 10.4 %fusion.2 = bf16[1024,2048]{1,0:T(8,128)(2,1)S(1)} fusion(bf16[1024,1536]{1,0:T(8,128)(2,1)} %pad_maximum_fusion.6, bf16[2048,768]{1,0:T(8,128)(2,1)} %collective-permute-done.6, bf16[2048,768]{1,0:T(8,128)(2,1)} %bitcast.8), kind=kOutput, calls=%fused_computation.5 | convolution fusion | flops 6457131008 | bytes 13631488 | tf_op jit(solution)/shard_map/dot_general | solution.py:689
  577.3 9.4 %slice_reduce_fusion = (f32[512,3,256]{2,1,0:T(4,128)S(1)}, f32[512,3,256]{2,1,0:T(4,128)S(1)}) fusion(f32[512,3,2,256]{3,2,1,0:T(2,128)S(1)} %reshape.526), kind=kLoop, calls=%fused_computation.39 | loop fusion | bytes 6291456 | tf_op jit(solution)/shard_map/slice | solution.py:950
  595.2 9.4 %weight_gradient.11 = bf16[2048,768]{1,0:T(8,128)(2,1)} custom-call(bf16[1024,2048]{1,0:T(8,128)(2,1)} %constant_dynamic-update-slice_fusion.left_ref, bf16[1024,768]{1,0:T(8,128)(2,1)S(1)} %slice.553.right_ref, bf16[2048,768]{1,0:T(8,128)(2,1)} %collective-permute-done.46.refs_0_), custom_call_target="tpu_custom_call" | custom-call | flops 4831838208 | bytes 1572864 | tf_op jit(solution)/shard_map/weight_gradient/pallas_call | solution.py:707
  634.6 18.8 %collective-permute-done.69 = bf16[2,2,176,176]{3,2,1,0:T(8,128)(2,1)} collective-permute-done((bf16[2,2,176,176]{3,2,1,0:T(8,128)(2,1)S(1)}, bf16[2,2,176,176]{3,2,1,0:T(8,128)(2,1)}, u32[]{:S(2)}, u32[]{:S(2)}) %collective-permute-start.69) | collective-permute-done | bytes 247840 | tf_op jit(solution)/shard_map/ppermute | solution.py:23
  678.0 15.0 %collective-permute-done.71 = bf16[2,2,176,176]{3,2,1,0:T(8,128)(2,1)S(1)} collective-permute-done((bf16[2,2,176,176]{3,2,1,0:T(8,128)(2,1)S(1)}, bf16[2,2,176,176]{3,2,1,0:T(8,128)(2,1)S(1)}, u32[]{:S(2)}, u32[]{:S(2)}) %collective-permute-start.71) | collective-permute-done | bytes 247840 | tf_op jit(solution)/shard_map/ppermute | solution.py:23
  704.8 8.7 %collective-permute-done.53 = bf16[128,2048]{1,0:T(8,128)(2,1)S(1)} collective-permute-done((bf16[128,2048]{1,0:T(8,128)(2,1)S(1)}, bf16[128,2048]{1,0:T(8,128)(2,1)S(1)}, u32[]{:S(2)}, u32[]{:S(2)}) %collective-permute-start.53) | collective-permute-done | bytes 524320 | tf_op jit(solution)/shard_map/ppermute | solution.py:23
  739.8 61.4 %collective-permute-done.76 = bf16[352,256]{1,0:T(8,128)(2,1)S(1)} collective-permute-done((bf16[352,256]{1,0:T(8,128)(2,1)S(1)}, bf16[352,256]{1,0:T(8,128)(2,1)S(1)}, u32[]{:S(2)}, u32[]{:S(2)}) %collective-permute-start.76) | collective-permute-done | bytes 180256 | tf_op jit(solution)/shard_map/ppermute | solution.py:168
  (523 shorter events, 355.4 us)
Async XLA Ops:
  7.2 46.3 %all-gather.6.cloned.1.call-start = ((), (), s32[]{:S(2)}) async-start(), calls=%async_computation.5 | async-start | bytes 1802240 | tf_op jit(solution)/shard_map/all_gather | solution.py:800
  7.9 101.8 %all-gather.8.cloned.1.call-start = ((), (), s32[]{:S(2)}) async-start(), calls=%async_computation.9 | async-start | bytes 3932160 | tf_op jit(solution)/shard_map/all_gather | solution.py:803
  27.1 250.5 %all-gather.10.cloned.1.call-start = ((), (), s32[]{:S(2)}) async-start(), calls=%async_computation.10 | async-start | bytes 11796480 | tf_op jit(solution)/shard_map/all_gather | solution.py:844
  29.1 24.3 %collective-permute-start = (bf16[256,2048]{1,0:T(8,128)(2,1)}, bf16[256,2048]{1,0:T(8,128)(2,1)S(1)}, u32[]{:S(2)}, u32[]{:S(2)}) collective-permute-start(bf16[256,2048]{1,0:T(8,128)(2,1)} %get-tuple-element.304), channel_id=1, source_target_pairs={{0,8},{4,12},{8,0},{12,4},{16,24},{20,28},{24,16},{28,20},{1,9},{5... | collective-permute-start | bytes 3145736 | tf_op jit(solution)/shard_map/ppermute | solution.py:23
  29.5 23.9 %collective-permute-start.1 = (bf16[256,2048]{1,0:T(8,128)(2,1)}, bf16[256,2048]{1,0:T(8,128)(2,1)S(1)}, u32[]{:S(2)}, u32[]{:S(2)}) collective-permute-start(bf16[256,2048]{1,0:T(8,128)(2,1)} %get-tuple-element.304), channel_id=1, source_target_pairs={{0,16},{4,20},{8,24},{12,28},{16,0},{20,4},{24,8},{28,12},{1,17},{... | collective-permute-start | bytes 3145736 | tf_op jit(solution)/shard_map/ppermute | solution.py:23
  111.3 432.9 %reduce-scatter.4.cloned.1.call-start = ((), (), s32[]{:S(2)}) async-start(), calls=%async_computation.6 | async-start | bytes 7864320 | tf_op jit(solution)/shard_map/reduce_scatter | solution.py:884
  122.6 67.3 %collective-permute-start.11 = (bf16[384,2048]{1,0:T(8,128)(2,1)}, bf16[384,2048]{1,0:T(8,128)(2,1)}, u32[]{:S(2)}, u32[]{:S(2)}) collective-permute-start(bf16[384,2048]{1,0:T(8,128)(2,1)} %pad.81), channel_id=1, source_target_pairs={{0,4},{4,0},{8,12},{12,8},{16,20},{20,16},{24,28},{28,24},{1,5},{5... | collective-permute-start | bytes 4718600 | tf_op jit(solution)/shard_map/ppermute | solution.py:23
  122.6 24.3 %collective-permute-start.4 = (bf16[256,2048]{1,0:T(8,128)(2,1)S(1)}, bf16[256,2048]{1,0:T(8,128)(2,1)S(1)}, u32[]{:S(2)}, u32[]{:S(2)}) collective-permute-start(bf16[256,2048]{1,0:T(8,128)(2,1)S(1)} %bitcast.328), channel_id=1, source_target_pairs={{0,8},{4,12},{8,0},{12,4},{16,24},{20,28},{24,16},{28,20},{1,9},{5... | collective-permute-start | bytes 3145736 | tf_op jit(solution)/shard_map/ppermute | solution.py:23
  122.9 24.0 %collective-permute-start.5 = (bf16[256,2048]{1,0:T(8,128)(2,1)S(1)}, bf16[256,2048]{1,0:T(8,128)(2,1)S(1)}, u32[]{:S(2)}, u32[]{:S(2)}) collective-permute-start(bf16[256,2048]{1,0:T(8,128)(2,1)S(1)} %bitcast.329), channel_id=1, source_target_pairs={{0,16},{4,20},{8,24},{12,28},{16,0},{20,4},{24,8},{28,12},{1,17},{... | collective-permute-start | bytes 3145736 | tf_op jit(solution)/shard_map/ppermute | solution.py:23
  200.7 22.4 %collective-permute-start.19 = (bf16[128,2048]{1,0:T(8,128)(2,1)S(1)}, bf16[128,2048]{1,0:T(8,128)(2,1)S(1)}, u32[]{:S(2)}, u32[]{:S(2)}) collective-permute-start(bf16[128,2048]{1,0:T(8,128)(2,1)S(1)} %get-tuple-element.328), channel_id=1, source_target_pairs={{0,16},{4,20},{8,24},{12,28},{16,0},{20,4},{24,8},{28,12},{1,17},{... | collective-permute-start | bytes 1572872 | tf_op jit(solution)/shard_map/ppermute | solution.py:23
  212.3 22.1 %collective-permute-start.17 = (bf16[128,2048]{1,0:T(8,128)(2,1)S(1)}, bf16[128,2048]{1,0:T(8,128)(2,1)S(1)}, u32[]{:S(2)}, u32[]{:S(2)}) collective-permute-start(bf16[128,2048]{1,0:T(8,128)(2,1)S(1)} %get-tuple-element.331), channel_id=1, source_target_pairs={{0,16},{4,20},{8,24},{12,28},{16,0},{20,4},{24,8},{28,12},{1,17},{... | collective-permute-start | bytes 1572872 | tf_op jit(solution)/shard_map/ppermute | solution.py:23
  288.3 28.7 %collective-permute-start.24 = (bf16[768,2048]{1,0:T(8,128)(2,1)S(1)}, bf16[768,2048]{1,0:T(8,128)(2,1)}, u32[]{:S(2)}, u32[]{:S(2)}) collective-permute-start(bf16[768,2048]{1,0:T(8,128)(2,1)S(1)} %unpack_down.1.down0_ref), channel_id=1, source_target_pairs={{0,4},{4,0},{8,12},{12,8},{16,20},{20,16},{24,28},{28,24},{1,5},{5... | collective-permute-start | bytes 9437192 | tf_op jit(solution)/shard_map/ppermute | solution.py:23
  344.5 33.9 %collective-permute-start.29 = (bf16[2048,1536]{1,0:T(8,128)(2,1)}, bf16[2048,1536]{1,0:T(8,128)(2,1)}, u32[]{:S(2)}, u32[]{:S(2)}) collective-permute-start(bf16[2048,1536]{1,0:T(8,128)(2,1)} %weight_gradient.6), channel_id=1, source_target_pairs={{0,4},{4,0},{8,12},{12,8},{16,20},{20,16},{24,28},{28,24},{1,5},{5... | collective-permute-start | bytes 18874376 | tf_op jit(solution)/shard_map/ppermute | solution.py:23
  366.8 27.6 %collective-permute-start.26 = (bf16[128,2048]{1,0:T(8,128)(2,1)}, bf16[128,2048]{1,0:T(8,128)(2,1)}, u32[]{:S(2)}, u32[]{:S(2)}) collective-permute-start(bf16[128,2048]{1,0:T(8,128)(2,1)} %get-tuple-element.321), channel_id=1, source_target_pairs={{0,8},{4,12},{8,0},{12,4},{16,24},{20,28},{24,16},{28,20},{1,9},{5... | collective-permute-start | bytes 1572872 | tf_op jit(solution)/shard_map/ppermute | solution.py:23
  368.0 26.4 %collective-permute-start.32 = (bf16[128,2048]{1,0:T(8,128)(2,1)}, bf16[128,2048]{1,0:T(8,128)(2,1)}, u32[]{:S(2)}, u32[]{:S(2)}) collective-permute-start(bf16[128,2048]{1,0:T(8,128)(2,1)} %get-tuple-element.322), channel_id=1, source_target_pairs={{0,16},{4,20},{8,24},{12,28},{16,0},{20,4},{24,8},{28,12},{1,17},{... | collective-permute-start | bytes 1572872 | tf_op jit(solution)/shard_map/ppermute | solution.py:23
  405.0 315.3 %reduce-scatter.8.cloned.1.call-start = ((), (), s32[]{:S(2)}) async-start(), calls=%async_computation.8 | async-start | bytes 5898240 | tf_op jit(solution)/shard_map/reduce_scatter | solution.py:937
  411.4 23.2 %collective-permute-start.33 = (bf16[256,2048]{1,0:T(8,128)(2,1)S(1)}, bf16[256,2048]{1,0:T(8,128)(2,1)S(1)}, u32[]{:S(2)}, u32[]{:S(2)}) collective-permute-start(bf16[256,2048]{1,0:T(8,128)(2,1)S(1)} %fusion.76), channel_id=1, source_target_pairs={{0,8},{4,12},{8,0},{12,4},{16,24},{20,28},{24,16},{28,20},{1,9},{5... | collective-permute-start | bytes 3145736 | tf_op jit(solution)/shard_map/ppermute | solution.py:23
  412.6 22.8 %collective-permute-start.34 = (bf16[256,2048]{1,0:T(8,128)(2,1)S(1)}, bf16[256,2048]{1,0:T(8,128)(2,1)S(1)}, u32[]{:S(2)}, u32[]{:S(2)}) collective-permute-start(bf16[256,2048]{1,0:T(8,128)(2,1)S(1)} %fusion.76), channel_id=1, source_target_pairs={{0,16},{4,20},{8,24},{12,28},{16,0},{20,4},{24,8},{28,12},{1,17},{... | collective-permute-start | bytes 3145736 | tf_op jit(solution)/shard_map/ppermute | solution.py:23
  454.5 38.2 %collective-permute-start.40 = (bf16[768,2048]{1,0:T(8,128)(2,1)}, bf16[768,2048]{1,0:T(8,128)(2,1)}, u32[]{:S(2)}, u32[]{:S(2)}) collective-permute-start(bf16[768,2048]{1,0:T(8,128)(2,1)} %weight_gradient.8), channel_id=1, source_target_pairs={{0,4},{4,0},{8,12},{12,8},{16,20},{20,16},{24,28},{28,24},{1,5},{5... | collective-permute-start | bytes 9437192 | tf_op jit(solution)/shard_map/ppermute | solution.py:23
  554.6 36.6 %collective-permute-start.46 = (bf16[2048,768]{1,0:T(8,128)(2,1)}, bf16[2048,768]{1,0:T(8,128)(2,1)}, u32[]{:S(2)}, u32[]{:S(2)}) collective-permute-start(bf16[2048,768]{1,0:T(8,128)(2,1)} %weight_gradient.10), channel_id=1, source_target_pairs={{0,4},{4,0},{8,12},{12,8},{16,20},{20,16},{24,28},{28,24},{1,5},{5... | collective-permute-start | bytes 9437192 | tf_op jit(solution)/shard_map/ppermute | solution.py:23
  562.2 241.3 %reduce-scatter.6.cloned.1.call-start = ((), (), s32[]{:S(2)}) async-start(), calls=%async_computation.7 | async-start | bytes 3932160 | tf_op jit(solution)/shard_map/reduce_scatter | solution.py:952
  572.3 82.4 %collective-permute-start.43 = (bf16[128,2048]{1,0:T(8,128)(2,1)}, bf16[128,2048]{1,0:T(8,128)(2,1)}, u32[]{:S(2)}, u32[]{:S(2)}) collective-permute-start(bf16[128,2048]{1,0:T(8,128)(2,1)} %get-tuple-element.315), channel_id=1, source_target_pairs={{0,8},{4,12},{8,0},{12,4},{16,24},{20,28},{24,16},{28,20},{1,9},{5... | collective-permute-start | bytes 1572872 | tf_op jit(solution)/shard_map/ppermute | solution.py:23
  589.7 65.0 %collective-permute-start.49 = (bf16[128,2048]{1,0:T(8,128)(2,1)}, bf16[128,2048]{1,0:T(8,128)(2,1)}, u32[]{:S(2)}, u32[]{:S(2)}) collective-permute-start(bf16[128,2048]{1,0:T(8,128)(2,1)} %get-tuple-element.316), channel_id=1, source_target_pairs={{0,16},{4,20},{8,24},{12,28},{16,0},{20,4},{24,8},{28,12},{1,17},{... | collective-permute-start | bytes 1572872 | tf_op jit(solution)/shard_map/ppermute | solution.py:23
  624.2 30.4 %collective-permute-start.47 = (bf16[128,2048]{1,0:T(8,128)(2,1)}, bf16[128,2048]{1,0:T(8,128)(2,1)}, u32[]{:S(2)}, u32[]{:S(2)}) collective-permute-start(bf16[128,2048]{1,0:T(8,128)(2,1)} %get-tuple-element.319), channel_id=1, source_target_pairs={{0,16},{4,20},{8,24},{12,28},{16,0},{20,4},{24,8},{28,12},{1,17},{... | collective-permute-start | bytes 1572872 | tf_op jit(solution)/shard_map/ppermute | solution.py:23
  628.1 26.6 %collective-permute-start.48 = (bf16[128,2048]{1,0:T(8,128)(2,1)}, bf16[128,2048]{1,0:T(8,128)(2,1)}, u32[]{:S(2)}, u32[]{:S(2)}) collective-permute-start(bf16[128,2048]{1,0:T(8,128)(2,1)} %get-tuple-element.320), channel_id=1, source_target_pairs={{0,8},{4,12},{8,0},{12,4},{16,24},{20,28},{24,16},{28,20},{1,9},{5... | collective-permute-start | bytes 1572872 | tf_op jit(solution)/shard_map/ppermute | solution.py:23
  630.4 23.0 %collective-permute-start.69 = (bf16[2,2,176,176]{3,2,1,0:T(8,128)(2,1)S(1)}, bf16[2,2,176,176]{3,2,1,0:T(8,128)(2,1)}, u32[]{:S(2)}, u32[]{:S(2)}) collective-permute-start(bf16[2,2,176,176]{3,2,1,0:T(8,128)(2,1)S(1)} %fusion.32), channel_id=1, source_target_pairs={{0,1},{1,0},{2,3},{3,2},{4,5},{5,4},{6,7},{7,6},{8,9},{9,8},{10,11... | collective-permute-start | bytes 743432 | tf_op jit(solution)/shard_map/ppermute | solution.py:23
  669.5 35.3 %collective-permute-start.50 = (bf16[128,2048]{1,0:T(8,128)(2,1)S(1)}, bf16[128,2048]{1,0:T(8,128)(2,1)S(1)}, u32[]{:S(2)}, u32[]{:S(2)}) collective-permute-start(bf16[128,2048]{1,0:T(8,128)(2,1)S(1)} %copy-done.54), channel_id=1, source_target_pairs={{0,8},{4,12},{8,0},{12,4},{16,24},{20,28},{24,16},{28,20},{1,9},{5... | collective-permute-start | bytes 1572872 | tf_op jit(solution)/shard_map/ppermute | solution.py:23
  670.7 34.1 %collective-permute-start.55 = (bf16[128,2048]{1,0:T(8,128)(2,1)S(1)}, bf16[128,2048]{1,0:T(8,128)(2,1)S(1)}, u32[]{:S(2)}, u32[]{:S(2)}) collective-permute-start(bf16[128,2048]{1,0:T(8,128)(2,1)S(1)} %copy-done.53), channel_id=1, source_target_pairs={{0,16},{4,20},{8,24},{12,28},{16,0},{20,4},{24,8},{28,12},{1,17},{... | collective-permute-start | bytes 1572872 | tf_op jit(solution)/shard_map/ppermute | solution.py:23
  675.3 26.3 %collective-permute-start.73 = (bf16[2,2,176,176]{3,2,1,0:T(8,128)(2,1)S(1)}, bf16[2,2,176,176]{3,2,1,0:T(8,128)(2,1)S(1)}, u32[]{:S(2)}, u32[]{:S(2)}) collective-permute-start(bf16[2,2,176,176]{3,2,1,0:T(8,128)(2,1)S(1)} %add_convert_fusion.9), channel_id=1, source_target_pairs={{0,24},{4,28},{8,16},{12,20},{16,8},{20,12},{24,0},{28,4},{1,25},{... | collective-permute-start | bytes 743432 | tf_op jit(solution)/shard_map/ppermute | solution.py:23
  731.8 70.3 %collective-permute-start.77 = (bf16[768,256]{1,0:T(8,128)(2,1)S(1)}, bf16[768,256]{1,0:T(8,128)(2,1)S(1)}, u32[]{:S(2)}, u32[]{:S(2)}) collective-permute-start(bf16[768,256]{1,0:T(8,128)(2,1)S(1)} %bitcast.361), channel_id=1, source_target_pairs={{0,0},{1,8},{2,16},{3,24},{4,28},{5,20},{6,12},{7,4},{8,9},{9,1},{... | collective-permute-start | bytes 1179656 | tf_op jit(solution)/shard_map/ppermute | solution.py:168
  737.4 64.8 %collective-permute-start.78 = (bf16[768,256]{1,0:T(8,128)(2,1)S(1)}, bf16[768,256]{1,0:T(8,128)(2,1)S(1)}, u32[]{:S(2)}, u32[]{:S(2)}) collective-permute-start(bf16[768,256]{1,0:T(8,128)(2,1)S(1)} %bitcast.360), channel_id=1, source_target_pairs={{0,4},{1,12},{2,20},{3,28},{4,24},{5,16},{6,8},{7,0},{8,13},{9,5},... | collective-permute-start | bytes 1179656 | tf_op jit(solution)/shard_map/ppermute | solution.py:168
  738.7 62.4 %collective-permute-start.76 = (bf16[352,256]{1,0:T(8,128)(2,1)S(1)}, bf16[352,256]{1,0:T(8,128)(2,1)S(1)}, u32[]{:S(2)}, u32[]{:S(2)}) collective-permute-start(bf16[352,256]{1,0:T(8,128)(2,1)S(1)} %bitcast.366), channel_id=1, source_target_pairs={{0,4},{1,12},{2,20},{3,28},{4,24},{5,16},{6,8},{7,0},{8,13},{9,5},... | collective-permute-start | bytes 540680 | tf_op jit(solution)/shard_map/ppermute | solution.py:168
  (124 other events, 1291.9 us)
Sparse Core Ops, SparseCore 0:
  9.6 35.4 all-gather.5
  46.6 63.0 all-gather.7
  111.9 165.6 all-gather.9
  405.1 115.8 reduce-scatter.3
  562.4 91.2 reduce-scatter.7
  662.6 61.5 reduce-scatter.5

commit v3 on v2

--- a/solution.py
+++ b/solution.py
@@ -43,30 +43,58 @@
     return jnp.concatenate(slots, axis=0), *beside
 
 
-def scatter_tokens(partial, *beside):
+def scatter_begin(partial):
     chips = lax.axis_size("dp") // 2
-    wide = [partial[o].astype(F32) for o in range(chips)]
     if chips == 4:
         half = partial.shape[1] // 2
         via_x = xor_send(partial[3, :half], "dp", 2)
         via_y = xor_send(partial[3, half:], "dp", 4)
         x_top = xor_send(partial[1, :half], "dp", 2)
         y_bottom = xor_send(partial[2, half:], "dp", 4)
-        via_x, via_y, *beside = tie(via_x, via_y, *beside)
-        x_bottom = xor_send((wide[1][half:] + via_y.astype(F32)).astype(BF16), "dp", 2)
-        y_top = xor_send((wide[2][:half] + via_x.astype(F32)).astype(BF16), "dp", 4)
-        total = jnp.concatenate(
-            [
-                wide[0][:half] + x_top.astype(F32) + y_top.astype(F32),
-                wide[0][half:] + x_bottom.astype(F32) + y_bottom.astype(F32),
-            ],
-            axis=0,
-        )
-        return total, *beside
-    total = wide[0]
-    for o in range(1, chips):
-        total = total + xor_send(partial[o], "dp", 2 * o).astype(F32)
-    return total, *beside
+        return (via_x, via_y), (x_top, y_bottom, partial)
+    return (), tuple(xor_send(partial[o], "dp", 2 * o) for o in range(1, chips)) + (partial,)
+
+
+def scatter_middle(via, kept):
+    if not via:
+        return ()
+    partial = kept[-1]
+    half = partial.shape[1] // 2
+    to_x = (partial[1, half:].astype(F32) + via[1].astype(F32)).astype(BF16)
+    to_y = (partial[2, :half].astype(F32) + via[0].astype(F32)).astype(BF16)
+    return to_x, to_y
+
+
+def scatter_send(sums):
+    return (xor_send(sums[0], "dp", 2), xor_send(sums[1], "dp", 4)) if sums else ()
+
+
+def scatter_end(hops, kept):
+    partial = kept[-1]
+    mine = partial[0].astype(F32)
+    if not hops:
+        for moved in kept[:-1]:
+            mine = mine + moved.astype(F32)
+        return mine
+    x_bottom, y_top = hops
+    x_top, y_bottom, _ = kept
+    half = partial.shape[1] // 2
+    return jnp.concatenate(
+        [
+            mine[:half] + x_top.astype(F32) + y_top.astype(F32),
+            mine[half:] + x_bottom.astype(F32) + y_bottom.astype(F32),
+        ],
+        axis=0,
+    )
+
+
+def scatter_tokens(partial, *beside):
+    via, kept = scatter_begin(partial)
+    if via:
+        *via, = tie(*via, *beside)
+        via, beside = via[:2], via[2:]
+    hops = scatter_send(scatter_middle(via, kept))
+    return scatter_end(hops, kept), *beside
 
 
 def join_cores(own_half, other_half):
@@ -93,8 +121,9 @@
     return slots
 
 
-def widen_blocks_kernel(mine_ref, slot_ref, out_ref):
-    out_ref[...] = slot_ref[0].astype(F32)
+def widen_blocks_kernel(mine_ref, slot_ref, *out_refs):
+    for kind, out_ref in enumerate(out_refs):
+        out_ref[...] = slot_ref[0, kind].astype(F32)
 
 
 def widen_blocks(slots):
@@ -102,24 +131,24 @@
     mine = lax.axis_index("dp").astype(jnp.int32).reshape(1)
     return pl.pallas_call(
         widen_blocks_kernel,
-        out_shape=jax.ShapeDtypeStruct((kinds, count * heads, rows, cols), F32),
+        out_shape=(jax.ShapeDtypeStruct((count * heads, rows, cols), F32),) * kinds,
         grid_spec=pltpu.PrefetchScalarGridSpec(
             num_scalar_prefetch=1,
             grid=(count,),
             in_specs=[
                 pl.BlockSpec((1, kinds, heads, rows, cols), lambda d, m: (d ^ m[0], 0, 0, 0, 0))
             ],
-            out_specs=pl.BlockSpec((kinds, heads, rows, cols), lambda d, m: (0, d, 0, 0)),
+            out_specs=(pl.BlockSpec((heads, rows, cols), lambda d, m: (d, 0, 0)),) * kinds,
         ),
         compiler_params=params(),
         name="widen_blocks",
     )(mine, slots)
 
 
-def sum_over(value, axis):
-    offset = 1
+def sum_over(value, axis, begin=1, end=None):
+    offset = begin
     total = value
-    while offset < lax.axis_size(axis):
+    while offset < (end or lax.axis_size(axis)):
         moved = xor_send(total, axis, offset)
         total = (total.astype(F32) + moved.astype(F32)).astype(value.dtype)
         offset *= 2
@@ -149,25 +178,32 @@
     return group ^ flip
 
 
-def place_rows(block):
+def move_in_plane(block):
     dp_count, seq_count = lax.axis_size("dp"), lax.axis_size("seq")
-    ratio = dp_count // seq_count
-    rows, cols = block.shape
-    width = cols // ratio
-    mine, seat = lax.axis_index("dp"), lax.axis_index("seq")
-    parts = block.reshape(rows, ratio, width)
-    out = jnp.zeros((ratio, rows, width), block.dtype)
-    for turn in range(ratio):
-        perm = []
-        for d in range(dp_count):
-            for s in range(seq_count):
-                quarter = s ^ shift_of(d, ratio, seq_count)
-                to = ratio * quarter + (d + turn) % ratio
-                perm.append((d * seq_count + s, to * seq_count + d // ratio))
-        chosen = lax.dynamic_index_in_dim(parts, (mine + turn) % ratio, 1, keepdims=False)
-        got = lax.ppermute(chosen, ("dp", "seq"), perm)
-        out = lax.dynamic_update_index_in_dim(out, got, (mine - turn) % ratio, 0)
-    return out.reshape(ratio * rows, width)
+    perm = []
+    for d in range(dp_count):
+        for s in range(seq_count):
+            quarter = s ^ shift_of(d, dp_count // seq_count, seq_count)
+            perm.append((d * seq_count + s, (2 * quarter + d % 2) * seq_count + s))
+    return lax.ppermute(block, ("dp", "seq"), perm)
+
+
+def move_across(block):
+    dp_count, seq_count = lax.axis_size("dp"), lax.axis_size("seq")
+    assert dp_count == 2 * seq_count
+    perm = []
+    for d in range(dp_count):
+        for s in range(seq_count):
+            perm.append((d * seq_count + s, d * seq_count + (s ^ shift_of(d, 2, seq_count))))
+    block = lax.ppermute(block, ("dp", "seq"), perm)
+    half = block.shape[1] // 2
+    first_core = lax.axis_index("dp") % 2 == 0
+    left, right = block[:, :half], block[:, half:]
+    kept = jnp.where(first_core, left, right)
+    moved = xor_send(jnp.where(first_core, right, left), "dp", 1)
+    return jnp.concatenate(
+        [jnp.where(first_core, kept, moved), jnp.where(first_core, moved, kept)], axis=0
+    )
 
 
 def scaled_norm(values, gain_vec):
@@ -311,8 +347,8 @@
 def back_gates_kernel(
     gl_ref, tail_ref, rate_ref, m_ref, r_ref, i_ref, conv_ref, prev_ref, bt_ref,
     hin_ref, prior_ref, taps_ref, vec_ref, w_ref,
-    gbranch_ref, last_ref, head_ref, dw_ref, total_ref,
-    later, sums_ref,
+    gbranch_ref, last_ref, head_ref, dw_own_ref, dw_other_ref, total_ref,
+    later, sums_ref, dw_ref,
 ):
     chunk, slots, width = rate_ref.shape
     lag = later.shape[0]
@@ -342,8 +378,8 @@
     over_rows = (((0,), (0,)), ((), ()))
     over_cols = (((1,), (1,)), ((), ()))
     dw_ref[0] += lax.dot_general(rows_own, dpr, over_rows, preferred_element_type=F32)
-    dw_ref[1] += lax.dot_general(rows_other, dpr, over_rows, preferred_element_type=F32)
-    dw_ref[2] += lax.dot_general(rows_own, dpi, over_rows, preferred_element_type=F32)
+    dw_ref[1] += lax.dot_general(rows_own, dpi, over_rows, preferred_element_type=F32)
+    dw_ref[2] += lax.dot_general(rows_other, dpr, over_rows, preferred_element_type=F32)
     dw_ref[3] += lax.dot_general(rows_other, dpi, over_rows, preferred_element_type=F32)
 
     def through(which):
@@ -380,6 +416,14 @@
         for kind in range(total_ref.shape[1]):
             total_ref[0, kind] = jnp.sum(sums_ref[kind, :half], axis=0)
             total_ref[1, kind] = jnp.sum(sums_ref[kind, half:], axis=0)
+        heads, head = dw_own_ref.shape[1:3]
+        for kind in range(2):
+            for h in range(heads):
+                for begin, ref in ((0, dw_own_ref), (2, dw_other_ref)):
+                    rows = dw_ref[begin + kind, h * head : (h + 1) * head, :]
+                    if h:
+                        rows = pltpu.roll(rows, width - h * head, 1)
+                    ref[kind, h] = rows[:, :head].astype(ref.dtype)
 
 
 def specs_for(slots, length, width, backwards):
@@ -479,7 +523,7 @@
     )(gm, gm, both, both, across, rate)
 
 
-def back_gates(kept, hin, prior, taps, vecs, w):
+def back_gates(kept, hin, prior, taps, vecs, w, heads, head):
     length, slots, width = kept[0].shape
     lag = prior.shape[0]
     count, tm, cols = specs_for(slots, length, width, True)
@@ -490,7 +534,8 @@
             jax.ShapeDtypeStruct((slots // 2, length, 2 * width), BF16),
             jax.ShapeDtypeStruct((lag, slots, width), F32),
             jax.ShapeDtypeStruct((lag, slots, width), F32),
-            jax.ShapeDtypeStruct(w.shape, F32),
+            jax.ShapeDtypeStruct((2, heads, head, head), F32),
+            jax.ShapeDtypeStruct((2, heads, head, head), BF16),
             jax.ShapeDtypeStruct((2, 5 + lag, width), F32),
         ),
         grid=(count,),
@@ -501,11 +546,12 @@
         ],
         out_specs=(
             cols(0, 2), whole(lag, slots, width), whole(lag, slots, width),
-            whole(*w.shape), whole(2, 5 + lag, width),
+            whole(2, heads, head, head), whole(2, heads, head, head), whole(2, 5 + lag, width),
         ),
         scratch_shapes=[
             pltpu.VMEM((lag, slots, width), F32),
             pltpu.VMEM((5 + lag, slots, width), F32),
+            pltpu.VMEM(w.shape, F32),
         ],
         compiler_params=params(),
         cost_estimate=cost(n, 76 * n, n),
@@ -675,18 +721,6 @@
         cost_estimate=cost(0, 2 * rows * dp_count * part * 2, 0),
         name="unpack_down",
     )(packed)
-
-
-def rows_of(value):
-    return value.reshape(-1, value.shape[-1])
-
-
-def mm(left, right):
-    return jnp.dot(left, right, preferred_element_type=F32)
-
-
-def mm_back(grad_rows, weight):
-    return lax.dot_general(grad_rows, weight, (((1,), (1,)), ((), ())), preferred_element_type=F32)
 
 
 def weight_kernel(left_ref, right_ref, *refs):
@@ -720,8 +754,7 @@
     )(left, right, *added)
 
 
-def weight_rows_kernel(shift_ref, left_ref, right_ref, added_ref, *refs):
-    out_ref = refs[-1]
+def weight_rows_kernel(shift_ref, left_ref, right_ref, added_ref, out_ref):
     product = lax.dot_general(
         left_ref[...], right_ref[...], (((0,), (0,)), ((), ())), preferred_element_type=F32
     )
@@ -731,17 +764,15 @@
         out_ref[quarter ^ shift_ref[0]] = product[:, quarter * cols : (quarter + 1) * cols]
 
 
-def weight_rows(left, right, added, total_rows, first_row, into=None):
+def weight_rows(left, right, added):
     depth, rows = left.shape
     cols = right.shape[1]
     count = lax.axis_size("seq")
     tile = 128
     shift = quarter_shift().astype(jnp.int32).reshape(1)
-    begin = first_row // tile
-    more = [] if into is None else [into]
     return pl.pallas_call(
         weight_rows_kernel,
-        out_shape=jax.ShapeDtypeStruct((count, total_rows, cols // count), BF16),
+        out_shape=jax.ShapeDtypeStruct((count, rows, cols // count), BF16),
         grid_spec=pltpu.PrefetchScalarGridSpec(
             num_scalar_prefetch=1,
             grid=(rows // tile,),
@@ -749,17 +780,25 @@
                 pl.BlockSpec((depth, tile), lambda i, s: (0, i)),
                 pl.BlockSpec((depth, cols), lambda i, s: (0, 0), pipeline_mode=pl.Buffered(1)),
                 pl.BlockSpec((tile, cols), lambda i, s: (i, 0)),
-            ]
-            + [pl.BlockSpec(memory_space=pl.ANY)] * len(more),
-            out_specs=pl.BlockSpec(
-                (count, tile, cols // count), lambda i, s: (0, begin + i, 0)
-            ),
-        ),
-        input_output_aliases={4: 0} if more else {},
+            ],
+            out_specs=pl.BlockSpec((count, tile, cols // count), lambda i, s: (0, i, 0)),
+        ),
         compiler_params=params(),
         cost_estimate=cost(3 * rows * cols * depth, rows * cols, 0),
         name="weight_rows",
-    )(shift, left, right, added, *more)
+    )(shift, left, right, added)
+
+
+def rows_of(value):
+    return value.reshape(-1, value.shape[-1])
+
+
+def mm(left, right):
+    return jnp.dot(left, right, preferred_element_type=F32)
+
+
+def mm_back(grad_rows, weight):
+    return lax.dot_general(grad_rows, weight, (((1,), (1,)), ((), ())), preferred_element_type=F32)
 
 
 def local(
@@ -824,6 +863,8 @@
         [block_diagonal(w, i) for w in (recur_weight, input_weight) for i in (mine, mine ^ 1)]
     )
 
+    taps, vecs, w_gates = tie(taps, vecs, w_gates)
+
     normed = scaled_norm(tokens, norm_gain).astype(BF16)
     normed_all, w_out = gather_tokens(normed, w_out)
     w_out = jnp.pad(w_out, ((0, width - own), (0, 0)))
@@ -870,9 +911,13 @@
     w_down = (w_down, partner(w_down))
     hidden, kept = zip(*[mlp_forward(normed_two_all, weight) for weight in w_second])
     hidden = list(hidden)
+    moved_down, grad_all = tie(mm_weight(hidden[1], grad_all), grad_all)
+    moved_down = xor_send(moved_down, "dp", 1)
     grad_ffn = list(hidden_backward(grad_all, w_down, kept))
     moved = mm_weight(normed_two_all, grad_ffn[1])
-    grad_ffn[0], moved = tie(grad_ffn[0], moved)
+    grad_down = weight_rows(hidden[0], grad_all, moved_down)
+    grad_ffn[0], moved, grad_down = tie(grad_ffn[0], moved, grad_down)
+    down_cols = lax.psum_scatter(grad_down, "seq", scatter_dimension=0, tiled=False)
     moved = xor_send(moved, "dp", 1)
     partial = normed_backward(grad_ffn, w_second)
     partial, grad_ffn[0], normed_two_all = tie(partial, grad_ffn[0], normed_two_all)
@@ -895,28 +940,26 @@
 
     grad_rec, hidden[0], hidden[1] = tie(grad_residual.astype(BF16), *hidden)
     out_partial = mm(hidden[0], w_down[0]) + mm(hidden[1], w_down[1])
-    grad_rec_all, out_partial, hidden[0], hidden[1] = gather_tokens(
-        grad_rec, out_partial.astype(BF16), *hidden
-    )
-    moved = mm_weight(hidden[1], grad_all)
-    grad_rec_all, moved = tie(grad_rec_all, moved)
-    grad_rows = weight_rows(
-        hidden[0], grad_all, xor_send(moved, "dp", 1), hidden_width + width, 0
-    )
+    grad_rec_all, out_partial, down_cols = gather_tokens(
+        grad_rec, out_partial.astype(BF16), down_cols
+    )
+    grad_rec_all, out_partial = tie(grad_rec_all, out_partial)
+    via, kept_out = scatter_begin(out_partial.reshape(chips, length, model))
     gm = mm_back(grad_rec_all, w_out)
     gm = gm.reshape(chips, length, 2 * width)
     ggate, gl, tail, end = back_mix(gm, both, across, rate)
     hin = carry_in(end[0], end[1], -1)
     moved = mm_weight(mixed[:, width:], grad_rec_all)
-    hin, moved, grad_rows = tie(hin, moved, grad_rows)
-    moved = xor_send(moved, "dp", 1)
-    grad_rows = weight_rows(
-        mixed[:, :width], grad_rec_all, moved, hidden_width + width, hidden_width, grad_rows
-    )
-    gbranch, last, head_rows, dw, sums = back_gates(
-        (gl, tail, rate, m, r, g, conv, prev, bt), hin, prior, taps, vecs, w_gates
-    )
-    later = shift_send(head_rows, "seq", -1)
+    hin, moved, *out_sums = tie(hin, moved, *scatter_middle(via, kept_out))
+    hops = scatter_send(out_sums)
+    grad_out = weight_rows(mixed[:, :width], grad_rec_all, xor_send(moved, "dp", 1))
+    hin, grad_out = tie(hin, grad_out)
+    gbranch, last, head_rows, dw_own, dw_other, sums = back_gates(
+        (gl, tail, rate, m, r, g, conv, prev, bt), hin, prior, taps, vecs, w_gates,
+        own_heads, head,
+    )
+    later, down_cols = tie(shift_send(head_rows, "seq", -1), down_cols)
+    down_cols = move_in_plane(down_cols)
     fixed = []
     for j in range(lag):
         row = last[j]
@@ -931,49 +974,52 @@
         [gbranch[:, :width], ggate[:, :width], gbranch[:, width:], ggate[:, width:]], axis=1
     )
     moved = mm_weight(normed_all, grad_first[:, 2 * width :])
-    grad_first, moved, grad_rows, grad_second_rows = tie(
-        grad_first, moved, grad_rows, grad_second_rows
-    )
-    row_cols = lax.psum_scatter(grad_rows, "seq", scatter_dimension=0, tiled=False)
+    blocks = (dw_own + xor_send(dw_other, "dp", 1).astype(F32)).astype(BF16)
+    blocks = sum_over(blocks, "seq", 1, 2)
+    grad_first, moved, grad_second_rows, blocks = tie(
+        grad_first, moved, grad_second_rows, blocks
+    )
+    blocks = sum_over(blocks, "seq", 2)
     moved = xor_send(moved, "dp", 1)
     partial = mm_back(grad_first, w_first).astype(BF16)
-    partial, normed_all = tie(partial, normed_all)
-    grad_normed, moved, grad_first, dw, sums = scatter_tokens(
-        partial.reshape(chips, length, model), moved, grad_first, dw, sums
-    )
+    partial, normed_all, sums, blocks, grad_out = tie(
+        partial, normed_all, sums, blocks, grad_out
+    )
+    out_cols = lax.psum_scatter(grad_out, "seq", scatter_dimension=0, tiled=False)
     grad_first_w = mm_weight(normed_all, grad_first[:, : 2 * width], moved)
-    grad_normed, grad_first_w, out_partial = tie(grad_normed, grad_first_w, out_partial)
-    (total,) = scatter_tokens(out_partial.reshape(chips, length, model))
+    sums = sums[0] + xor_send(sums[1], "dp", 1)
+    partial, grad_first_w = tie(partial, grad_first_w)
+    grad_normed, sums, out_cols, normed_all, down_cols, *hops = scatter_tokens(
+        partial.reshape(chips, length, model),
+        sum_over(sums, "seq", 1, 2), out_cols, normed_all, down_cols, *hops,
+    )
+    out_cols = move_in_plane(out_cols[:own])
+    norm_gain_term = jnp.sum(partial.astype(F32) * normed_all.astype(F32), axis=0) / norm_gain
+    grad_normed, sums, blocks = tie(grad_normed, sum_over(sums, "seq", 2), blocks)
+    total = scatter_end(hops, kept_out)
     block_output = (residual + total).astype(BF16).reshape(block_input.shape)
-    grad_second_rows = grad_second_rows.reshape(-1, hidden_width // tile, 2, tile).astype(F32)
-    grad_mgate_w = grad_second_rows[:, :, 0].reshape(-1, hidden_width)
-    grad_mup_w = grad_second_rows[:, :, 1].reshape(-1, hidden_width)
-    norm_gain_term = jnp.sum(partial.astype(F32) * normed_all.astype(F32), axis=0) / norm_gain
+    sums, blocks = gather_small(sums), gather_small(blocks)
+
+    def tiles_of(which):
+        begins = range(which * tile, 2 * hidden_width, 2 * tile)
+        return jnp.concatenate([grad_second_rows[:, at : at + tile] for at in begins], axis=1)
+
+    grad_mgate_w, grad_mup_w = tiles_of(0).astype(F32), tiles_of(1).astype(F32)
     grad_first_w = lax.psum_scatter(grad_first_w, "seq", scatter_dimension=0, tiled=True)
-    grad_in_w = grad_first_w[:, :own].astype(F32)
-    grad_gate_w = grad_first_w[:, width : width + own].astype(F32)
     inv_one = lax.rsqrt(jnp.mean(tokens * tokens, axis=-1, keepdims=True) + EPSILON)
     grad_tokens, _ = norm_back(grad_normed, tokens, inv_one, norm_gain)
     input_grad = (grad_tokens + grad_residual).reshape(block_input.shape)
-
-    down_cols, out_cols = row_cols[:hidden_width], row_cols[hidden_width : hidden_width + own]
-    grad_down_w = place_rows(down_cols).astype(F32)
-    grad_out_w = place_rows(out_cols).astype(F32)
-
-    sums = sum_over(sums[0] + xor_send(sums[1], "dp", 1), "seq")
-    sums = natural_order(gather_small(sums))[:, :, :own]
-    sums = jnp.swapaxes(sums, 0, 1).reshape(-1, recur_width)
+    grad_first_w, down_cols, out_cols, input_grad = tie(
+        grad_first_w, down_cols, out_cols, input_grad
+    )
+    grad_down_w = move_across(down_cols).astype(F32)
+    grad_out_w = move_across(out_cols).astype(F32)
+    grad_in_w = grad_first_w[:, :own].astype(F32)
+    grad_gate_w = grad_first_w[:, width : width + own].astype(F32)
+
+    sums = jnp.swapaxes(natural_order(sums)[:, :, :own], 0, 1).reshape(-1, recur_width)
     decay_term = sums[2] * (8.0 * jax.nn.sigmoid(-decay_param))
-
-    def diagonal(full):
-        return jnp.stack(
-            [full[h * head : (h + 1) * head, h * head : (h + 1) * head] for h in range(own_heads)]
-        )
-
-    blocks = jnp.stack([diagonal(dw[0]), diagonal(dw[2])])
-    blocks = join_cores(blocks, jnp.stack([diagonal(dw[1]), diagonal(dw[3])]))
-    blocks = sum_over(blocks, "seq")
-    blocks = widen_blocks(gather_small(blocks))
+    blocks = widen_blocks(blocks)
     gains = sum_over(sum_over(jnp.stack([norm_gain_term, mlp_gain_term]), "dp"), "seq")
     return (
         block_output,

time: 824 us -> 750 us (0.910)
  waiting for transfers between devices: 274 us -> 205 us
  local copies, waits for them, and re-layouts: 113 us -> 91.6 us
  starting transfers between devices: 85.9 us -> 102 us
    ppermute x4, waiting for transfers between devices: 61.4 us -> 13.8 us  [the longest x2 13.7 us: move_across(): block = lax.ppermute(block, ('dp', 'seq'), perm)]
    ppermute x67 -> x69, waiting for transfers between devices: 193 us -> 162 us  [xor_send(): return lax.ppermute(value, axis, [(i, i ^ offset) for i in range(count)])]
    ppermute x67 -> x69, starting transfers between devices: 56.9 us -> 71.9 us  [xor_send(): return lax.ppermute(value, axis, [(i, i ^ offset) for i in range(count)])]
    reduce_scatter x1 -> x2, waiting for transfers between devices: 0.01 us -> 11.4 us  [the longest x1 11.4 us: local(): lax.psum_scatter(grad_out, 'seq', scatter_dimension=0, tiled=False)]
    slice x4 -> x2, local copies, waits for them, and re-layouts: 10.4 us -> 0.13 us  [the longest x1 0.1 us: tiles_of(): grad_second_rows[:, at:at + tile]]
    unnamed x168 -> x171, local copies, waits for them, and re-layouts: 39.7 us -> 37 us
  transfers between devices with their start and end apart: 85 -> 88, of which waited for: 32 -> 33; matrix products, arithmetic and copies ran while one was open for 21% -> 22% of each run, Pallas kernels for 20% -> 24%
where the time goes in v3:
time: 750 us; the launch traced here: 737 us
  waiting for transfers between devices  205 us (27%)
  Pallas kernels  182 us (24%)
  starting transfers between devices  102 us (14%)
  local copies, waits for them, and re-layouts  91.6 us (12%)
  other arithmetic  53.4 us (7%)
  matrix products  45 us (6%)
  blocking collectives  41.4 us (6%)
  between operations  16.1 us (2%)
    ppermute x69, waiting for transfers between devices, xor_send(): return lax.ppermute(value, axis, [(i, i ^ offset) for i in range(count)])  162 us
    ppermute x69, starting transfers between devices, xor_send(): return lax.ppermute(value, axis, [(i, i ^ offset) for i in range(count)])  71.9 us
    pallas_call x6, Pallas kernels, mm_weight(): pl.pallas_call(weight_kernel, out_shape=jax.ShapeDtypeStruct((rows, cols)...  52.6 us
    all_to_all x2, blocking collectives, spread(): return lax.all_to_all(joined, 'dp', split_axis=0, concat_axis=0, tiled=True)  41.4 us
    unnamed x171, local copies, waits for them, and re-layouts  37 us
    dot_general x4, matrix products, mm(): return jnp.dot(left, right, preferred_element_type=F32)  26.9 us
    pallas_call x2, Pallas kernels, mlp_forward(): pl.pallas_call(mlp_forward_kernel, out_shape=(jax.ShapeDtypeStruct((rows,...  23.6 us
    dot_general x2, matrix products, mm_back(): lax.dot_general(grad_rows, weight, (((1,), (1,)), ((), ())), preferred_el...  18.1 us
  transfers between devices with their start and end apart: 88, of which 33 were waited for; matrix products, arithmetic and copies ran while one was open for 22% of the time, Pallas kernels for 24%

profile of v3, /device:TPU:3, one launch (start us, length us, event | category | flops | bytes accessed | tf_op | source)
XLA Modules:
  0.0 737.5 jit_solution(3826236424421257419)
XLA Ops:
  11.6 15.5 %all_to_all.10 = bf16[8,64,768]{2,1,0:T(8,128)(2,1)} all-to-all(bf16[8,64,768]{2,1,0:T(8,128)(2,1)S(1)} %copy.117), channel_id=1, replica_groups=mesh['dp'=8,'seq'=4] {'dp'}, dimensions={0} | all-to-all | bytes 1572864 | tf_op jit(solution)/shard_map/all_to_all | solution.py:831
  37.0 16.5 %collective-permute-done.1 = bf16[256,2048]{1,0:T(8,128)(2,1)S(1)} collective-permute-done((bf16[256,2048]{1,0:T(8,128)(2,1)}, bf16[256,2048]{1,0:T(8,128)(2,1)S(1)}, u32[]{:S(2)}, u32[]{:S(2)}) %collective-permute-start.1) | collective-permute-done | bytes 1048608 | tf_op jit(solution)/shard_map/ppermute | solution.py:23
  80.4 25.9 %all_to_all.11 = bf16[8,64,1536]{2,1,0:T(8,128)(2,1)S(1)} all-to-all(bf16[8,64,1536]{2,1,0:T(8,128)(2,1)S(1)} %copy.116), channel_id=1, replica_groups=mesh['dp'=8,'seq'=4] {'dp'}, dimensions={0} | all-to-all | bytes 3145728 | tf_op jit(solution)/shard_map/all_to_all | solution.py:831
  124.6 9.0 %fusion.1 = f32[1024,1536]{1,0:T(8,128)S(1)} fusion(bf16[1024,2048]{1,0:T(8,128)(2,1)S(1)} %copy-done.41, bf16[2048,768]{1,0:T(8,128)(2,1)} %collective-permute-done.6, bf16[2048,768]{1,0:T(8,128)(2,1)} %bitcast.8), kind=kOutput, calls=%fused_computation.4 | convolution fusion | flops 6455033856 | bytes 16777216 | tf_op jit(solution)/shard_map/dot_general | solution.py:797
  133.7 13.0 %collective-permute-done.5 = bf16[256,2048]{1,0:T(8,128)(2,1)S(1)} collective-permute-done((bf16[256,2048]{1,0:T(8,128)(2,1)S(1)}, bf16[256,2048]{1,0:T(8,128)(2,1)S(1)}, u32[]{:S(2)}, u32[]{:S(2)}) %collective-permute-start.5) | collective-permute-done | bytes 1048608 | tf_op jit(solution)/shard_map/ppermute | solution.py:23
  151.0 13.2 %gates_forward.1 = (f32[256,8,384]{2,1,0:T(8,128)S(1)}, f32[256,8,384]{2,1,0:T(8,128)}, f32[256,8,384]{2,1,0:T(8,128)}, f32[256,8,384]{2,1,0:T(8,128)}, f32[256,...) custom-call(f32[4,256,1536]{2,1,0:T(8,128)} %bitcast.249, ...), custom_call_target="tpu_custom_call" | custom-call | flops 786432 | bytes 45613056 | tf_op jit(solution)/shard_map/gates_forward/pallas_call | solution.py:463
  181.3 8.3 %mix_forward.1 = (bf16[4,256,768]{2,1,0:T(8,128)(2,1)S(1)}, f32[256,8,384]{2,1,0:T(8,128)S(1)}, f32[8,256,384]{2,1,0:T(8,128)}) custom-call(f32[256,8,384]{2,1,0:T(8,128)} %get-tuple-element.136.loc_ref, f32[256,8,384]{2,1,0:T(8,128)} %get-tuple-element.137.run_ref, f32[8,384]{1,0:T(8,128)S(1)} %fusion.61.carry_ref, f32[4,256,1536]{2,1,0:T(8,128)} %bitcast.251, ...), custom_call_target="tpu_custom_call" | custom-call | flops 786432 | bytes 28311552 | tf_op jit(solution)/shard_map/mix_forward/pallas_call | solution.py:487
  189.6 7.2 convolution_convert_fusion
  201.9 9.0 %collective-permute-done.16 = bf16[128,2048]{1,0:T(8,128)(2,1)S(1)} collective-permute-done((bf16[128,2048]{1,0:T(8,128)(2,1)S(1)}, bf16[128,2048]{1,0:T(8,128)(2,1)S(1)}, u32[]{:S(2)}, u32[]{:S(2)}) %collective-permute-start.16) | collective-permute-done | bytes 524320 | tf_op jit(solution)/shard_map/ppermute | solution.py:23
  213.8 8.1 %collective-permute-done.14 = bf16[128,2048]{1,0:T(8,128)(2,1)S(1)} collective-permute-done((bf16[128,2048]{1,0:T(8,128)(2,1)S(1)}, bf16[128,2048]{1,0:T(8,128)(2,1)S(1)}, u32[]{:S(2)}, u32[]{:S(2)}) %collective-permute-start.14) | collective-permute-done | bytes 524320 | tf_op jit(solution)/shard_map/ppermute | solution.py:23
  222.1 11.2 %collective-permute-done.17 = bf16[128,2048]{1,0:T(8,128)(2,1)S(1)} collective-permute-done((bf16[128,2048]{1,0:T(8,128)(2,1)S(1)}, bf16[128,2048]{1,0:T(8,128)(2,1)S(1)}, u32[]{:S(2)}, u32[]{:S(2)}) %collective-permute-start.17) | collective-permute-done | bytes 524320 | tf_op jit(solution)/shard_map/ppermute | solution.py:23
  238.2 20.0 %collective-permute-done.21 = bf16[256,2048]{1,0:T(8,128)(2,1)S(1)} collective-permute-done((bf16[256,2048]{1,0:T(8,128)(2,1)S(1)}, bf16[256,2048]{1,0:T(8,128)(2,1)S(1)}, u32[]{:S(2)}, u32[]{:S(2)}) %collective-permute-start.21) | collective-permute-done | bytes 1048608 | tf_op jit(solution)/shard_map/ppermute | solution.py:23
  294.1 11.8 %mlp_forward.2 = (bf16[1024,768]{1,0:T(8,128)(2,1)S(1)}, bf16[1024,1536]{1,0:T(8,128)(2,1)S(1)}) custom-call(bf16[1024,2048]{1,0:T(8,128)(2,1)} %constant_dynamic-update-slice_fusion.10.x_ref.left_ref, bf16[4,8,64,1536]{3,2,1,0:T(8,128)(2,1)} %copy-done.75), custom_call_target="tpu_custom_call" | custom-call | flops 11274289152 | bytes 2097152 | tf_op jit(solution)/shard_map/mlp_forward/pallas_call | solution.py:587
  307.5 7.6 %weight_gradient.6 = bf16[768,2048]{1,0:T(8,128)(2,1)} custom-call(bf16[1024,768]{1,0:T(8,128)(2,1)S(1)} %get-tuple-element.172.left_ref, bf16[1024,2048]{1,0:T(8,128)(2,1)} %constant_dynamic-update-slice_fusion.5.right_ref.g_ref), custom_call_target="tpu_custom_call" | custom-call | flops 4831838208 | bytes 1572864 | tf_op jit(solution)/shard_map/weight_gradient/pallas_call | solution.py:741
  315.5 11.8 %mlp_forward.3 = (bf16[1024,768]{1,0:T(8,128)(2,1)S(1)}, bf16[1024,1536]{1,0:T(8,128)(2,1)S(1)}) custom-call(bf16[1024,2048]{1,0:T(8,128)(2,1)} %constant_dynamic-update-slice_fusion.10.x_ref.left_ref, bf16[4,8,64,1536]{3,2,1,0:T(8,128)(2,1)} %copy-done.42), custom_call_target="tpu_custom_call" | custom-call | flops 11274289152 | bytes 2097152 | tf_op jit(solution)/shard_map/mlp_forward/pallas_call | solution.py:587
  329.1 14.5 %hidden_backward.1 = (bf16[1024,1536]{1,0:T(8,128)(2,1)S(1)}, bf16[1024,1536]{1,0:T(8,128)(2,1)}) custom-call(bf16[1024,2048]{1,0:T(8,128)(2,1)} %constant_dynamic-update-slice_fusion.5.right_ref.g_ref, bf16[768,2048]{1,0:T(8,128)(2,1)} %copy-done.5, bf16[768,2048]{1,0:T(8,128)(2,1)} %collective-permute-done.25.down1_ref, bf16[1024,1536]{1,0:T(8,128)(2,1)} %copy-done.24, ...), custom_call_target="tpu_custom_call" | custom-call | flops 11274289152 | bytes 2097152 | tf_op jit(solution)/shard_map/hidden_backward/pallas_call | solution.py:645
  345.5 11.1 %weight_gradient.7 = bf16[2048,1536]{1,0:T(8,128)(2,1)} custom-call(bf16[1024,2048]{1,0:T(8,128)(2,1)} %constant_dynamic-update-slice_fusion.10.x_ref.left_ref, bf16[1024,1536]{1,0:T(8,128)(2,1)S(1)} %copy-done.22), custom_call_target="tpu_custom_call" | custom-call | flops 9663676416 | bytes 3145728 | tf_op jit(solution)/shard_map/weight_gradient/pallas_call | solution.py:741
  356.6 8.8 %weight_rows.2 = bf16[4,768,512]{2,1,0:T(8,128)(2,1)} custom-call(s32[1]{0:T(128)} %bitcast.39.shift_ref, bf16[1024,768]{1,0:T(8,128)(2,1)S(1)} %get-tuple-element.171.left_ref, bf16[1024,2048]{1,0:T(8,128)(2,1)} %constant_dynamic-update-slice_fusion.5.right_ref.g_ref, bf16[768,2048]{1,0:T(8,128)(2,1)} %collective-permute-done.26.added_ref), custom_call_target="tpu_custom_call" | custom-call | flops 4831838208 | bytes 1572864 | tf_op jit(solution)/shard_map/weight_rows/pallas_call | solution.py:773
  365.6 18.0 %normed_backward.1 = bf16[1024,2048]{1,0:T(8,128)(2,1)} custom-call(bf16[1024,1536]{1,0:T(8,128)(2,1)S(1)} %get-tuple-element.167.ffn0_ref.right_ref, bf16[1024,1536]{1,0:T(8,128)(2,1)} %get-tuple-element.157.right_ref.ffn1_ref, bf16[4,8,64,1536]{3,2,1,0:T(8,128)(2,1)} %copy-done.42, bf16[4,8,64,1536]{3,2,1,0:T(8,128)(2,1)} %copy-done.75), custom_call_target="tpu_custom_call" | custom-call | flops 22548578304 | bytes 1572864 | tf_op jit(solution)/shard_map/normed_backward/pallas_call | solution.py:687
  391.0 20.1 %collective-permute-done.29 = bf16[128,2048]{1,0:T(8,128)(2,1)S(1)} collective-permute-done((bf16[128,2048]{1,0:T(8,128)(2,1)S(1)}, bf16[128,2048]{1,0:T(8,128)(2,1)S(1)}, u32[]{:S(2)}, u32[]{:S(2)}) %collective-permute-start.29) | collective-permute-done | bytes 524320 | tf_op jit(solution)/shard_map/ppermute | solution.py:23
  414.9 12.4 %weight_gradient.8 = bf16[2048,1536]{1,0:T(8,128)(2,1)} custom-call(bf16[1024,2048]{1,0:T(8,128)(2,1)} %constant_dynamic-update-slice_fusion.10.x_ref.left_ref, bf16[1024,1536]{1,0:T(8,128)(2,1)S(1)} %get-tuple-element.167.ffn0_ref.right_ref, bf16[2048,1536]{1,0:T(8,128)(2,1)} %collective-permute-done.30.refs_0_), custom_call_target="tpu_custom_call" | custom-call | flops 9663676416 | bytes 3145728 | tf_op jit(solution)/shard_map/weight_gradient/pallas_call | solution.py:741
  444.3 7.2 add_convert_fusion
  451.5 11.1 %collective-permute-done.35 = bf16[256,2048]{1,0:T(8,128)(2,1)S(1)} collective-permute-done((bf16[256,2048]{1,0:T(8,128)(2,1)}, bf16[256,2048]{1,0:T(8,128)(2,1)S(1)}, u32[]{:S(2)}, u32[]{:S(2)}) %collective-permute-start.35) | collective-permute-done | bytes 1048608 | tf_op jit(solution)/shard_map/ppermute | solution.py:23
  479.2 7.0 fusion.18
  486.2 9.6 %mix_backward.1 = (bf16[4,256,768]{2,1,0:T(8,128)(2,1)S(1)}, f32[256,8,384]{2,1,0:T(8,128)S(1)}, f32[256,8,384]{2,1,0:T(8,128)}, f32[2,8,384]{2,1,0:T(8,128)S(1)}) custom-call(f32[4,256,768]{2,1,0:T(8,128)} %bitcast.261, f32[4,256,768]{2,1,0:T(8,128)} %bitcast.262, f32[4,256,1536]{2,1,0:T(8,128)} %bitcast.253, f32[4,256,1536]{2,1,0:T(8,128)} %bitcast.254, ...), custom_call_target="tpu_custom_call" | custom-call | flops 786432 | bytes 34603008 | tf_op jit(solution)/shard_map/mix_backward/pallas_call | solution.py:508
  524.0 17.9 %gates_backward.1 = (bf16[4,256,768]{2,1,0:T(8,128)(2,1)S(1)}, f32[3,8,384]{2,1,0:T(8,128)S(1)}, f32[3,8,384]{2,1,0:T(8,128)S(1)}, f32[2,2,176,176]{3,2,1,0:T(8,...) custom-call(f32[256,8,384]{2,1,0:T(8,128)} %copy-done.4, ...), custom_call_target="tpu_custom_call" | custom-call | flops 786432 | bytes 59768832 | tf_op jit(solution)/shard_map/gates_backward/pallas_call | solution.py:531
  550.4 7.5 %weight_gradient.10 = bf16[2048,768]{1,0:T(8,128)(2,1)S(1)} custom-call(bf16[1024,2048]{1,0:T(8,128)(2,1)} %constant_dynamic-update-slice_fusion.left_ref, bf16[1024,768]{1,0:T(8,128)(2,1)S(1)} %pad_maximum_fusion.14.right_ref), custom_call_target="tpu_custom_call" | custom-call | flops 4831838208 | bytes 1572864 | tf_op jit(solution)/shard_map/weight_gradient/pallas_call | solution.py:741
  572.0 11.1 %fusion.2 = bf16[1024,2048]{1,0:T(8,128)(2,1)} fusion(bf16[1024,1536]{1,0:T(8,128)(2,1)S(1)} %pad_maximum_fusion.6, bf16[2048,768]{1,0:T(8,128)(2,1)} %collective-permute-done.6, bf16[2048,768]{1,0:T(8,128)(2,1)} %bitcast.8), kind=kOutput, calls=%fused_computation.5 | convolution fusion | flops 6457131008 | bytes 13631488 | tf_op jit(solution)/shard_map/dot_general | solution.py:801
  594.8 9.4 %weight_gradient.11 = bf16[2048,768]{1,0:T(8,128)(2,1)} custom-call(bf16[1024,2048]{1,0:T(8,128)(2,1)} %constant_dynamic-update-slice_fusion.left_ref, bf16[1024,768]{1,0:T(8,128)(2,1)S(1)} %slice.455.right_ref, bf16[2048,768]{1,0:T(8,128)(2,1)} %collective-permute-done.49.refs_0_), custom_call_target="tpu_custom_call" | custom-call | flops 4831838208 | bytes 1572864 | tf_op jit(solution)/shard_map/weight_gradient/pallas_call | solution.py:741
  612.9 11.4 %reduce-scatter.9.cloned.1.call-done = bf16[1,384,512]{2,1,0:T(8,128)(2,1)} async-done(((bf16[4,384,512]{2,1,0:T(8,128)(2,1)}), bf16[1,384,512]{2,1,0:T(8,128)(2,1)}) %reduce-scatter.9.cloned.1.call-update) | async-done | bytes 393232 | tf_op jit(solution)/shard_map/reduce_scatter | solution.py:988
  641.5 9.4 %collective-permute-done.66 = f32[2,2048]{1,0:T(2,128)S(1)} collective-permute-done((f32[2,2048]{1,0:T(2,128)S(1)}, f32[2,2048]{1,0:T(2,128)S(1)}, u32[]{:S(2)}, u32[]{:S(2)}) %collective-permute-start.66) | collective-permute-done | bytes 16416 | tf_op jit(solution)/shard_map/ppermute | solution.py:23
  710.0 13.7 %collective-permute-done.77 = bf16[352,512]{1,0:T(8,128)(2,1)S(1)} collective-permute-done((bf16[352,512]{1,0:T(8,128)(2,1)S(1)}, bf16[352,512]{1,0:T(8,128)(2,1)S(1)}, u32[]{:S(2)}, u32[]{:S(2)}) %collective-permute-start.77) | collective-permute-done | bytes 360480 | tf_op jit(solution)/shard_map/ppermute | solution.py:198
  (507 shorter events, 332.8 us)
Async XLA Ops:
  7.2 46.3 %all-gather.6.cloned.1.call-start = ((), (), s32[]{:S(2)}) async-start(), calls=%async_computation.6 | async-start | bytes 1802240 | tf_op jit(solution)/shard_map/all_gather | solution.py:839
  7.9 101.8 %all-gather.8.cloned.1.call-start = ((), (), s32[]{:S(2)}) async-start(), calls=%async_computation.11 | async-start | bytes 3932160 | tf_op jit(solution)/shard_map/all_gather | solution.py:842
  27.1 250.5 %all-gather.10.cloned.1.call-start = ((), (), s32[]{:S(2)}) async-start(), calls=%async_computation.12 | async-start | bytes 11796480 | tf_op jit(solution)/shard_map/all_gather | solution.py:885
  29.1 24.3 %collective-permute-start.1 = (bf16[256,2048]{1,0:T(8,128)(2,1)}, bf16[256,2048]{1,0:T(8,128)(2,1)S(1)}, u32[]{:S(2)}, u32[]{:S(2)}) collective-permute-start(bf16[256,2048]{1,0:T(8,128)(2,1)} %get-tuple-element.346), channel_id=1, source_target_pairs={{0,16},{4,20},{8,24},{12,28},{16,0},{20,4},{24,8},{28,12},{1,17},{... | collective-permute-start | bytes 3145736 | tf_op jit(solution)/shard_map/ppermute | solution.py:23
  29.3 24.2 %collective-permute-start = (bf16[256,2048]{1,0:T(8,128)(2,1)}, bf16[256,2048]{1,0:T(8,128)(2,1)S(1)}, u32[]{:S(2)}, u32[]{:S(2)}) collective-permute-start(bf16[256,2048]{1,0:T(8,128)(2,1)} %get-tuple-element.346), channel_id=1, source_target_pairs={{0,8},{4,12},{8,0},{12,4},{16,24},{20,28},{24,16},{28,20},{1,9},{5... | collective-permute-start | bytes 3145736 | tf_op jit(solution)/shard_map/ppermute | solution.py:23
  111.3 340.1 %reduce-scatter.5.cloned.1.call-start = ((), (), s32[]{:S(2)}) async-start(), calls=%async_computation.7 | async-start | bytes 3932160 | tf_op jit(solution)/shard_map/reduce_scatter | solution.py:920
  122.3 67.3 %collective-permute-start.11 = (bf16[384,2048]{1,0:T(8,128)(2,1)}, bf16[384,2048]{1,0:T(8,128)(2,1)}, u32[]{:S(2)}, u32[]{:S(2)}) collective-permute-start(bf16[384,2048]{1,0:T(8,128)(2,1)} %pad.81), channel_id=1, source_target_pairs={{0,4},{4,0},{8,12},{12,8},{16,20},{20,16},{24,28},{28,24},{1,5},{5... | collective-permute-start | bytes 4718600 | tf_op jit(solution)/shard_map/ppermute | solution.py:23
  122.3 24.3 %collective-permute-start.5 = (bf16[256,2048]{1,0:T(8,128)(2,1)S(1)}, bf16[256,2048]{1,0:T(8,128)(2,1)S(1)}, u32[]{:S(2)}, u32[]{:S(2)}) collective-permute-start(bf16[256,2048]{1,0:T(8,128)(2,1)S(1)} %bitcast.263), channel_id=1, source_target_pairs={{0,16},{4,20},{8,24},{12,28},{16,0},{20,4},{24,8},{28,12},{1,17},{... | collective-permute-start | bytes 3145736 | tf_op jit(solution)/shard_map/ppermute | solution.py:23
  123.5 24.0 %collective-permute-start.4 = (bf16[256,2048]{1,0:T(8,128)(2,1)S(1)}, bf16[256,2048]{1,0:T(8,128)(2,1)S(1)}, u32[]{:S(2)}, u32[]{:S(2)}) collective-permute-start(bf16[256,2048]{1,0:T(8,128)(2,1)S(1)} %bitcast.264), channel_id=1, source_target_pairs={{0,8},{4,12},{8,0},{12,4},{16,24},{20,28},{24,16},{28,20},{1,9},{5... | collective-permute-start | bytes 3145736 | tf_op jit(solution)/shard_map/ppermute | solution.py:23
  236.0 22.3 %collective-permute-start.21 = (bf16[256,2048]{1,0:T(8,128)(2,1)S(1)}, bf16[256,2048]{1,0:T(8,128)(2,1)S(1)}, u32[]{:S(2)}, u32[]{:S(2)}) collective-permute-start(bf16[256,2048]{1,0:T(8,128)(2,1)S(1)} %get-tuple-element.344), channel_id=1, source_target_pairs={{0,16},{4,20},{8,24},{12,28},{16,0},{20,4},{24,8},{28,12},{1,17},{... | collective-permute-start | bytes 3145736 | tf_op jit(solution)/shard_map/ppermute | solution.py:23
  288.4 40.7 %collective-permute-start.25 = (bf16[768,2048]{1,0:T(8,128)(2,1)S(1)}, bf16[768,2048]{1,0:T(8,128)(2,1)}, u32[]{:S(2)}, u32[]{:S(2)}) collective-permute-start(bf16[768,2048]{1,0:T(8,128)(2,1)S(1)} %unpack_down.1.down0_ref), channel_id=1, source_target_pairs={{0,4},{4,0},{8,12},{12,8},{16,20},{20,16},{24,28},{28,24},{1,5},{5... | collective-permute-start | bytes 9437192 | tf_op jit(solution)/shard_map/ppermute | solution.py:23
  315.2 41.4 %collective-permute-start.26 = (bf16[768,2048]{1,0:T(8,128)(2,1)}, bf16[768,2048]{1,0:T(8,128)(2,1)}, u32[]{:S(2)}, u32[]{:S(2)}) collective-permute-start(bf16[768,2048]{1,0:T(8,128)(2,1)} %weight_gradient.6), channel_id=1, source_target_pairs={{0,4},{4,0},{8,12},{12,8},{16,20},{20,16},{24,28},{28,24},{1,5},{5... | collective-permute-start | bytes 9437192 | tf_op jit(solution)/shard_map/ppermute | solution.py:23
  365.4 45.7 %collective-permute-start.30 = (bf16[2048,1536]{1,0:T(8,128)(2,1)}, bf16[2048,1536]{1,0:T(8,128)(2,1)}, u32[]{:S(2)}, u32[]{:S(2)}) collective-permute-start(bf16[2048,1536]{1,0:T(8,128)(2,1)} %weight_gradient.7), channel_id=1, source_target_pairs={{0,4},{4,0},{8,12},{12,8},{16,20},{20,16},{24,28},{28,24},{1,5},{5... | collective-permute-start | bytes 18874376 | tf_op jit(solution)/shard_map/ppermute | solution.py:23
  365.6 201.6 %reduce-scatter.7.cloned.1.call-start = ((), (), s32[]{:S(2)}) async-start(), calls=%async_computation.8 | async-start | bytes 7864320 | tf_op jit(solution)/shard_map/reduce_scatter | solution.py:929
  386.5 40.7 %collective-permute-start.27 = (bf16[128,2048]{1,0:T(8,128)(2,1)}, bf16[128,2048]{1,0:T(8,128)(2,1)}, u32[]{:S(2)}, u32[]{:S(2)}) collective-permute-start(bf16[128,2048]{1,0:T(8,128)(2,1)} %get-tuple-element.361), channel_id=1, source_target_pairs={{0,8},{4,12},{8,0},{12,4},{16,24},{20,28},{24,16},{28,20},{1,9},{5... | collective-permute-start | bytes 1572872 | tf_op jit(solution)/shard_map/ppermute | solution.py:23
  386.8 40.4 %collective-permute-start.33 = (bf16[128,2048]{1,0:T(8,128)(2,1)}, bf16[128,2048]{1,0:T(8,128)(2,1)}, u32[]{:S(2)}, u32[]{:S(2)}) collective-permute-start(bf16[128,2048]{1,0:T(8,128)(2,1)} %get-tuple-element.362), channel_id=1, source_target_pairs={{0,16},{4,20},{8,24},{12,28},{16,0},{20,4},{24,8},{28,12},{1,17},{... | collective-permute-start | bytes 1572872 | tf_op jit(solution)/shard_map/ppermute | solution.py:23
  387.9 23.2 %collective-permute-start.29 = (bf16[128,2048]{1,0:T(8,128)(2,1)S(1)}, bf16[128,2048]{1,0:T(8,128)(2,1)S(1)}, u32[]{:S(2)}, u32[]{:S(2)}) collective-permute-start(bf16[128,2048]{1,0:T(8,128)(2,1)S(1)} %get-tuple-element.363), channel_id=1, source_target_pairs={{0,16},{4,20},{8,24},{12,28},{16,0},{20,4},{24,8},{28,12},{1,17},{... | collective-permute-start | bytes 1572872 | tf_op jit(solution)/shard_map/ppermute | solution.py:23
  388.3 22.9 %collective-permute-start.28 = (bf16[128,2048]{1,0:T(8,128)(2,1)S(1)}, bf16[128,2048]{1,0:T(8,128)(2,1)S(1)}, u32[]{:S(2)}, u32[]{:S(2)}) collective-permute-start(bf16[128,2048]{1,0:T(8,128)(2,1)S(1)} %get-tuple-element.364), channel_id=1, source_target_pairs={{0,8},{4,12},{8,0},{12,4},{16,24},{20,28},{24,16},{28,20},{1,9},{5... | collective-permute-start | bytes 1572872 | tf_op jit(solution)/shard_map/ppermute | solution.py:23
  431.4 193.0 %reduce-scatter.9.cloned.1.call-start = ((), (), s32[]{:S(2)}) async-start(), calls=%async_computation.9 | async-start | bytes 1966080 | tf_op jit(solution)/shard_map/reduce_scatter | solution.py:988
  439.6 23.0 %collective-permute-start.35 = (bf16[256,2048]{1,0:T(8,128)(2,1)}, bf16[256,2048]{1,0:T(8,128)(2,1)S(1)}, u32[]{:S(2)}, u32[]{:S(2)}) collective-permute-start(bf16[256,2048]{1,0:T(8,128)(2,1)} %fusion.74), channel_id=1, source_target_pairs={{0,16},{4,20},{8,24},{12,28},{16,0},{20,4},{24,8},{28,12},{1,17},{... | collective-permute-start | bytes 3145736 | tf_op jit(solution)/shard_map/ppermute | solution.py:23
  439.9 22.7 %collective-permute-start.34 = (bf16[256,2048]{1,0:T(8,128)(2,1)}, bf16[256,2048]{1,0:T(8,128)(2,1)}, u32[]{:S(2)}, u32[]{:S(2)}) collective-permute-start(bf16[256,2048]{1,0:T(8,128)(2,1)} %fusion.74), channel_id=1, source_target_pairs={{0,8},{4,12},{8,0},{12,4},{16,24},{20,28},{24,16},{28,20},{1,9},{5... | collective-permute-start | bytes 3145736 | tf_op jit(solution)/shard_map/ppermute | solution.py:23
  476.9 32.0 %collective-permute-start.43 = (bf16[128,2048]{1,0:T(8,128)(2,1)S(1)}, bf16[128,2048]{1,0:T(8,128)(2,1)S(1)}, u32[]{:S(2)}, u32[]{:S(2)}) collective-permute-start(bf16[128,2048]{1,0:T(8,128)(2,1)S(1)} %get-tuple-element.357), channel_id=1, source_target_pairs={{0,8},{4,12},{8,0},{12,4},{16,24},{20,28},{24,16},{28,20},{1,9},{5... | collective-permute-start | bytes 1572872 | tf_op jit(solution)/shard_map/ppermute | solution.py:23
  478.1 30.9 %collective-permute-start.42 = (bf16[128,2048]{1,0:T(8,128)(2,1)S(1)}, bf16[128,2048]{1,0:T(8,128)(2,1)S(1)}, u32[]{:S(2)}, u32[]{:S(2)}) collective-permute-start(bf16[128,2048]{1,0:T(8,128)(2,1)S(1)} %get-tuple-element.358), channel_id=1, source_target_pairs={{0,16},{4,20},{8,24},{12,28},{16,0},{20,4},{24,8},{28,12},{1,17},{... | collective-permute-start | bytes 1572872 | tf_op jit(solution)/shard_map/ppermute | solution.py:23
  567.2 27.6 %collective-permute-start.49 = (bf16[2048,768]{1,0:T(8,128)(2,1)}, bf16[2048,768]{1,0:T(8,128)(2,1)}, u32[]{:S(2)}, u32[]{:S(2)}) collective-permute-start(bf16[2048,768]{1,0:T(8,128)(2,1)} %copy-done.17), channel_id=1, source_target_pairs={{0,4},{4,0},{8,12},{12,8},{16,20},{20,16},{24,28},{28,24},{1,5},{5... | collective-permute-start | bytes 9437192 | tf_op jit(solution)/shard_map/ppermute | solution.py:23
  589.2 105.0 %reduce-scatter.11.cloned.1.call-start = ((), (), s32[]{:S(2)}) async-start(), calls=%async_computation.10 | async-start | bytes 3932160 | tf_op jit(solution)/shard_map/reduce_scatter | solution.py:1008
  610.8 40.5 %collective-permute-start.38 = (bf16[128,2048]{1,0:T(8,128)(2,1)}, bf16[128,2048]{1,0:T(8,128)(2,1)S(1)}, u32[]{:S(2)}, u32[]{:S(2)}) collective-permute-start(bf16[128,2048]{1,0:T(8,128)(2,1)} %get-tuple-element.355), channel_id=1, source_target_pairs={{0,8},{4,12},{8,0},{12,4},{16,24},{20,28},{24,16},{28,20},{1,9},{5... | collective-permute-start | bytes 1572872 | tf_op jit(solution)/shard_map/ppermute | solution.py:23
  611.7 40.5 %collective-permute-start.57 = (bf16[128,2048]{1,0:T(8,128)(2,1)}, bf16[128,2048]{1,0:T(8,128)(2,1)}, u32[]{:S(2)}, u32[]{:S(2)}) collective-permute-start(bf16[128,2048]{1,0:T(8,128)(2,1)} %get-tuple-element.356), channel_id=1, source_target_pairs={{0,16},{4,20},{8,24},{12,28},{16,0},{20,4},{24,8},{28,12},{1,17},{... | collective-permute-start | bytes 1572872 | tf_op jit(solution)/shard_map/ppermute | solution.py:23
  637.2 27.1 %collective-permute-start.59 = (bf16[128,2048]{1,0:T(8,128)(2,1)S(1)}, bf16[128,2048]{1,0:T(8,128)(2,1)S(1)}, u32[]{:S(2)}, u32[]{:S(2)}) collective-permute-start(bf16[128,2048]{1,0:T(8,128)(2,1)S(1)} %copy-done.57), channel_id=1, source_target_pairs={{0,8},{4,12},{8,0},{12,4},{16,24},{20,28},{24,16},{28,20},{1,9},{5... | collective-permute-start | bytes 1572872 | tf_op jit(solution)/shard_map/ppermute | solution.py:23
  637.6 26.7 %collective-permute-start.62 = (bf16[128,2048]{1,0:T(8,128)(2,1)S(1)}, bf16[128,2048]{1,0:T(8,128)(2,1)S(1)}, u32[]{:S(2)}, u32[]{:S(2)}) collective-permute-start(bf16[128,2048]{1,0:T(8,128)(2,1)S(1)} %copy-done.56), channel_id=1, source_target_pairs={{0,16},{4,20},{8,24},{12,28},{16,0},{20,4},{24,8},{28,12},{1,17},{... | collective-permute-start | bytes 1572872 | tf_op jit(solution)/shard_map/ppermute | solution.py:23
  661.3 30.5 %collective-permute-start.58 = (bf16[352,512]{1,0:T(8,128)(2,1)S(1)}, bf16[352,512]{1,0:T(8,128)(2,1)S(1)}, u32[]{:S(2)}, u32[]{:S(2)}) collective-permute-start(bf16[352,512]{1,0:T(8,128)(2,1)S(1)} %slice.462), channel_id=1, source_target_pairs={{0,0},{1,9},{2,18},{3,27},{4,28},{5,21},{6,14},{7,7},{8,8},{9,1},{... | collective-permute-start | bytes 1081352 | tf_op jit(solution)/shard_map/ppermute | solution.py:188
  694.2 30.8 %collective-permute-start.79 = (bf16[768,512]{1,0:T(8,128)(2,1)}, bf16[768,512]{1,0:T(8,128)(2,1)S(1)}, u32[]{:S(2)}, u32[]{:S(2)}) collective-permute-start(bf16[768,512]{1,0:T(8,128)(2,1)} %collective-permute-done.54), channel_id=1, source_target_pairs={{0,0},{1,1},{2,2},{3,3},{4,7},{5,6},{6,5},{7,4},{8,9},{9,8},{10,11... | collective-permute-start | bytes 2359304 | tf_op jit(solution)/shard_map/ppermute | solution.py:198
  701.5 22.3 %collective-permute-start.77 = (bf16[352,512]{1,0:T(8,128)(2,1)S(1)}, bf16[352,512]{1,0:T(8,128)(2,1)S(1)}, u32[]{:S(2)}, u32[]{:S(2)}) collective-permute-start(bf16[352,512]{1,0:T(8,128)(2,1)S(1)} %collective-permute-done.58), channel_id=1, source_target_pairs={{0,0},{1,1},{2,2},{3,3},{4,7},{5,6},{6,5},{7,4},{8,9},{9,8},{10,11... | collective-permute-start | bytes 1081352 | tf_op jit(solution)/shard_map/ppermute | solution.py:198
  (132 other events, 1229.0 us)
Sparse Core Ops, SparseCore 0:
  9.6 35.4 all-gather.5
  46.6 63.0 all-gather.7
  111.9 165.6 all-gather.9
  365.7 60.8 reduce-scatter.4
  431.5 114.4 reduce-scatter.6
  589.3 34.9 reduce-scatter.8
  634.6 59.5 reduce-scatter.10

commit v4 on v3

--- a/solution.py
+++ b/solution.py
@@ -697,28 +697,30 @@
 
 
 def unpack_down_kernel(packed_ref, out_ref):
-    out_ref[...] = jnp.concatenate(
-        [packed_ref[0, block] for block in range(packed_ref.shape[1])], axis=1
-    )
+    _, blocks, shard, lanes = packed_ref.shape
+    part = out_ref.shape[1] // blocks
+    for k in range(lanes // part):
+        cols = slice(k * part, (k + 1) * part)
+        for block in range(blocks):
+            out_ref[k * shard : (k + 1) * shard, block * part : (block + 1) * part] = packed_ref[
+                0, block, :, cols
+            ]
 
 
 def unpack_down(packed, first_column, rows):
     seq_count, dp_count, shard, _ = packed.shape
     lay = rows // (seq_count * shard)
-    part = (packed.shape[3] - first_column) // lay
-    begin = first_column // part
+    lanes = packed.shape[3] - first_column
+    begin = first_column // lanes
+    cols = dp_count * lanes // lay
     return pl.pallas_call(
         unpack_down_kernel,
-        out_shape=jax.ShapeDtypeStruct((rows, dp_count * part), packed.dtype),
-        grid=(seq_count, lay),
-        in_specs=[
-            pl.BlockSpec((1, dp_count, shard, part), lambda s, k: (s, 0, 0, begin + k))
-        ],
-        out_specs=pl.BlockSpec((shard, dp_count * part), lambda s, k: (s * lay + k, 0)),
-        compiler_params=pltpu.CompilerParams(
-            dimension_semantics=("arbitrary", "arbitrary"), vmem_limit_bytes=VMEM_LIMIT
-        ),
-        cost_estimate=cost(0, 2 * rows * dp_count * part * 2, 0),
+        out_shape=jax.ShapeDtypeStruct((rows, cols), packed.dtype),
+        grid=(seq_count,),
+        in_specs=[pl.BlockSpec((1, dp_count, shard, lanes), lambda s: (s, 0, 0, begin))],
+        out_specs=pl.BlockSpec((lay * shard, cols), lambda s: (s, 0)),
+        compiler_params=params(),
+        cost_estimate=cost(0, 4 * rows * cols, 0),
         name="unpack_down",
     )(packed)
 
@@ -989,10 +991,11 @@
     grad_first_w = mm_weight(normed_all, grad_first[:, : 2 * width], moved)
     sums = sums[0] + xor_send(sums[1], "dp", 1)
     partial, grad_first_w = tie(partial, grad_first_w)
-    grad_normed, sums, out_cols, normed_all, down_cols, *hops = scatter_tokens(
+    grad_normed, sums, normed_all, down_cols, *hops = scatter_tokens(
         partial.reshape(chips, length, model),
-        sum_over(sums, "seq", 1, 2), out_cols, normed_all, down_cols, *hops,
-    )
+        sum_over(sums, "seq", 1, 2), normed_all, down_cols, *hops,
+    )
+    grad_first_w, out_cols = tie(grad_first_w, out_cols)
     out_cols = move_in_plane(out_cols[:own])
     norm_gain_term = jnp.sum(partial.astype(F32) * normed_all.astype(F32), axis=0) / norm_gain
     grad_normed, sums, blocks = tie(grad_normed, sum_over(sums, "seq", 2), blocks)

time: 750 us -> 746 us (level)
    ppermute x69, waiting for transfers between devices: 162 us -> 177 us  [xor_send(): return lax.ppermute(value, axis, [(i, i ^ offset) for i in range(count)])]
    reduce_scatter x1, waiting for transfers between devices: 11.4 us -> 0.01 us  [local(): lax.psum_scatter(grad_out, 'seq', scatter_dimension=0, tiled=False)]
    unnamed x171 -> x175, local copies, waits for them, and re-layouts: 37 us -> 37 us
  transfers between devices with their start and end apart: 88 -> 88, of which waited for: 33 -> 32; matrix products, arithmetic and copies ran while one was open for 22% -> 22% of each run, Pallas kernels for 24% -> 23%
where the time goes in v4:
time: 746 us; the launch traced here: 734 us
  waiting for transfers between devices  208 us (28%)
  Pallas kernels  180 us (24%)
  starting transfers between devices  102 us (14%)
  local copies, waits for them, and re-layouts  91.6 us (12%)
  other arithmetic  50.1 us (7%)
  matrix products  45 us (6%)
  blocking collectives  41.4 us (6%)
  between operations  16.1 us (2%)
    ppermute x69, waiting for transfers between devices, xor_send(): return lax.ppermute(value, axis, [(i, i ^ offset) for i in range(count)])  177 us
    ppermute x69, starting transfers between devices, xor_send(): return lax.ppermute(value, axis, [(i, i ^ offset) for i in range(count)])  71.4 us
    pallas_call x6, Pallas kernels, mm_weight(): pl.pallas_call(weight_kernel, out_shape=jax.ShapeDtypeStruct((rows, cols)...  52.6 us
    all_to_all x2, blocking collectives, spread(): return lax.all_to_all(joined, 'dp', split_axis=0, concat_axis=0, tiled=True)  41.4 us
    unnamed x175, local copies, waits for them, and re-layouts  37 us
    dot_general x4, matrix products, mm(): return jnp.dot(left, right, preferred_element_type=F32)  26.9 us
    pallas_call x2, Pallas kernels, mlp_forward(): pl.pallas_call(mlp_forward_kernel, out_shape=(jax.ShapeDtypeStruct((rows,...  23.6 us
    dot_general x2, matrix products, mm_back(): lax.dot_general(grad_rows, weight, (((1,), (1,)), ((), ())), preferred_el...  18.1 us
  transfers between devices with their start and end apart: 88, of which 32 were waited for; matrix products, arithmetic and copies ran while one was open for 22% of the time, Pallas kernels for 23%

profile of v4, /device:TPU:3, one launch (start us, length us, event | category | flops | bytes accessed | tf_op | source)
XLA Modules:
  0.0 733.8 jit_solution(16541493493335193618)
XLA Ops:
  11.6 15.5 %all_to_all.10 = bf16[8,64,768]{2,1,0:T(8,128)(2,1)} all-to-all(bf16[8,64,768]{2,1,0:T(8,128)(2,1)S(1)} %copy.117), channel_id=1, replica_groups=mesh['dp'=8,'seq'=4] {'dp'}, dimensions={0} | all-to-all | bytes 1572864 | tf_op jit(solution)/shard_map/all_to_all | solution.py:833
  37.0 16.5 %collective-permute-done.1 = bf16[256,2048]{1,0:T(8,128)(2,1)S(1)} collective-permute-done((bf16[256,2048]{1,0:T(8,128)(2,1)}, bf16[256,2048]{1,0:T(8,128)(2,1)S(1)}, u32[]{:S(2)}, u32[]{:S(2)}) %collective-permute-start.1) | collective-permute-done | bytes 1048608 | tf_op jit(solution)/shard_map/ppermute | solution.py:23
  80.4 25.9 %all_to_all.11 = bf16[8,64,1536]{2,1,0:T(8,128)(2,1)S(1)} all-to-all(bf16[8,64,1536]{2,1,0:T(8,128)(2,1)S(1)} %copy.116), channel_id=1, replica_groups=mesh['dp'=8,'seq'=4] {'dp'}, dimensions={0} | all-to-all | bytes 3145728 | tf_op jit(solution)/shard_map/all_to_all | solution.py:833
  124.6 9.0 %fusion.1 = f32[1024,1536]{1,0:T(8,128)S(1)} fusion(bf16[1024,2048]{1,0:T(8,128)(2,1)S(1)} %copy-done.42, bf16[2048,768]{1,0:T(8,128)(2,1)} %collective-permute-done.6, bf16[2048,768]{1,0:T(8,128)(2,1)} %bitcast.8), kind=kOutput, calls=%fused_computation.4 | convolution fusion | flops 6455033856 | bytes 16777216 | tf_op jit(solution)/shard_map/dot_general | solution.py:799
  133.7 13.0 %collective-permute-done.5 = bf16[256,2048]{1,0:T(8,128)(2,1)S(1)} collective-permute-done((bf16[256,2048]{1,0:T(8,128)(2,1)S(1)}, bf16[256,2048]{1,0:T(8,128)(2,1)S(1)}, u32[]{:S(2)}, u32[]{:S(2)}) %collective-permute-start.5) | collective-permute-done | bytes 1048608 | tf_op jit(solution)/shard_map/ppermute | solution.py:23
  151.0 13.2 %gates_forward.1 = (f32[256,8,384]{2,1,0:T(8,128)S(1)}, f32[256,8,384]{2,1,0:T(8,128)}, f32[256,8,384]{2,1,0:T(8,128)}, f32[256,8,384]{2,1,0:T(8,128)}, f32[256,...) custom-call(f32[4,256,1536]{2,1,0:T(8,128)} %bitcast.249, ...), custom_call_target="tpu_custom_call" | custom-call | flops 786432 | bytes 45613056 | tf_op jit(solution)/shard_map/gates_forward/pallas_call | solution.py:463
  181.3 8.2 %mix_forward.1 = (bf16[4,256,768]{2,1,0:T(8,128)(2,1)S(1)}, f32[256,8,384]{2,1,0:T(8,128)S(1)}, f32[8,256,384]{2,1,0:T(8,128)}) custom-call(f32[256,8,384]{2,1,0:T(8,128)} %get-tuple-element.137.loc_ref, f32[256,8,384]{2,1,0:T(8,128)} %get-tuple-element.138.run_ref, f32[8,384]{1,0:T(8,128)S(1)} %fusion.61.carry_ref, f32[4,256,1536]{2,1,0:T(8,128)} %bitcast.251, ...), custom_call_target="tpu_custom_call" | custom-call | flops 786432 | bytes 28311552 | tf_op jit(solution)/shard_map/mix_forward/pallas_call | solution.py:487
  189.5 7.2 convolution_convert_fusion
  201.7 9.0 %collective-permute-done.16 = bf16[128,2048]{1,0:T(8,128)(2,1)S(1)} collective-permute-done((bf16[128,2048]{1,0:T(8,128)(2,1)S(1)}, bf16[128,2048]{1,0:T(8,128)(2,1)S(1)}, u32[]{:S(2)}, u32[]{:S(2)}) %collective-permute-start.16) | collective-permute-done | bytes 524320 | tf_op jit(solution)/shard_map/ppermute | solution.py:23
  213.8 8.1 %collective-permute-done.14 = bf16[128,2048]{1,0:T(8,128)(2,1)S(1)} collective-permute-done((bf16[128,2048]{1,0:T(8,128)(2,1)S(1)}, bf16[128,2048]{1,0:T(8,128)(2,1)S(1)}, u32[]{:S(2)}, u32[]{:S(2)}) %collective-permute-start.14) | collective-permute-done | bytes 524320 | tf_op jit(solution)/shard_map/ppermute | solution.py:23
  222.0 11.2 %collective-permute-done.17 = bf16[128,2048]{1,0:T(8,128)(2,1)S(1)} collective-permute-done((bf16[128,2048]{1,0:T(8,128)(2,1)S(1)}, bf16[128,2048]{1,0:T(8,128)(2,1)S(1)}, u32[]{:S(2)}, u32[]{:S(2)}) %collective-permute-start.17) | collective-permute-done | bytes 524320 | tf_op jit(solution)/shard_map/ppermute | solution.py:23
  238.1 19.9 %collective-permute-done.21 = bf16[256,2048]{1,0:T(8,128)(2,1)S(1)} collective-permute-done((bf16[256,2048]{1,0:T(8,128)(2,1)S(1)}, bf16[256,2048]{1,0:T(8,128)(2,1)S(1)}, u32[]{:S(2)}, u32[]{:S(2)}) %collective-permute-start.21) | collective-permute-done | bytes 1048608 | tf_op jit(solution)/shard_map/ppermute | solution.py:23
  294.1 11.8 %mlp_forward.2 = (bf16[1024,768]{1,0:T(8,128)(2,1)S(1)}, bf16[1024,1536]{1,0:T(8,128)(2,1)S(1)}) custom-call(bf16[1024,2048]{1,0:T(8,128)(2,1)} %constant_dynamic-update-slice_fusion.10.x_ref.left_ref, bf16[4,8,64,1536]{3,2,1,0:T(8,128)(2,1)} %copy-done.77), custom_call_target="tpu_custom_call" | custom-call | flops 11274289152 | bytes 2097152 | tf_op jit(solution)/shard_map/mlp_forward/pallas_call | solution.py:587
  307.6 7.6 %weight_gradient.6 = bf16[768,2048]{1,0:T(8,128)(2,1)} custom-call(bf16[1024,768]{1,0:T(8,128)(2,1)S(1)} %get-tuple-element.173.left_ref, bf16[1024,2048]{1,0:T(8,128)(2,1)} %constant_dynamic-update-slice_fusion.5.right_ref.g_ref), custom_call_target="tpu_custom_call" | custom-call | flops 4831838208 | bytes 1572864 | tf_op jit(solution)/shard_map/weight_gradient/pallas_call | solution.py:743
  315.6 11.8 %mlp_forward.3 = (bf16[1024,768]{1,0:T(8,128)(2,1)S(1)}, bf16[1024,1536]{1,0:T(8,128)(2,1)S(1)}) custom-call(bf16[1024,2048]{1,0:T(8,128)(2,1)} %constant_dynamic-update-slice_fusion.10.x_ref.left_ref, bf16[4,8,64,1536]{3,2,1,0:T(8,128)(2,1)} %copy-done.44), custom_call_target="tpu_custom_call" | custom-call | flops 11274289152 | bytes 2097152 | tf_op jit(solution)/shard_map/mlp_forward/pallas_call | solution.py:587
  329.1 14.5 %hidden_backward.1 = (bf16[1024,1536]{1,0:T(8,128)(2,1)S(1)}, bf16[1024,1536]{1,0:T(8,128)(2,1)}) custom-call(bf16[1024,2048]{1,0:T(8,128)(2,1)} %constant_dynamic-update-slice_fusion.5.right_ref.g_ref, bf16[768,2048]{1,0:T(8,128)(2,1)} %copy-done.5, bf16[768,2048]{1,0:T(8,128)(2,1)} %collective-permute-done.25.down1_ref, bf16[1024,1536]{1,0:T(8,128)(2,1)} %copy-done.24, ...), custom_call_target="tpu_custom_call" | custom-call | flops 11274289152 | bytes 2097152 | tf_op jit(solution)/shard_map/hidden_backward/pallas_call | solution.py:645
  345.5 11.1 %weight_gradient.7 = bf16[2048,1536]{1,0:T(8,128)(2,1)} custom-call(bf16[1024,2048]{1,0:T(8,128)(2,1)} %constant_dynamic-update-slice_fusion.10.x_ref.left_ref, bf16[1024,1536]{1,0:T(8,128)(2,1)S(1)} %copy-done.22), custom_call_target="tpu_custom_call" | custom-call | flops 9663676416 | bytes 3145728 | tf_op jit(solution)/shard_map/weight_gradient/pallas_call | solution.py:743
  356.7 8.8 %weight_rows.2 = bf16[4,768,512]{2,1,0:T(8,128)(2,1)} custom-call(s32[1]{0:T(128)} %bitcast.39.shift_ref, bf16[1024,768]{1,0:T(8,128)(2,1)S(1)} %get-tuple-element.172.left_ref, bf16[1024,2048]{1,0:T(8,128)(2,1)} %constant_dynamic-update-slice_fusion.5.right_ref.g_ref, bf16[768,2048]{1,0:T(8,128)(2,1)} %collective-permute-done.26.added_ref), custom_call_target="tpu_custom_call" | custom-call | flops 4831838208 | bytes 1572864 | tf_op jit(solution)/shard_map/weight_rows/pallas_call | solution.py:775
  365.7 18.0 %normed_backward.1 = bf16[1024,2048]{1,0:T(8,128)(2,1)} custom-call(bf16[1024,1536]{1,0:T(8,128)(2,1)S(1)} %get-tuple-element.168.ffn0_ref.right_ref, bf16[1024,1536]{1,0:T(8,128)(2,1)} %get-tuple-element.158.right_ref.ffn1_ref, bf16[4,8,64,1536]{3,2,1,0:T(8,128)(2,1)} %copy-done.44, bf16[4,8,64,1536]{3,2,1,0:T(8,128)(2,1)} %copy-done.77), custom_call_target="tpu_custom_call" | custom-call | flops 22548578304 | bytes 1572864 | tf_op jit(solution)/shard_map/normed_backward/pallas_call | solution.py:687
  391.0 20.1 %collective-permute-done.29 = bf16[128,2048]{1,0:T(8,128)(2,1)S(1)} collective-permute-done((bf16[128,2048]{1,0:T(8,128)(2,1)S(1)}, bf16[128,2048]{1,0:T(8,128)(2,1)S(1)}, u32[]{:S(2)}, u32[]{:S(2)}) %collective-permute-start.29) | collective-permute-done | bytes 524320 | tf_op jit(solution)/shard_map/ppermute | solution.py:23
  414.9 12.4 %weight_gradient.8 = bf16[2048,1536]{1,0:T(8,128)(2,1)} custom-call(bf16[1024,2048]{1,0:T(8,128)(2,1)} %constant_dynamic-update-slice_fusion.10.x_ref.left_ref, bf16[1024,1536]{1,0:T(8,128)(2,1)S(1)} %get-tuple-element.168.ffn0_ref.right_ref, bf16[2048,1536]{1,0:T(8,128)(2,1)} %collective-permute-done.30.refs_0_), custom_call_target="tpu_custom_call" | custom-call | flops 9663676416 | bytes 3145728 | tf_op jit(solution)/shard_map/weight_gradient/pallas_call | solution.py:743
  444.4 7.2 add_convert_fusion
  451.6 11.0 %collective-permute-done.35 = bf16[256,2048]{1,0:T(8,128)(2,1)S(1)} collective-permute-done((bf16[256,2048]{1,0:T(8,128)(2,1)}, bf16[256,2048]{1,0:T(8,128)(2,1)S(1)}, u32[]{:S(2)}, u32[]{:S(2)}) %collective-permute-start.35) | collective-permute-done | bytes 1048608 | tf_op jit(solution)/shard_map/ppermute | solution.py:23
  479.3 7.0 fusion.18
  486.3 9.7 %mix_backward.1 = (bf16[4,256,768]{2,1,0:T(8,128)(2,1)S(1)}, f32[256,8,384]{2,1,0:T(8,128)S(1)}, f32[256,8,384]{2,1,0:T(8,128)}, f32[2,8,384]{2,1,0:T(8,128)S(1)}) custom-call(f32[4,256,768]{2,1,0:T(8,128)} %bitcast.261, f32[4,256,768]{2,1,0:T(8,128)} %bitcast.262, f32[4,256,1536]{2,1,0:T(8,128)} %bitcast.253, f32[4,256,1536]{2,1,0:T(8,128)} %bitcast.254, ...), custom_call_target="tpu_custom_call" | custom-call | flops 786432 | bytes 34603008 | tf_op jit(solution)/shard_map/mix_backward/pallas_call | solution.py:508
  524.1 17.8 %gates_backward.1 = (bf16[4,256,768]{2,1,0:T(8,128)(2,1)S(1)}, f32[3,8,384]{2,1,0:T(8,128)S(1)}, f32[3,8,384]{2,1,0:T(8,128)S(1)}, f32[2,2,176,176]{3,2,1,0:T(8,...) custom-call(f32[256,8,384]{2,1,0:T(8,128)} %copy-done.4, ...), custom_call_target="tpu_custom_call" | custom-call | flops 786432 | bytes 59768832 | tf_op jit(solution)/shard_map/gates_backward/pallas_call | solution.py:531
  550.5 7.5 %weight_gradient.10 = bf16[2048,768]{1,0:T(8,128)(2,1)S(1)} custom-call(bf16[1024,2048]{1,0:T(8,128)(2,1)} %constant_dynamic-update-slice_fusion.left_ref, bf16[1024,768]{1,0:T(8,128)(2,1)S(1)} %pad_maximum_fusion.14.right_ref), custom_call_target="tpu_custom_call" | custom-call | flops 4831838208 | bytes 1572864 | tf_op jit(solution)/shard_map/weight_gradient/pallas_call | solution.py:743
  572.0 11.1 %fusion.2 = bf16[1024,2048]{1,0:T(8,128)(2,1)} fusion(bf16[1024,1536]{1,0:T(8,128)(2,1)S(1)} %pad_maximum_fusion.6, bf16[2048,768]{1,0:T(8,128)(2,1)} %collective-permute-done.6, bf16[2048,768]{1,0:T(8,128)(2,1)} %bitcast.8), kind=kOutput, calls=%fused_computation.5 | convolution fusion | flops 6457131008 | bytes 13631488 | tf_op jit(solution)/shard_map/dot_general | solution.py:803
  594.8 9.4 %weight_gradient.11 = bf16[2048,768]{1,0:T(8,128)(2,1)} custom-call(bf16[1024,2048]{1,0:T(8,128)(2,1)} %constant_dynamic-update-slice_fusion.left_ref, bf16[1024,768]{1,0:T(8,128)(2,1)S(1)} %slice.455.right_ref, bf16[2048,768]{1,0:T(8,128)(2,1)} %collective-permute-done.49.refs_0_), custom_call_target="tpu_custom_call" | custom-call | flops 4831838208 | bytes 1572864 | tf_op jit(solution)/shard_map/weight_gradient/pallas_call | solution.py:743
  613.0 9.6 %collective-permute-done.51 = bf16[128,2048]{1,0:T(8,128)(2,1)} collective-permute-done((bf16[128,2048]{1,0:T(8,128)(2,1)S(1)}, bf16[128,2048]{1,0:T(8,128)(2,1)}, u32[]{:S(2)}, u32[]{:S(2)}) %collective-permute-start.51) | collective-permute-done | bytes 524320 | tf_op jit(solution)/shard_map/ppermute | solution.py:23
  638.0 9.5 %collective-permute-done.66 = f32[2,2048]{1,0:T(2,128)S(1)} collective-permute-done((f32[2,2048]{1,0:T(2,128)S(1)}, f32[2,2048]{1,0:T(2,128)S(1)}, u32[]{:S(2)}, u32[]{:S(2)}) %collective-permute-start.66) | collective-permute-done | bytes 16416 | tf_op jit(solution)/shard_map/ppermute | solution.py:23
  706.4 13.7 %collective-permute-done.77 = bf16[352,512]{1,0:T(8,128)(2,1)S(1)} collective-permute-done((bf16[352,512]{1,0:T(8,128)(2,1)S(1)}, bf16[352,512]{1,0:T(8,128)(2,1)S(1)}, u32[]{:S(2)}, u32[]{:S(2)}) %collective-permute-start.77) | collective-permute-done | bytes 360480 | tf_op jit(solution)/shard_map/ppermute | solution.py:198
  (511 shorter events, 331.1 us)
Async XLA Ops:
  7.2 46.3 %all-gather.6.cloned.1.call-start = ((), (), s32[]{:S(2)}) async-start(), calls=%async_computation.6 | async-start | bytes 1802240 | tf_op jit(solution)/shard_map/all_gather | solution.py:841
  7.9 101.8 %all-gather.8.cloned.1.call-start = ((), (), s32[]{:S(2)}) async-start(), calls=%async_computation.11 | async-start | bytes 3932160 | tf_op jit(solution)/shard_map/all_gather | solution.py:844
  27.1 250.6 %all-gather.10.cloned.1.call-start = ((), (), s32[]{:S(2)}) async-start(), calls=%async_computation.12 | async-start | bytes 11796480 | tf_op jit(solution)/shard_map/all_gather | solution.py:887
  29.1 24.3 %collective-permute-start.1 = (bf16[256,2048]{1,0:T(8,128)(2,1)}, bf16[256,2048]{1,0:T(8,128)(2,1)S(1)}, u32[]{:S(2)}, u32[]{:S(2)}) collective-permute-start(bf16[256,2048]{1,0:T(8,128)(2,1)} %get-tuple-element.348), channel_id=1, source_target_pairs={{0,16},{4,20},{8,24},{12,28},{16,0},{20,4},{24,8},{28,12},{1,17},{... | collective-permute-start | bytes 3145736 | tf_op jit(solution)/shard_map/ppermute | solution.py:23
  29.3 24.2 %collective-permute-start = (bf16[256,2048]{1,0:T(8,128)(2,1)}, bf16[256,2048]{1,0:T(8,128)(2,1)S(1)}, u32[]{:S(2)}, u32[]{:S(2)}) collective-permute-start(bf16[256,2048]{1,0:T(8,128)(2,1)} %get-tuple-element.348), channel_id=1, source_target_pairs={{0,8},{4,12},{8,0},{12,4},{16,24},{20,28},{24,16},{28,20},{1,9},{5... | collective-permute-start | bytes 3145736 | tf_op jit(solution)/shard_map/ppermute | solution.py:23
  111.3 340.2 %reduce-scatter.5.cloned.1.call-start = ((), (), s32[]{:S(2)}) async-start(), calls=%async_computation.7 | async-start | bytes 3932160 | tf_op jit(solution)/shard_map/reduce_scatter | solution.py:922
  122.3 67.1 %collective-permute-start.11 = (bf16[384,2048]{1,0:T(8,128)(2,1)}, bf16[384,2048]{1,0:T(8,128)(2,1)}, u32[]{:S(2)}, u32[]{:S(2)}) collective-permute-start(bf16[384,2048]{1,0:T(8,128)(2,1)} %pad.81), channel_id=1, source_target_pairs={{0,4},{4,0},{8,12},{12,8},{16,20},{20,16},{24,28},{28,24},{1,5},{5... | collective-permute-start | bytes 4718600 | tf_op jit(solution)/shard_map/ppermute | solution.py:23
  122.4 24.3 %collective-permute-start.5 = (bf16[256,2048]{1,0:T(8,128)(2,1)S(1)}, bf16[256,2048]{1,0:T(8,128)(2,1)S(1)}, u32[]{:S(2)}, u32[]{:S(2)}) collective-permute-start(bf16[256,2048]{1,0:T(8,128)(2,1)S(1)} %bitcast.263), channel_id=1, source_target_pairs={{0,16},{4,20},{8,24},{12,28},{16,0},{20,4},{24,8},{28,12},{1,17},{... | collective-permute-start | bytes 3145736 | tf_op jit(solution)/shard_map/ppermute | solution.py:23
  123.5 24.0 %collective-permute-start.4 = (bf16[256,2048]{1,0:T(8,128)(2,1)S(1)}, bf16[256,2048]{1,0:T(8,128)(2,1)S(1)}, u32[]{:S(2)}, u32[]{:S(2)}) collective-permute-start(bf16[256,2048]{1,0:T(8,128)(2,1)S(1)} %bitcast.264), channel_id=1, source_target_pairs={{0,8},{4,12},{8,0},{12,4},{16,24},{20,28},{24,16},{28,20},{1,9},{5... | collective-permute-start | bytes 3145736 | tf_op jit(solution)/shard_map/ppermute | solution.py:23
  235.8 22.3 %collective-permute-start.21 = (bf16[256,2048]{1,0:T(8,128)(2,1)S(1)}, bf16[256,2048]{1,0:T(8,128)(2,1)S(1)}, u32[]{:S(2)}, u32[]{:S(2)}) collective-permute-start(bf16[256,2048]{1,0:T(8,128)(2,1)S(1)} %get-tuple-element.346), channel_id=1, source_target_pairs={{0,16},{4,20},{8,24},{12,28},{16,0},{20,4},{24,8},{28,12},{1,17},{... | collective-permute-start | bytes 3145736 | tf_op jit(solution)/shard_map/ppermute | solution.py:23
  285.6 43.5 %collective-permute-start.25 = (bf16[768,2048]{1,0:T(8,128)(2,1)S(1)}, bf16[768,2048]{1,0:T(8,128)(2,1)}, u32[]{:S(2)}, u32[]{:S(2)}) collective-permute-start(bf16[768,2048]{1,0:T(8,128)(2,1)S(1)} %unpack_down.1.down0_ref), channel_id=1, source_target_pairs={{0,4},{4,0},{8,12},{12,8},{16,20},{20,16},{24,28},{28,24},{1,5},{5... | collective-permute-start | bytes 9437192 | tf_op jit(solution)/shard_map/ppermute | solution.py:23
  315.2 41.4 %collective-permute-start.26 = (bf16[768,2048]{1,0:T(8,128)(2,1)}, bf16[768,2048]{1,0:T(8,128)(2,1)}, u32[]{:S(2)}, u32[]{:S(2)}) collective-permute-start(bf16[768,2048]{1,0:T(8,128)(2,1)} %weight_gradient.6), channel_id=1, source_target_pairs={{0,4},{4,0},{8,12},{12,8},{16,20},{20,16},{24,28},{28,24},{1,5},{5... | collective-permute-start | bytes 9437192 | tf_op jit(solution)/shard_map/ppermute | solution.py:23
  365.5 45.7 %collective-permute-start.30 = (bf16[2048,1536]{1,0:T(8,128)(2,1)}, bf16[2048,1536]{1,0:T(8,128)(2,1)}, u32[]{:S(2)}, u32[]{:S(2)}) collective-permute-start(bf16[2048,1536]{1,0:T(8,128)(2,1)} %weight_gradient.7), channel_id=1, source_target_pairs={{0,4},{4,0},{8,12},{12,8},{16,20},{20,16},{24,28},{28,24},{1,5},{5... | collective-permute-start | bytes 18874376 | tf_op jit(solution)/shard_map/ppermute | solution.py:23
  365.6 201.6 %reduce-scatter.7.cloned.1.call-start = ((), (), s32[]{:S(2)}) async-start(), calls=%async_computation.8 | async-start | bytes 7864320 | tf_op jit(solution)/shard_map/reduce_scatter | solution.py:931
  386.5 40.8 %collective-permute-start.27 = (bf16[128,2048]{1,0:T(8,128)(2,1)}, bf16[128,2048]{1,0:T(8,128)(2,1)}, u32[]{:S(2)}, u32[]{:S(2)}) collective-permute-start(bf16[128,2048]{1,0:T(8,128)(2,1)} %get-tuple-element.363), channel_id=1, source_target_pairs={{0,8},{4,12},{8,0},{12,4},{16,24},{20,28},{24,16},{28,20},{1,9},{5... | collective-permute-start | bytes 1572872 | tf_op jit(solution)/shard_map/ppermute | solution.py:23
  386.8 40.4 %collective-permute-start.33 = (bf16[128,2048]{1,0:T(8,128)(2,1)}, bf16[128,2048]{1,0:T(8,128)(2,1)}, u32[]{:S(2)}, u32[]{:S(2)}) collective-permute-start(bf16[128,2048]{1,0:T(8,128)(2,1)} %get-tuple-element.364), channel_id=1, source_target_pairs={{0,16},{4,20},{8,24},{12,28},{16,0},{20,4},{24,8},{28,12},{1,17},{... | collective-permute-start | bytes 1572872 | tf_op jit(solution)/shard_map/ppermute | solution.py:23
  388.0 23.2 %collective-permute-start.29 = (bf16[128,2048]{1,0:T(8,128)(2,1)S(1)}, bf16[128,2048]{1,0:T(8,128)(2,1)S(1)}, u32[]{:S(2)}, u32[]{:S(2)}) collective-permute-start(bf16[128,2048]{1,0:T(8,128)(2,1)S(1)} %get-tuple-element.365), channel_id=1, source_target_pairs={{0,16},{4,20},{8,24},{12,28},{16,0},{20,4},{24,8},{28,12},{1,17},{... | collective-permute-start | bytes 1572872 | tf_op jit(solution)/shard_map/ppermute | solution.py:23
  388.3 22.8 %collective-permute-start.28 = (bf16[128,2048]{1,0:T(8,128)(2,1)S(1)}, bf16[128,2048]{1,0:T(8,128)(2,1)S(1)}, u32[]{:S(2)}, u32[]{:S(2)}) collective-permute-start(bf16[128,2048]{1,0:T(8,128)(2,1)S(1)} %get-tuple-element.366), channel_id=1, source_target_pairs={{0,8},{4,12},{8,0},{12,4},{16,24},{20,28},{24,16},{28,20},{1,9},{5... | collective-permute-start | bytes 1572872 | tf_op jit(solution)/shard_map/ppermute | solution.py:23
  431.4 199.5 %reduce-scatter.9.cloned.1.call-start = ((), (), s32[]{:S(2)}) async-start(), calls=%async_computation.9 | async-start | bytes 1966080 | tf_op jit(solution)/shard_map/reduce_scatter | solution.py:990
  439.7 23.0 %collective-permute-start.35 = (bf16[256,2048]{1,0:T(8,128)(2,1)}, bf16[256,2048]{1,0:T(8,128)(2,1)S(1)}, u32[]{:S(2)}, u32[]{:S(2)}) collective-permute-start(bf16[256,2048]{1,0:T(8,128)(2,1)} %fusion.74), channel_id=1, source_target_pairs={{0,16},{4,20},{8,24},{12,28},{16,0},{20,4},{24,8},{28,12},{1,17},{... | collective-permute-start | bytes 3145736 | tf_op jit(solution)/shard_map/ppermute | solution.py:23
  439.9 22.7 %collective-permute-start.34 = (bf16[256,2048]{1,0:T(8,128)(2,1)}, bf16[256,2048]{1,0:T(8,128)(2,1)}, u32[]{:S(2)}, u32[]{:S(2)}) collective-permute-start(bf16[256,2048]{1,0:T(8,128)(2,1)} %fusion.74), channel_id=1, source_target_pairs={{0,8},{4,12},{8,0},{12,4},{16,24},{20,28},{24,16},{28,20},{1,9},{5... | collective-permute-start | bytes 3145736 | tf_op jit(solution)/shard_map/ppermute | solution.py:23
  477.1 31.7 %collective-permute-start.43 = (bf16[128,2048]{1,0:T(8,128)(2,1)S(1)}, bf16[128,2048]{1,0:T(8,128)(2,1)S(1)}, u32[]{:S(2)}, u32[]{:S(2)}) collective-permute-start(bf16[128,2048]{1,0:T(8,128)(2,1)S(1)} %get-tuple-element.359), channel_id=1, source_target_pairs={{0,8},{4,12},{8,0},{12,4},{16,24},{20,28},{24,16},{28,20},{1,9},{5... | collective-permute-start | bytes 1572872 | tf_op jit(solution)/shard_map/ppermute | solution.py:23
  478.1 30.8 %collective-permute-start.42 = (bf16[128,2048]{1,0:T(8,128)(2,1)S(1)}, bf16[128,2048]{1,0:T(8,128)(2,1)S(1)}, u32[]{:S(2)}, u32[]{:S(2)}) collective-permute-start(bf16[128,2048]{1,0:T(8,128)(2,1)S(1)} %get-tuple-element.360), channel_id=1, source_target_pairs={{0,16},{4,20},{8,24},{12,28},{16,0},{20,4},{24,8},{28,12},{1,17},{... | collective-permute-start | bytes 1572872 | tf_op jit(solution)/shard_map/ppermute | solution.py:23
  567.2 27.6 %collective-permute-start.49 = (bf16[2048,768]{1,0:T(8,128)(2,1)}, bf16[2048,768]{1,0:T(8,128)(2,1)}, u32[]{:S(2)}, u32[]{:S(2)}) collective-permute-start(bf16[2048,768]{1,0:T(8,128)(2,1)} %copy-done.17), channel_id=1, source_target_pairs={{0,4},{4,0},{8,12},{12,8},{16,20},{20,16},{24,28},{28,24},{1,5},{5... | collective-permute-start | bytes 9437192 | tf_op jit(solution)/shard_map/ppermute | solution.py:23
  589.3 101.3 %reduce-scatter.11.cloned.1.call-start = ((), (), s32[]{:S(2)}) async-start(), calls=%async_computation.10 | async-start | bytes 3932160 | tf_op jit(solution)/shard_map/reduce_scatter | solution.py:1011
  610.8 37.1 %collective-permute-start.38 = (bf16[128,2048]{1,0:T(8,128)(2,1)}, bf16[128,2048]{1,0:T(8,128)(2,1)S(1)}, u32[]{:S(2)}, u32[]{:S(2)}) collective-permute-start(bf16[128,2048]{1,0:T(8,128)(2,1)} %get-tuple-element.357), channel_id=1, source_target_pairs={{0,8},{4,12},{8,0},{12,4},{16,24},{20,28},{24,16},{28,20},{1,9},{5... | collective-permute-start | bytes 1572872 | tf_op jit(solution)/shard_map/ppermute | solution.py:23
  611.8 36.6 %collective-permute-start.57 = (bf16[128,2048]{1,0:T(8,128)(2,1)}, bf16[128,2048]{1,0:T(8,128)(2,1)S(1)}, u32[]{:S(2)}, u32[]{:S(2)}) collective-permute-start(bf16[128,2048]{1,0:T(8,128)(2,1)} %get-tuple-element.358), channel_id=1, source_target_pairs={{0,16},{4,20},{8,24},{12,28},{16,0},{20,4},{24,8},{28,12},{1,17},{... | collective-permute-start | bytes 1572872 | tf_op jit(solution)/shard_map/ppermute | solution.py:23
  633.7 28.8 %collective-permute-start.59 = (bf16[128,2048]{1,0:T(8,128)(2,1)S(1)}, bf16[128,2048]{1,0:T(8,128)(2,1)S(1)}, u32[]{:S(2)}, u32[]{:S(2)}) collective-permute-start(bf16[128,2048]{1,0:T(8,128)(2,1)S(1)} %copy-done.59), channel_id=1, source_target_pairs={{0,8},{4,12},{8,0},{12,4},{16,24},{20,28},{24,16},{28,20},{1,9},{5... | collective-permute-start | bytes 1572872 | tf_op jit(solution)/shard_map/ppermute | solution.py:23
  634.1 28.4 %collective-permute-start.62 = (bf16[128,2048]{1,0:T(8,128)(2,1)S(1)}, bf16[128,2048]{1,0:T(8,128)(2,1)S(1)}, u32[]{:S(2)}, u32[]{:S(2)}) collective-permute-start(bf16[128,2048]{1,0:T(8,128)(2,1)S(1)} %copy-done.58), channel_id=1, source_target_pairs={{0,16},{4,20},{8,24},{12,28},{16,0},{20,4},{24,8},{28,12},{1,17},{... | collective-permute-start | bytes 1572872 | tf_op jit(solution)/shard_map/ppermute | solution.py:23
  659.7 28.6 %collective-permute-start.58 = (bf16[352,512]{1,0:T(8,128)(2,1)S(1)}, bf16[352,512]{1,0:T(8,128)(2,1)S(1)}, u32[]{:S(2)}, u32[]{:S(2)}) collective-permute-start(bf16[352,512]{1,0:T(8,128)(2,1)S(1)} %slice.462), channel_id=1, source_target_pairs={{0,0},{1,9},{2,18},{3,27},{4,28},{5,21},{6,14},{7,7},{8,8},{9,1},{... | collective-permute-start | bytes 1081352 | tf_op jit(solution)/shard_map/ppermute | solution.py:188
  690.5 30.8 %collective-permute-start.79 = (bf16[768,512]{1,0:T(8,128)(2,1)}, bf16[768,512]{1,0:T(8,128)(2,1)S(1)}, u32[]{:S(2)}, u32[]{:S(2)}) collective-permute-start(bf16[768,512]{1,0:T(8,128)(2,1)} %collective-permute-done.54), channel_id=1, source_target_pairs={{0,0},{1,1},{2,2},{3,3},{4,7},{5,6},{6,5},{7,4},{8,9},{9,8},{10,11... | collective-permute-start | bytes 2359304 | tf_op jit(solution)/shard_map/ppermute | solution.py:198
  697.8 22.3 %collective-permute-start.77 = (bf16[352,512]{1,0:T(8,128)(2,1)S(1)}, bf16[352,512]{1,0:T(8,128)(2,1)S(1)}, u32[]{:S(2)}, u32[]{:S(2)}) collective-permute-start(bf16[352,512]{1,0:T(8,128)(2,1)S(1)} %collective-permute-done.58), channel_id=1, source_target_pairs={{0,0},{1,1},{2,2},{3,3},{4,7},{5,6},{6,5},{7,4},{8,9},{9,8},{10,11... | collective-permute-start | bytes 1081352 | tf_op jit(solution)/shard_map/ppermute | solution.py:198
  (134 other events, 1270.2 us)
Sparse Core Ops, SparseCore 0:
  9.6 35.4 all-gather.5
  46.6 63.0 all-gather.7
  111.9 165.6 all-gather.9
  365.7 60.6 reduce-scatter.4
  431.5 114.3 reduce-scatter.6
  589.4 34.9 reduce-scatter.8
  631.1 59.4 reduce-scatter.10

commit v5 on v4

--- a/solution.py
+++ b/solution.py
@@ -188,22 +188,21 @@
     return lax.ppermute(block, ("dp", "seq"), perm)
 
 
-def move_across(block):
+def move_across(block, *beside):
     dp_count, seq_count = lax.axis_size("dp"), lax.axis_size("seq")
     assert dp_count == 2 * seq_count
     perm = []
     for d in range(dp_count):
         for s in range(seq_count):
             perm.append((d * seq_count + s, d * seq_count + (s ^ shift_of(d, 2, seq_count))))
-    block = lax.ppermute(block, ("dp", "seq"), perm)
+    block, *beside = tie(lax.ppermute(block, ("dp", "seq"), perm), *beside)
     half = block.shape[1] // 2
     first_core = lax.axis_index("dp") % 2 == 0
     left, right = block[:, :half], block[:, half:]
     kept = jnp.where(first_core, left, right)
     moved = xor_send(jnp.where(first_core, right, left), "dp", 1)
-    return jnp.concatenate(
-        [jnp.where(first_core, kept, moved), jnp.where(first_core, moved, kept)], axis=0
-    )
+    rows = jnp.where(first_core, kept, moved), jnp.where(first_core, moved, kept)
+    return rows, *beside
 
 
 def scaled_norm(values, gain_vec):
@@ -1012,11 +1011,9 @@
     inv_one = lax.rsqrt(jnp.mean(tokens * tokens, axis=-1, keepdims=True) + EPSILON)
     grad_tokens, _ = norm_back(grad_normed, tokens, inv_one, norm_gain)
     input_grad = (grad_tokens + grad_residual).reshape(block_input.shape)
-    grad_first_w, down_cols, out_cols, input_grad = tie(
-        grad_first_w, down_cols, out_cols, input_grad
-    )
-    grad_down_w = move_across(down_cols).astype(F32)
-    grad_out_w = move_across(out_cols).astype(F32)
+    grad_first_w, placed_rows, input_grad = tie(
+        grad_first_w, jnp.concatenate([down_cols, out_cols], axis=0), input_grad
+    )
     grad_in_w = grad_first_w[:, :own].astype(F32)
     grad_gate_w = grad_first_w[:, width : width + own].astype(F32)
 
@@ -1024,6 +1021,11 @@
     decay_term = sums[2] * (8.0 * jax.nn.sigmoid(-decay_param))
     blocks = widen_blocks(blocks)
     gains = sum_over(sum_over(jnp.stack([norm_gain_term, mlp_gain_term]), "dp"), "seq")
+    blocks_of_rows, gains, sums, grad_in_w, grad_gate_w, *blocks = move_across(
+        placed_rows, gains, sums, grad_in_w, grad_gate_w, *blocks
+    )
+    grad_down_w = jnp.concatenate([part[:hidden_width] for part in blocks_of_rows]).astype(F32)
+    grad_out_w = jnp.concatenate([part[hidden_width:] for part in blocks_of_rows]).astype(F32)
     return (
         block_output,
         input_grad,

time: 746 us -> 749 us (level)
  waiting for transfers between devices: 208 us -> 220 us
  starting transfers between devices: 102 us -> 92.2 us
    ppermute x69 -> x68, starting transfers between devices: 71.4 us -> 63.6 us  [xor_send(): return lax.ppermute(value, axis, [(i, i ^ offset) for i in range(count)])]
    ppermute x2 -> x1, waiting for transfers between devices: 13.7 us -> 19.3 us  [move_across(): block, *beside = tie(lax.ppermute(block, ('dp', 'seq'), perm), *beside)]
    ppermute x69 -> x68, waiting for transfers between devices: 177 us -> 181 us  [xor_send(): return lax.ppermute(value, axis, [(i, i ^ offset) for i in range(count)])]
  transfers between devices with their start and end apart: 88 -> 86, of which waited for: 32 -> 35; matrix products, arithmetic and copies ran while one was open for 22% -> 21% of each run, Pallas kernels for 23% -> 23%
where the time goes in v5:
time: 749 us; the launch traced here: 736 us
  waiting for transfers between devices  220 us (29%)
  Pallas kernels  180 us (24%)
  starting transfers between devices  92.2 us (12%)
  local copies, waits for them, and re-layouts  90.1 us (12%)
  other arithmetic  52.4 us (7%)
  matrix products  45 us (6%)
  blocking collectives  41.4 us (6%)
  between operations  16.1 us (2%)
    ppermute x68, waiting for transfers between devices, xor_send(): return lax.ppermute(value, axis, [(i, i ^ offset) for i in range(count)])  181 us
    ppermute x68, starting transfers between devices, xor_send(): return lax.ppermute(value, axis, [(i, i ^ offset) for i in range(count)])  63.6 us
    pallas_call x6, Pallas kernels, mm_weight(): pl.pallas_call(weight_kernel, out_shape=jax.ShapeDtypeStruct((rows, cols)...  52.6 us
    all_to_all x2, blocking collectives, spread(): return lax.all_to_all(joined, 'dp', split_axis=0, concat_axis=0, tiled=True)  41.4 us
    unnamed x175, local copies, waits for them, and re-layouts  36.9 us
    dot_general x4, matrix products, mm(): return jnp.dot(left, right, preferred_element_type=F32)  26.9 us
    pallas_call x2, Pallas kernels, mlp_forward(): pl.pallas_call(mlp_forward_kernel, out_shape=(jax.ShapeDtypeStruct((rows,...  23.6 us
    ppermute x1, waiting for transfers between devices, move_across(): block, *beside = tie(lax.ppermute(block, ('dp', 'seq'), perm), *beside)  19.3 us
  transfers between devices with their start and end apart: 86, of which 35 were waited for; matrix products, arithmetic and copies ran while one was open for 21% of the time, Pallas kernels for 23%

profile of v5, /device:TPU:3, one launch (start us, length us, event | category | flops | bytes accessed | tf_op | source)
XLA Modules:
  0.0 736.4 jit_solution(197002308291949848)
XLA Ops:
  11.6 15.5 %all_to_all.10 = bf16[8,64,768]{2,1,0:T(8,128)(2,1)} all-to-all(bf16[8,64,768]{2,1,0:T(8,128)(2,1)S(1)} %copy.117), channel_id=1, replica_groups=mesh['dp'=8,'seq'=4] {'dp'}, dimensions={0} | all-to-all | bytes 1572864 | tf_op jit(solution)/shard_map/all_to_all | solution.py:832
  37.0 16.5 %collective-permute-done.1 = bf16[256,2048]{1,0:T(8,128)(2,1)S(1)} collective-permute-done((bf16[256,2048]{1,0:T(8,128)(2,1)}, bf16[256,2048]{1,0:T(8,128)(2,1)S(1)}, u32[]{:S(2)}, u32[]{:S(2)}) %collective-permute-start.1) | collective-permute-done | bytes 1048608 | tf_op jit(solution)/shard_map/ppermute | solution.py:23
  80.4 25.9 %all_to_all.11 = bf16[8,64,1536]{2,1,0:T(8,128)(2,1)S(1)} all-to-all(bf16[8,64,1536]{2,1,0:T(8,128)(2,1)S(1)} %copy.116), channel_id=1, replica_groups=mesh['dp'=8,'seq'=4] {'dp'}, dimensions={0} | all-to-all | bytes 3145728 | tf_op jit(solution)/shard_map/all_to_all | solution.py:832
  124.6 9.0 %fusion.1 = f32[1024,1536]{1,0:T(8,128)S(1)} fusion(bf16[1024,2048]{1,0:T(8,128)(2,1)S(1)} %copy-done.42, bf16[2048,768]{1,0:T(8,128)(2,1)} %collective-permute-done.6, bf16[2048,768]{1,0:T(8,128)(2,1)} %bitcast.8), kind=kOutput, calls=%fused_computation.4 | convolution fusion | flops 6455033856 | bytes 16777216 | tf_op jit(solution)/shard_map/dot_general | solution.py:798
  133.7 13.0 %collective-permute-done.5 = bf16[256,2048]{1,0:T(8,128)(2,1)S(1)} collective-permute-done((bf16[256,2048]{1,0:T(8,128)(2,1)S(1)}, bf16[256,2048]{1,0:T(8,128)(2,1)S(1)}, u32[]{:S(2)}, u32[]{:S(2)}) %collective-permute-start.5) | collective-permute-done | bytes 1048608 | tf_op jit(solution)/shard_map/ppermute | solution.py:23
  151.0 13.2 %gates_forward.1 = (f32[256,8,384]{2,1,0:T(8,128)S(1)}, f32[256,8,384]{2,1,0:T(8,128)}, f32[256,8,384]{2,1,0:T(8,128)}, f32[256,8,384]{2,1,0:T(8,128)}, f32[256,...) custom-call(f32[4,256,1536]{2,1,0:T(8,128)} %bitcast.249, ...), custom_call_target="tpu_custom_call" | custom-call | flops 786432 | bytes 45613056 | tf_op jit(solution)/shard_map/gates_forward/pallas_call | solution.py:462
  181.3 8.2 %mix_forward.1 = (bf16[4,256,768]{2,1,0:T(8,128)(2,1)S(1)}, f32[256,8,384]{2,1,0:T(8,128)S(1)}, f32[8,256,384]{2,1,0:T(8,128)}) custom-call(f32[256,8,384]{2,1,0:T(8,128)} %get-tuple-element.143.loc_ref, f32[256,8,384]{2,1,0:T(8,128)} %get-tuple-element.144.run_ref, f32[8,384]{1,0:T(8,128)S(1)} %fusion.61.carry_ref, f32[4,256,1536]{2,1,0:T(8,128)} %bitcast.251, ...), custom_call_target="tpu_custom_call" | custom-call | flops 786432 | bytes 28311552 | tf_op jit(solution)/shard_map/mix_forward/pallas_call | solution.py:486
  189.6 7.2 convolution_convert_fusion
  201.8 9.0 %collective-permute-done.16 = bf16[128,2048]{1,0:T(8,128)(2,1)S(1)} collective-permute-done((bf16[128,2048]{1,0:T(8,128)(2,1)S(1)}, bf16[128,2048]{1,0:T(8,128)(2,1)S(1)}, u32[]{:S(2)}, u32[]{:S(2)}) %collective-permute-start.16) | collective-permute-done | bytes 524320 | tf_op jit(solution)/shard_map/ppermute | solution.py:23
  213.8 8.0 %collective-permute-done.14 = bf16[128,2048]{1,0:T(8,128)(2,1)S(1)} collective-permute-done((bf16[128,2048]{1,0:T(8,128)(2,1)S(1)}, bf16[128,2048]{1,0:T(8,128)(2,1)S(1)}, u32[]{:S(2)}, u32[]{:S(2)}) %collective-permute-start.14) | collective-permute-done | bytes 524320 | tf_op jit(solution)/shard_map/ppermute | solution.py:23
  222.1 11.2 %collective-permute-done.17 = bf16[128,2048]{1,0:T(8,128)(2,1)S(1)} collective-permute-done((bf16[128,2048]{1,0:T(8,128)(2,1)S(1)}, bf16[128,2048]{1,0:T(8,128)(2,1)S(1)}, u32[]{:S(2)}, u32[]{:S(2)}) %collective-permute-start.17) | collective-permute-done | bytes 524320 | tf_op jit(solution)/shard_map/ppermute | solution.py:23
  238.2 20.0 %collective-permute-done.21 = bf16[256,2048]{1,0:T(8,128)(2,1)S(1)} collective-permute-done((bf16[256,2048]{1,0:T(8,128)(2,1)S(1)}, bf16[256,2048]{1,0:T(8,128)(2,1)S(1)}, u32[]{:S(2)}, u32[]{:S(2)}) %collective-permute-start.21) | collective-permute-done | bytes 1048608 | tf_op jit(solution)/shard_map/ppermute | solution.py:23
  294.1 11.8 %mlp_forward.2 = (bf16[1024,768]{1,0:T(8,128)(2,1)S(1)}, bf16[1024,1536]{1,0:T(8,128)(2,1)S(1)}) custom-call(bf16[1024,2048]{1,0:T(8,128)(2,1)} %constant_dynamic-update-slice_fusion.10.x_ref.left_ref, bf16[4,8,64,1536]{3,2,1,0:T(8,128)(2,1)} %copy-done.77), custom_call_target="tpu_custom_call" | custom-call | flops 11274289152 | bytes 2097152 | tf_op jit(solution)/shard_map/mlp_forward/pallas_call | solution.py:586
  307.5 7.7 %weight_gradient.6 = bf16[768,2048]{1,0:T(8,128)(2,1)} custom-call(bf16[1024,768]{1,0:T(8,128)(2,1)S(1)} %get-tuple-element.179.left_ref, bf16[1024,2048]{1,0:T(8,128)(2,1)} %constant_dynamic-update-slice_fusion.5.right_ref.g_ref), custom_call_target="tpu_custom_call" | custom-call | flops 4831838208 | bytes 1572864 | tf_op jit(solution)/shard_map/weight_gradient/pallas_call | solution.py:742
  315.5 11.8 %mlp_forward.3 = (bf16[1024,768]{1,0:T(8,128)(2,1)S(1)}, bf16[1024,1536]{1,0:T(8,128)(2,1)S(1)}) custom-call(bf16[1024,2048]{1,0:T(8,128)(2,1)} %constant_dynamic-update-slice_fusion.10.x_ref.left_ref, bf16[4,8,64,1536]{3,2,1,0:T(8,128)(2,1)} %copy-done.44), custom_call_target="tpu_custom_call" | custom-call | flops 11274289152 | bytes 2097152 | tf_op jit(solution)/shard_map/mlp_forward/pallas_call | solution.py:586
  329.1 14.5 %hidden_backward.1 = (bf16[1024,1536]{1,0:T(8,128)(2,1)S(1)}, bf16[1024,1536]{1,0:T(8,128)(2,1)}) custom-call(bf16[1024,2048]{1,0:T(8,128)(2,1)} %constant_dynamic-update-slice_fusion.5.right_ref.g_ref, bf16[768,2048]{1,0:T(8,128)(2,1)} %copy-done.5, bf16[768,2048]{1,0:T(8,128)(2,1)} %collective-permute-done.25.down1_ref, bf16[1024,1536]{1,0:T(8,128)(2,1)} %copy-done.24, ...), custom_call_target="tpu_custom_call" | custom-call | flops 11274289152 | bytes 2097152 | tf_op jit(solution)/shard_map/hidden_backward/pallas_call | solution.py:644
  345.5 11.1 %weight_gradient.7 = bf16[2048,1536]{1,0:T(8,128)(2,1)} custom-call(bf16[1024,2048]{1,0:T(8,128)(2,1)} %constant_dynamic-update-slice_fusion.10.x_ref.left_ref, bf16[1024,1536]{1,0:T(8,128)(2,1)S(1)} %copy-done.22), custom_call_target="tpu_custom_call" | custom-call | flops 9663676416 | bytes 3145728 | tf_op jit(solution)/shard_map/weight_gradient/pallas_call | solution.py:742
  356.6 8.8 %weight_rows.2 = bf16[4,768,512]{2,1,0:T(8,128)(2,1)} custom-call(s32[1]{0:T(128)} %bitcast.39.shift_ref, bf16[1024,768]{1,0:T(8,128)(2,1)S(1)} %get-tuple-element.178.left_ref, bf16[1024,2048]{1,0:T(8,128)(2,1)} %constant_dynamic-update-slice_fusion.5.right_ref.g_ref, bf16[768,2048]{1,0:T(8,128)(2,1)} %collective-permute-done.26.added_ref), custom_call_target="tpu_custom_call" | custom-call | flops 4831838208 | bytes 1572864 | tf_op jit(solution)/shard_map/weight_rows/pallas_call | solution.py:774
  365.6 18.0 %normed_backward.1 = bf16[1024,2048]{1,0:T(8,128)(2,1)} custom-call(bf16[1024,1536]{1,0:T(8,128)(2,1)S(1)} %get-tuple-element.174.ffn0_ref.right_ref, bf16[1024,1536]{1,0:T(8,128)(2,1)} %get-tuple-element.164.right_ref.ffn1_ref, bf16[4,8,64,1536]{3,2,1,0:T(8,128)(2,1)} %copy-done.44, bf16[4,8,64,1536]{3,2,1,0:T(8,128)(2,1)} %copy-done.77), custom_call_target="tpu_custom_call" | custom-call | flops 22548578304 | bytes 1572864 | tf_op jit(solution)/shard_map/normed_backward/pallas_call | solution.py:686
  390.9 20.1 %collective-permute-done.29 = bf16[128,2048]{1,0:T(8,128)(2,1)S(1)} collective-permute-done((bf16[128,2048]{1,0:T(8,128)(2,1)S(1)}, bf16[128,2048]{1,0:T(8,128)(2,1)S(1)}, u32[]{:S(2)}, u32[]{:S(2)}) %collective-permute-start.29) | collective-permute-done | bytes 524320 | tf_op jit(solution)/shard_map/ppermute | solution.py:23
  414.7 12.4 %weight_gradient.8 = bf16[2048,1536]{1,0:T(8,128)(2,1)} custom-call(bf16[1024,2048]{1,0:T(8,128)(2,1)} %constant_dynamic-update-slice_fusion.10.x_ref.left_ref, bf16[1024,1536]{1,0:T(8,128)(2,1)S(1)} %get-tuple-element.174.ffn0_ref.right_ref, bf16[2048,1536]{1,0:T(8,128)(2,1)} %collective-permute-done.30.refs_0_), custom_call_target="tpu_custom_call" | custom-call | flops 9663676416 | bytes 3145728 | tf_op jit(solution)/shard_map/weight_gradient/pallas_call | solution.py:742
  444.1 7.2 add_convert_fusion
  451.3 11.0 %collective-permute-done.35 = bf16[256,2048]{1,0:T(8,128)(2,1)S(1)} collective-permute-done((bf16[256,2048]{1,0:T(8,128)(2,1)}, bf16[256,2048]{1,0:T(8,128)(2,1)S(1)}, u32[]{:S(2)}, u32[]{:S(2)}) %collective-permute-start.35) | collective-permute-done | bytes 1048608 | tf_op jit(solution)/shard_map/ppermute | solution.py:23
  485.9 9.6 %mix_backward.1 = (bf16[4,256,768]{2,1,0:T(8,128)(2,1)S(1)}, f32[256,8,384]{2,1,0:T(8,128)S(1)}, f32[256,8,384]{2,1,0:T(8,128)}, f32[2,8,384]{2,1,0:T(8,128)S(1)}) custom-call(f32[4,256,768]{2,1,0:T(8,128)} %bitcast.261, f32[4,256,768]{2,1,0:T(8,128)} %bitcast.262, f32[4,256,1536]{2,1,0:T(8,128)} %bitcast.253, f32[4,256,1536]{2,1,0:T(8,128)} %bitcast.254, ...), custom_call_target="tpu_custom_call" | custom-call | flops 786432 | bytes 34603008 | tf_op jit(solution)/shard_map/mix_backward/pallas_call | solution.py:507
  523.7 17.9 %gates_backward.1 = (bf16[4,256,768]{2,1,0:T(8,128)(2,1)S(1)}, f32[3,8,384]{2,1,0:T(8,128)S(1)}, f32[3,8,384]{2,1,0:T(8,128)S(1)}, f32[2,2,176,176]{3,2,1,0:T(8,...) custom-call(f32[256,8,384]{2,1,0:T(8,128)} %copy-done.4, ...), custom_call_target="tpu_custom_call" | custom-call | flops 786432 | bytes 59768832 | tf_op jit(solution)/shard_map/gates_backward/pallas_call | solution.py:530
  550.1 7.5 %weight_gradient.10 = bf16[2048,768]{1,0:T(8,128)(2,1)S(1)} custom-call(bf16[1024,2048]{1,0:T(8,128)(2,1)} %constant_dynamic-update-slice_fusion.left_ref, bf16[1024,768]{1,0:T(8,128)(2,1)S(1)} %pad_maximum_fusion.14.right_ref), custom_call_target="tpu_custom_call" | custom-call | flops 4831838208 | bytes 1572864 | tf_op jit(solution)/shard_map/weight_gradient/pallas_call | solution.py:742
  571.7 11.1 %fusion.2 = bf16[1024,2048]{1,0:T(8,128)(2,1)} fusion(bf16[1024,1536]{1,0:T(8,128)(2,1)S(1)} %pad_maximum_fusion.6, bf16[2048,768]{1,0:T(8,128)(2,1)} %collective-permute-done.6, bf16[2048,768]{1,0:T(8,128)(2,1)} %bitcast.8), kind=kOutput, calls=%fused_computation.5 | convolution fusion | flops 6457131008 | bytes 13631488 | tf_op jit(solution)/shard_map/dot_general | solution.py:802
  594.5 9.4 %weight_gradient.11 = bf16[2048,768]{1,0:T(8,128)(2,1)} custom-call(bf16[1024,2048]{1,0:T(8,128)(2,1)} %constant_dynamic-update-slice_fusion.left_ref, bf16[1024,768]{1,0:T(8,128)(2,1)S(1)} %slice.455.right_ref, bf16[2048,768]{1,0:T(8,128)(2,1)} %collective-permute-done.49.refs_0_), custom_call_target="tpu_custom_call" | custom-call | flops 4831838208 | bytes 1572864 | tf_op jit(solution)/shard_map/weight_gradient/pallas_call | solution.py:742
  612.7 9.5 %collective-permute-done.51 = bf16[128,2048]{1,0:T(8,128)(2,1)} collective-permute-done((bf16[128,2048]{1,0:T(8,128)(2,1)S(1)}, bf16[128,2048]{1,0:T(8,128)(2,1)}, u32[]{:S(2)}, u32[]{:S(2)}) %collective-permute-start.51) | collective-permute-done | bytes 524320 | tf_op jit(solution)/shard_map/ppermute | solution.py:23
  657.0 8.5 %collective-permute-done.60 = bf16[128,2048]{1,0:T(8,128)(2,1)S(1)} collective-permute-done((bf16[128,2048]{1,0:T(8,128)(2,1)S(1)}, bf16[128,2048]{1,0:T(8,128)(2,1)S(1)}, u32[]{:S(2)}, u32[]{:S(2)}) %collective-permute-start.60) | collective-permute-done | bytes 524320 | tf_op jit(solution)/shard_map/ppermute | solution.py:23
  678.2 9.8 %collective-permute-done.75 = bf16[2,2,176,176]{3,2,1,0:T(8,128)(2,1)S(1)} collective-permute-done((bf16[2,2,176,176]{3,2,1,0:T(8,128)(2,1)S(1)}, bf16[2,2,176,176]{3,2,1,0:T(8,128)(2,1)S(1)}, u32[]{:S(2)}, u32[]{:S(2)}) %collective-permute-start.75) | collective-permute-done | bytes 247840 | tf_op jit(solution)/shard_map/ppermute | solution.py:23
  701.1 19.3 %collective-permute-done.64 = bf16[1120,512]{1,0:T(8,128)(2,1)S(1)} collective-permute-done((bf16[1120,512]{1,0:T(8,128)(2,1)}, bf16[1120,512]{1,0:T(8,128)(2,1)S(1)}, u32[]{:S(2)}, u32[]{:S(2)}) %collective-permute-start.64) | collective-permute-done | bytes 1146912 | tf_op jit(solution)/shard_map/ppermute | solution.py:198
  (508 shorter events, 326.5 us)
Async XLA Ops:
  7.2 46.3 %all-gather.6.cloned.1.call-start = ((), (), s32[]{:S(2)}) async-start(), calls=%async_computation.6 | async-start | bytes 1802240 | tf_op jit(solution)/shard_map/all_gather | solution.py:840
  7.9 101.8 %all-gather.8.cloned.1.call-start = ((), (), s32[]{:S(2)}) async-start(), calls=%async_computation.11 | async-start | bytes 3932160 | tf_op jit(solution)/shard_map/all_gather | solution.py:843
  27.1 250.6 %all-gather.10.cloned.1.call-start = ((), (), s32[]{:S(2)}) async-start(), calls=%async_computation.12 | async-start | bytes 11796480 | tf_op jit(solution)/shard_map/all_gather | solution.py:886
  29.1 24.3 %collective-permute-start.1 = (bf16[256,2048]{1,0:T(8,128)(2,1)}, bf16[256,2048]{1,0:T(8,128)(2,1)S(1)}, u32[]{:S(2)}, u32[]{:S(2)}) collective-permute-start(bf16[256,2048]{1,0:T(8,128)(2,1)} %get-tuple-element.359), channel_id=1, source_target_pairs={{0,16},{4,20},{8,24},{12,28},{16,0},{20,4},{24,8},{28,12},{1,17},{... | collective-permute-start | bytes 3145736 | tf_op jit(solution)/shard_map/ppermute | solution.py:23
  29.3 24.2 %collective-permute-start = (bf16[256,2048]{1,0:T(8,128)(2,1)}, bf16[256,2048]{1,0:T(8,128)(2,1)S(1)}, u32[]{:S(2)}, u32[]{:S(2)}) collective-permute-start(bf16[256,2048]{1,0:T(8,128)(2,1)} %get-tuple-element.359), channel_id=1, source_target_pairs={{0,8},{4,12},{8,0},{12,4},{16,24},{20,28},{24,16},{28,20},{1,9},{5... | collective-permute-start | bytes 3145736 | tf_op jit(solution)/shard_map/ppermute | solution.py:23
  111.3 340.0 %reduce-scatter.5.cloned.1.call-start = ((), (), s32[]{:S(2)}) async-start(), calls=%async_computation.7 | async-start | bytes 3932160 | tf_op jit(solution)/shard_map/reduce_scatter | solution.py:921
  122.3 67.2 %collective-permute-start.11 = (bf16[384,2048]{1,0:T(8,128)(2,1)}, bf16[384,2048]{1,0:T(8,128)(2,1)}, u32[]{:S(2)}, u32[]{:S(2)}) collective-permute-start(bf16[384,2048]{1,0:T(8,128)(2,1)} %pad.81), channel_id=1, source_target_pairs={{0,4},{4,0},{8,12},{12,8},{16,20},{20,16},{24,28},{28,24},{1,5},{5... | collective-permute-start | bytes 4718600 | tf_op jit(solution)/shard_map/ppermute | solution.py:23
  122.3 24.3 %collective-permute-start.5 = (bf16[256,2048]{1,0:T(8,128)(2,1)S(1)}, bf16[256,2048]{1,0:T(8,128)(2,1)S(1)}, u32[]{:S(2)}, u32[]{:S(2)}) collective-permute-start(bf16[256,2048]{1,0:T(8,128)(2,1)S(1)} %bitcast.263), channel_id=1, source_target_pairs={{0,16},{4,20},{8,24},{12,28},{16,0},{20,4},{24,8},{28,12},{1,17},{... | collective-permute-start | bytes 3145736 | tf_op jit(solution)/shard_map/ppermute | solution.py:23
  123.5 24.0 %collective-permute-start.4 = (bf16[256,2048]{1,0:T(8,128)(2,1)S(1)}, bf16[256,2048]{1,0:T(8,128)(2,1)S(1)}, u32[]{:S(2)}, u32[]{:S(2)}) collective-permute-start(bf16[256,2048]{1,0:T(8,128)(2,1)S(1)} %bitcast.264), channel_id=1, source_target_pairs={{0,8},{4,12},{8,0},{12,4},{16,24},{20,28},{24,16},{28,20},{1,9},{5... | collective-permute-start | bytes 3145736 | tf_op jit(solution)/shard_map/ppermute | solution.py:23
  200.4 21.6 %collective-permute-start.19 = (bf16[128,2048]{1,0:T(8,128)(2,1)S(1)}, bf16[128,2048]{1,0:T(8,128)(2,1)S(1)}, u32[]{:S(2)}, u32[]{:S(2)}) collective-permute-start(bf16[128,2048]{1,0:T(8,128)(2,1)S(1)} %get-tuple-element.381), channel_id=1, source_target_pairs={{0,16},{4,20},{8,24},{12,28},{16,0},{20,4},{24,8},{28,12},{1,17},{... | collective-permute-start | bytes 1572872 | tf_op jit(solution)/shard_map/ppermute | solution.py:23
  211.2 22.1 %collective-permute-start.17 = (bf16[128,2048]{1,0:T(8,128)(2,1)S(1)}, bf16[128,2048]{1,0:T(8,128)(2,1)S(1)}, u32[]{:S(2)}, u32[]{:S(2)}) collective-permute-start(bf16[128,2048]{1,0:T(8,128)(2,1)S(1)} %get-tuple-element.384), channel_id=1, source_target_pairs={{0,16},{4,20},{8,24},{12,28},{16,0},{20,4},{24,8},{28,12},{1,17},{... | collective-permute-start | bytes 1572872 | tf_op jit(solution)/shard_map/ppermute | solution.py:23
  235.9 22.3 %collective-permute-start.21 = (bf16[256,2048]{1,0:T(8,128)(2,1)S(1)}, bf16[256,2048]{1,0:T(8,128)(2,1)S(1)}, u32[]{:S(2)}, u32[]{:S(2)}) collective-permute-start(bf16[256,2048]{1,0:T(8,128)(2,1)S(1)} %get-tuple-element.357), channel_id=1, source_target_pairs={{0,16},{4,20},{8,24},{12,28},{16,0},{20,4},{24,8},{28,12},{1,17},{... | collective-permute-start | bytes 3145736 | tf_op jit(solution)/shard_map/ppermute | solution.py:23
  237.1 21.8 %collective-permute-start.20 = (bf16[256,2048]{1,0:T(8,128)(2,1)S(1)}, bf16[256,2048]{1,0:T(8,128)(2,1)S(1)}, u32[]{:S(2)}, u32[]{:S(2)}) collective-permute-start(bf16[256,2048]{1,0:T(8,128)(2,1)S(1)} %get-tuple-element.357), channel_id=1, source_target_pairs={{0,8},{4,12},{8,0},{12,4},{16,24},{20,28},{24,16},{28,20},{1,9},{5... | collective-permute-start | bytes 3145736 | tf_op jit(solution)/shard_map/ppermute | solution.py:23
  285.6 43.5 %collective-permute-start.25 = (bf16[768,2048]{1,0:T(8,128)(2,1)S(1)}, bf16[768,2048]{1,0:T(8,128)(2,1)}, u32[]{:S(2)}, u32[]{:S(2)}) collective-permute-start(bf16[768,2048]{1,0:T(8,128)(2,1)S(1)} %unpack_down.1.down0_ref), channel_id=1, source_target_pairs={{0,4},{4,0},{8,12},{12,8},{16,20},{20,16},{24,28},{28,24},{1,5},{5... | collective-permute-start | bytes 9437192 | tf_op jit(solution)/shard_map/ppermute | solution.py:23
  315.2 41.4 %collective-permute-start.26 = (bf16[768,2048]{1,0:T(8,128)(2,1)}, bf16[768,2048]{1,0:T(8,128)(2,1)}, u32[]{:S(2)}, u32[]{:S(2)}) collective-permute-start(bf16[768,2048]{1,0:T(8,128)(2,1)} %weight_gradient.6), channel_id=1, source_target_pairs={{0,4},{4,0},{8,12},{12,8},{16,20},{20,16},{24,28},{28,24},{1,5},{5... | collective-permute-start | bytes 9437192 | tf_op jit(solution)/shard_map/ppermute | solution.py:23
  365.4 45.6 %collective-permute-start.30 = (bf16[2048,1536]{1,0:T(8,128)(2,1)}, bf16[2048,1536]{1,0:T(8,128)(2,1)}, u32[]{:S(2)}, u32[]{:S(2)}) collective-permute-start(bf16[2048,1536]{1,0:T(8,128)(2,1)} %weight_gradient.7), channel_id=1, source_target_pairs={{0,4},{4,0},{8,12},{12,8},{16,20},{20,16},{24,28},{28,24},{1,5},{5... | collective-permute-start | bytes 18874376 | tf_op jit(solution)/shard_map/ppermute | solution.py:23
  365.6 201.4 %reduce-scatter.7.cloned.1.call-start = ((), (), s32[]{:S(2)}) async-start(), calls=%async_computation.8 | async-start | bytes 7864320 | tf_op jit(solution)/shard_map/reduce_scatter | solution.py:930
  386.4 40.7 %collective-permute-start.27 = (bf16[128,2048]{1,0:T(8,128)(2,1)}, bf16[128,2048]{1,0:T(8,128)(2,1)}, u32[]{:S(2)}, u32[]{:S(2)}) collective-permute-start(bf16[128,2048]{1,0:T(8,128)(2,1)} %get-tuple-element.374), channel_id=1, source_target_pairs={{0,8},{4,12},{8,0},{12,4},{16,24},{20,28},{24,16},{28,20},{1,9},{5... | collective-permute-start | bytes 1572872 | tf_op jit(solution)/shard_map/ppermute | solution.py:23
  386.8 40.3 %collective-permute-start.33 = (bf16[128,2048]{1,0:T(8,128)(2,1)}, bf16[128,2048]{1,0:T(8,128)(2,1)}, u32[]{:S(2)}, u32[]{:S(2)}) collective-permute-start(bf16[128,2048]{1,0:T(8,128)(2,1)} %get-tuple-element.375), channel_id=1, source_target_pairs={{0,16},{4,20},{8,24},{12,28},{16,0},{20,4},{24,8},{28,12},{1,17},{... | collective-permute-start | bytes 1572872 | tf_op jit(solution)/shard_map/ppermute | solution.py:23
  387.9 23.1 %collective-permute-start.29 = (bf16[128,2048]{1,0:T(8,128)(2,1)S(1)}, bf16[128,2048]{1,0:T(8,128)(2,1)S(1)}, u32[]{:S(2)}, u32[]{:S(2)}) collective-permute-start(bf16[128,2048]{1,0:T(8,128)(2,1)S(1)} %get-tuple-element.376), channel_id=1, source_target_pairs={{0,16},{4,20},{8,24},{12,28},{16,0},{20,4},{24,8},{28,12},{1,17},{... | collective-permute-start | bytes 1572872 | tf_op jit(solution)/shard_map/ppermute | solution.py:23
  388.2 22.8 %collective-permute-start.28 = (bf16[128,2048]{1,0:T(8,128)(2,1)S(1)}, bf16[128,2048]{1,0:T(8,128)(2,1)S(1)}, u32[]{:S(2)}, u32[]{:S(2)}) collective-permute-start(bf16[128,2048]{1,0:T(8,128)(2,1)S(1)} %get-tuple-element.377), channel_id=1, source_target_pairs={{0,8},{4,12},{8,0},{12,4},{16,24},{20,28},{24,16},{28,20},{1,9},{5... | collective-permute-start | bytes 1572872 | tf_op jit(solution)/shard_map/ppermute | solution.py:23
  431.2 199.5 %reduce-scatter.9.cloned.1.call-start = ((), (), s32[]{:S(2)}) async-start(), calls=%async_computation.9 | async-start | bytes 1966080 | tf_op jit(solution)/shard_map/reduce_scatter | solution.py:989
  439.4 22.9 %collective-permute-start.35 = (bf16[256,2048]{1,0:T(8,128)(2,1)}, bf16[256,2048]{1,0:T(8,128)(2,1)S(1)}, u32[]{:S(2)}, u32[]{:S(2)}) collective-permute-start(bf16[256,2048]{1,0:T(8,128)(2,1)} %fusion.74), channel_id=1, source_target_pairs={{0,16},{4,20},{8,24},{12,28},{16,0},{20,4},{24,8},{28,12},{1,17},{... | collective-permute-start | bytes 3145736 | tf_op jit(solution)/shard_map/ppermute | solution.py:23
  439.8 22.6 %collective-permute-start.34 = (bf16[256,2048]{1,0:T(8,128)(2,1)}, bf16[256,2048]{1,0:T(8,128)(2,1)}, u32[]{:S(2)}, u32[]{:S(2)}) collective-permute-start(bf16[256,2048]{1,0:T(8,128)(2,1)} %fusion.74), channel_id=1, source_target_pairs={{0,8},{4,12},{8,0},{12,4},{16,24},{20,28},{24,16},{28,20},{1,9},{5... | collective-permute-start | bytes 3145736 | tf_op jit(solution)/shard_map/ppermute | solution.py:23
  476.6 32.2 %collective-permute-start.43 = (bf16[128,2048]{1,0:T(8,128)(2,1)S(1)}, bf16[128,2048]{1,0:T(8,128)(2,1)S(1)}, u32[]{:S(2)}, u32[]{:S(2)}) collective-permute-start(bf16[128,2048]{1,0:T(8,128)(2,1)S(1)} %get-tuple-element.370), channel_id=1, source_target_pairs={{0,8},{4,12},{8,0},{12,4},{16,24},{20,28},{24,16},{28,20},{1,9},{5... | collective-permute-start | bytes 1572872 | tf_op jit(solution)/shard_map/ppermute | solution.py:23
  477.8 31.1 %collective-permute-start.42 = (bf16[128,2048]{1,0:T(8,128)(2,1)S(1)}, bf16[128,2048]{1,0:T(8,128)(2,1)S(1)}, u32[]{:S(2)}, u32[]{:S(2)}) collective-permute-start(bf16[128,2048]{1,0:T(8,128)(2,1)S(1)} %get-tuple-element.371), channel_id=1, source_target_pairs={{0,16},{4,20},{8,24},{12,28},{16,0},{20,4},{24,8},{28,12},{1,17},{... | collective-permute-start | bytes 1572872 | tf_op jit(solution)/shard_map/ppermute | solution.py:23
  566.9 27.6 %collective-permute-start.49 = (bf16[2048,768]{1,0:T(8,128)(2,1)}, bf16[2048,768]{1,0:T(8,128)(2,1)}, u32[]{:S(2)}, u32[]{:S(2)}) collective-permute-start(bf16[2048,768]{1,0:T(8,128)(2,1)} %copy-done.17), channel_id=1, source_target_pairs={{0,4},{4,0},{8,12},{12,8},{16,20},{20,16},{24,28},{28,24},{1,5},{5... | collective-permute-start | bytes 9437192 | tf_op jit(solution)/shard_map/ppermute | solution.py:23
  589.0 101.4 %reduce-scatter.11.cloned.1.call-start = ((), (), s32[]{:S(2)}) async-start(), calls=%async_computation.10 | async-start | bytes 3932160 | tf_op jit(solution)/shard_map/reduce_scatter | solution.py:1010
  590.9 21.8 %collective-permute-start.54 = (bf16[768,512]{1,0:T(8,128)(2,1)}, bf16[768,512]{1,0:T(8,128)(2,1)}, u32[]{:S(2)}, u32[]{:S(2)}) collective-permute-start(bf16[768,512]{1,0:T(8,128)(2,1)} %bitcast.310), channel_id=1, source_target_pairs={{0,0},{1,9},{2,18},{3,27},{4,28},{5,21},{6,14},{7,7},{8,8},{9,1},{... | collective-permute-start | bytes 2359304 | tf_op jit(solution)/shard_map/ppermute | solution.py:188
  609.5 31.7 %collective-permute-start.38 = (bf16[128,2048]{1,0:T(8,128)(2,1)}, bf16[128,2048]{1,0:T(8,128)(2,1)S(1)}, u32[]{:S(2)}, u32[]{:S(2)}) collective-permute-start(bf16[128,2048]{1,0:T(8,128)(2,1)} %get-tuple-element.368), channel_id=1, source_target_pairs={{0,8},{4,12},{8,0},{12,4},{16,24},{20,28},{24,16},{28,20},{1,9},{5... | collective-permute-start | bytes 1572872 | tf_op jit(solution)/shard_map/ppermute | solution.py:23
  610.4 33.8 %collective-permute-start.57 = (bf16[128,2048]{1,0:T(8,128)(2,1)}, bf16[128,2048]{1,0:T(8,128)(2,1)}, u32[]{:S(2)}, u32[]{:S(2)}) collective-permute-start(bf16[128,2048]{1,0:T(8,128)(2,1)} %get-tuple-element.369), channel_id=1, source_target_pairs={{0,16},{4,20},{8,24},{12,28},{16,0},{20,4},{24,8},{28,12},{1,17},{... | collective-permute-start | bytes 1572872 | tf_op jit(solution)/shard_map/ppermute | solution.py:23
  690.4 30.0 %collective-permute-start.64 = (bf16[1120,512]{1,0:T(8,128)(2,1)}, bf16[1120,512]{1,0:T(8,128)(2,1)S(1)}, u32[]{:S(2)}, u32[]{:S(2)}) collective-permute-start(bf16[1120,512]{1,0:T(8,128)(2,1)} %pad_maximum_fusion.17), channel_id=1, source_target_pairs={{0,0},{1,1},{2,2},{3,3},{4,7},{5,6},{6,5},{7,4},{8,9},{9,8},{10,11... | collective-permute-start | bytes 3440648 | tf_op jit(solution)/shard_map/ppermute | solution.py:198
  (132 other events, 1193.3 us)
Sparse Core Ops, SparseCore 0:
  9.6 35.4 all-gather.5
  46.6 63.0 all-gather.7
  111.9 165.6 all-gather.9
  365.7 60.7 reduce-scatter.4
  431.3 114.4 reduce-scatter.6
  589.1 34.9 reduce-scatter.8
  630.8 59.5 reduce-scatter.10
